TPU v7x, 128 devices: a whole 4x4x4 slice. The times are simulated.
128 devices in a mesh: dom: 32 (over z, y, core), feat: 4 (over x).
Axes of the slice: x: 4, y: 4, z: 4, core: 2. Of those that a mesh axis runs over, the one named last changes fastest.
Arguments:
- features: bfloat16 [128, 131072], P('feat', 'dom'), may hold values from -6 to 6
- edge_source: int32 [32, 32, 512], P('dom'), may hold values from 0 to 4095
- edge_target: int32 [32, 32, 512], P(None, 'dom'), may hold values from 0 to 4095
- edge_count: int32 [32, 32], P(None, 'dom'), may hold values from 128 to 512, as said below
- hub_local: int32 [32, 64], P('dom'), may hold values from 0 to 4095, as said below
- second_source: int32 [32768, 10], P('dom'), may hold values from 0 to 6143
- self_one: bfloat16 [128, 256], replicated, may hold values from -0.5 to 0.5
- neigh_one: bfloat16 [128, 256], replicated, may hold values from -0.5 to 0.5
- self_two: bfloat16 [256, 256], replicated, may hold values from -0.375 to 0.375
- neigh_two: bfloat16 [256, 256], replicated, may hold values from -0.375 to 0.375
Outputs:
- embedding: bfloat16 [256, 32768], P('feat', 'dom')
Inputs may be any that keep to these rules, and one draw needn't show every extreme that they name: `edge_count`: one owner gets 512 live slots from every sender, and every sender fills 512 slots to some owner. `hub_local`: the ids of one owner's row are distinct.
All inputs are finite; a program needn't handle non-finite values.
Results may differ from a plain program's by a relative error of at most 0.0052.
Values may be sent and summed in bfloat16 or wider, within the bound.
A program may use at most 64 MiB of HBM per device.

v0:
```python
import math

import jax
import jax.numpy as jnp
from jax import lax
from jax.sharding import PartitionSpec as P


def left_product(weight, columns):
    return lax.dot_general(
        weight, columns, (((0,), (0,)), ((), ())), preferred_element_type=jnp.float32
    )


def pick_columns(data, index):
    width, extent = data.shape
    count = index.shape[0]
    block = math.gcd(count, 2048)
    blocks = index.reshape(count // block, block)
    places = jnp.arange(extent, dtype=jnp.int32)[:, None]

    def one_block(chosen):
        onehot = (places == chosen[None, :]).astype(data.dtype)
        return jnp.dot(data, onehot, preferred_element_type=jnp.float32).astype(data.dtype)

    picked = lax.map(one_block, blocks)
    return picked.transpose(1, 0, 2).reshape(width, count)


def add_columns(values, index, weight, extent):
    width, count = values.shape
    block = math.gcd(count, 2048)
    nblocks = count // block
    value_blocks = values.reshape(width, nblocks, block).transpose(1, 0, 2)
    index_blocks = index.reshape(nblocks, block)
    weight_blocks = weight.reshape(nblocks, block)
    places = jnp.arange(extent, dtype=jnp.int32)[None, :]

    def step(total, pieces):
        piece, chosen, scale = pieces
        marks = jnp.where(chosen[:, None] == places, scale[:, None], 0.0)
        piece = jnp.concatenate([piece, jnp.ones((1, block), piece.dtype)], axis=0)
        total = total + jnp.dot(
            piece, marks.astype(piece.dtype), preferred_element_type=jnp.float32
        )
        return (total, None)

    start = jnp.zeros((width + 1, extent), jnp.float32)
    total, _ = lax.scan(step, start, (value_blocks, index_blocks, weight_blocks))
    return (total[:width], total[width])


def body(
    features,
    edge_source,
    edge_target,
    edge_count,
    hub_local,
    second_source,
    self_one,
    neigh_one,
    self_two,
    neigh_two,
):
    n_feat = lax.axis_size("feat")
    n_dom = lax.axis_size("dom")
    column_index = lax.axis_index("feat")
    narrow, node_dev = features.shape
    sources = edge_source[0]
    slots = sources.shape[1]
    targets = edge_target[:, 0, :]
    counts = edge_count[:, 0]
    live = (jnp.arange(slots, dtype=jnp.int32)[None, :] < counts[:, None]).astype(jnp.float32)
    chosen = pick_columns(features, sources.reshape(-1)).reshape(narrow, n_dom, slots)
    received = lax.all_to_all(chosen, "dom", split_axis=1, concat_axis=1, tiled=True)
    neighbor_total, degree = add_columns(
        received.reshape(narrow, -1), targets.reshape(-1), live.reshape(-1), node_dev
    )
    mean_one = (neighbor_total / jnp.maximum(degree, 1.0)[None, :]).astype(jnp.bfloat16)
    hidden = self_one.shape[1]
    hcols = hidden // n_feat
    own_all, mean_all = (
        lax.all_gather(features, "feat", axis=0, tiled=True),
        lax.all_gather(mean_one, "feat", axis=0, tiled=True),
    )
    w_own = lax.dynamic_slice_in_dim(self_one, column_index * hcols, hcols, 1)
    w_near = lax.dynamic_slice_in_dim(neigh_one, column_index * hcols, hcols, 1)
    pre_one = left_product(w_own, own_all) + left_product(w_near, mean_all)
    hidden_one = jnp.maximum(pre_one, 0.0).astype(jnp.bfloat16)
    hub_rows = hidden_one[:, hub_local[0]]
    hub_count = hub_rows.shape[1]
    spread = jnp.broadcast_to(hub_rows[None], (n_dom,) + hub_rows.shape)
    landed = lax.all_to_all(spread, "dom", split_axis=0, concat_axis=0, tiled=True)
    hub_table = landed.transpose(1, 0, 2).reshape(hidden_one.shape[0], n_dom * hub_count)
    tgt_dev, fanout = second_source.shape
    near_places = jnp.arange(node_dev, dtype=jnp.int32)[:, None]
    hub_places = node_dev + jnp.arange(n_dom * hub_count, dtype=jnp.int32)[:, None]
    near_tally = jnp.zeros((node_dev, tgt_dev), jnp.bfloat16)
    hub_tally = jnp.zeros((n_dom * hub_count, tgt_dev), jnp.bfloat16)
    for column in range(fanout):
        picked = second_source[:, column][None, :]
        near_tally = near_tally + (near_places == picked).astype(jnp.bfloat16)
        hub_tally = hub_tally + (hub_places == picked).astype(jnp.bfloat16)
    total = jnp.dot(hidden_one, near_tally, preferred_element_type=jnp.float32)
    total = total + jnp.dot(hub_table, hub_tally, preferred_element_type=jnp.float32)
    mean_two = (total / fanout).astype(jnp.bfloat16)
    own_rows = hidden_one[:, :tgt_dev]
    both = lax.all_gather(jnp.stack([own_rows, mean_two]), "feat", axis=1, tiled=True)
    own_wide, mean_wide = both[0], both[1]
    v_own = lax.dynamic_slice_in_dim(self_two, column_index * hcols, hcols, 1)
    v_near = lax.dynamic_slice_in_dim(neigh_two, column_index * hcols, hcols, 1)
    result = left_product(v_own, own_wide) + left_product(v_near, mean_wide)
    return result.astype(jnp.bfloat16)


def solution(mesh):
    return jax.shard_map(
        body,
        mesh=mesh,
        in_specs=(
            P("feat", "dom"),
            P("dom", None, None),
            P(None, "dom", None),
            P(None, "dom"),
            P("dom", None),
            P("dom", None),
            P(),
            P(),
            P(),
            P(),
        ),
        out_specs=P("feat", "dom"),
        check_vma=False,
    )
```

profile of v0, /device:TPU:0, one launch (start us, length us, event | category | flops | bytes accessed | tf_op | source)
XLA Modules:
  0.0 213.9 jit_solution(5472910357324320693)
XLA Ops:
  6.5 0.9 reshape_reshape_squeeze.6
  7.4 50.8 %while.22 = (s32[]{:T(128)}, bf16[8,32,2048]{2,1,0:T(8,128)(2,1)S(1)}, s32[8,2048]{1,0:T(8,128)S(1)}, bf16[32,4096]{1,0:T(8,128)(2,1)}, s32[]{:T(128)}) while((s32[]{:T(128)}, bf16[8,32,2048]{2,1,0:T(8,128)(2,1)S(1)}, s32[8,2048]{1,0:T(8,128)S(1)}, bf16[32,4096]{1,0:T(8,128)(2,1)}, s32[]{:T(128)}) %tuple.49), condition=%wide.region_1.2_spmd.clone, body=%wide.region_0.1_spmd.clone.sunk | while | flops 545325056 | bytes 417861 | solution.py:26
  7.5 6.3 %fusion.106 = bf16[8,32,2048]{2,1,0:T(8,128)(2,1)S(1)} fusion(bf16[8,32,2048]{2,1,0:T(8,128)(2,1)S(1)} %get-tuple-element.196, s32[]{:T(128)} %get-tuple-element.195, bf16[32,4096]{1,0:T(8,128)(2,1)} %get-tuple-element.203, s32[2048]{0:T(1024)S(1)} %bitcast.68), kind=kOutput, calls=%fused_computation.8.clone.1 | convolution fusion | flops 545325056 | bytes 401412 | tf_op jit(solution)/shard_map/while/body/eval_jaxpr/dot_general | solution.py:24
  13.8 6.3 %fusion.106 = bf16[8,32,2048]{2,1,0:T(8,128)(2,1)S(1)} fusion(bf16[8,32,2048]{2,1,0:T(8,128)(2,1)S(1)} %get-tuple-element.196, s32[]{:T(128)} %get-tuple-element.195, bf16[32,4096]{1,0:T(8,128)(2,1)} %get-tuple-element.203, s32[2048]{0:T(1024)S(1)} %bitcast.68), kind=kOutput, calls=%fused_computation.8.clone.1 | convolution fusion | flops 545325056 | bytes 401412 | tf_op jit(solution)/shard_map/while/body/eval_jaxpr/dot_general | solution.py:24
  20.2 6.3 %fusion.106 = bf16[8,32,2048]{2,1,0:T(8,128)(2,1)S(1)} fusion(bf16[8,32,2048]{2,1,0:T(8,128)(2,1)S(1)} %get-tuple-element.196, s32[]{:T(128)} %get-tuple-element.195, bf16[32,4096]{1,0:T(8,128)(2,1)} %get-tuple-element.203, s32[2048]{0:T(1024)S(1)} %bitcast.68), kind=kOutput, calls=%fused_computation.8.clone.1 | convolution fusion | flops 545325056 | bytes 401412 | tf_op jit(solution)/shard_map/while/body/eval_jaxpr/dot_general | solution.py:24
  26.5 6.3 %fusion.106 = bf16[8,32,2048]{2,1,0:T(8,128)(2,1)S(1)} fusion(bf16[8,32,2048]{2,1,0:T(8,128)(2,1)S(1)} %get-tuple-element.196, s32[]{:T(128)} %get-tuple-element.195, bf16[32,4096]{1,0:T(8,128)(2,1)} %get-tuple-element.203, s32[2048]{0:T(1024)S(1)} %bitcast.68), kind=kOutput, calls=%fused_computation.8.clone.1 | convolution fusion | flops 545325056 | bytes 401412 | tf_op jit(solution)/shard_map/while/body/eval_jaxpr/dot_general | solution.py:24
  32.9 6.3 %fusion.106 = bf16[8,32,2048]{2,1,0:T(8,128)(2,1)S(1)} fusion(bf16[8,32,2048]{2,1,0:T(8,128)(2,1)S(1)} %get-tuple-element.196, s32[]{:T(128)} %get-tuple-element.195, bf16[32,4096]{1,0:T(8,128)(2,1)} %get-tuple-element.203, s32[2048]{0:T(1024)S(1)} %bitcast.68), kind=kOutput, calls=%fused_computation.8.clone.1 | convolution fusion | flops 545325056 | bytes 401412 | tf_op jit(solution)/shard_map/while/body/eval_jaxpr/dot_general | solution.py:24
  39.2 6.3 %fusion.106 = bf16[8,32,2048]{2,1,0:T(8,128)(2,1)S(1)} fusion(bf16[8,32,2048]{2,1,0:T(8,128)(2,1)S(1)} %get-tuple-element.196, s32[]{:T(128)} %get-tuple-element.195, bf16[32,4096]{1,0:T(8,128)(2,1)} %get-tuple-element.203, s32[2048]{0:T(1024)S(1)} %bitcast.68), kind=kOutput, calls=%fused_computation.8.clone.1 | convolution fusion | flops 545325056 | bytes 401412 | tf_op jit(solution)/shard_map/while/body/eval_jaxpr/dot_general | solution.py:24
  45.6 6.3 %fusion.106 = bf16[8,32,2048]{2,1,0:T(8,128)(2,1)S(1)} fusion(bf16[8,32,2048]{2,1,0:T(8,128)(2,1)S(1)} %get-tuple-element.196, s32[]{:T(128)} %get-tuple-element.195, bf16[32,4096]{1,0:T(8,128)(2,1)} %get-tuple-element.203, s32[2048]{0:T(1024)S(1)} %bitcast.68), kind=kOutput, calls=%fused_computation.8.clone.1 | convolution fusion | flops 545325056 | bytes 401412 | tf_op jit(solution)/shard_map/while/body/eval_jaxpr/dot_general | solution.py:24
  51.9 6.3 %fusion.106 = bf16[8,32,2048]{2,1,0:T(8,128)(2,1)S(1)} fusion(bf16[8,32,2048]{2,1,0:T(8,128)(2,1)S(1)} %get-tuple-element.196, s32[]{:T(128)} %get-tuple-element.195, bf16[32,4096]{1,0:T(8,128)(2,1)} %get-tuple-element.203, s32[2048]{0:T(1024)S(1)} %bitcast.68), kind=kOutput, calls=%fused_computation.8.clone.1 | convolution fusion | flops 545325056 | bytes 401412 | tf_op jit(solution)/shard_map/while/body/eval_jaxpr/dot_general | solution.py:24
  59.5 1.6 copy.20
  61.1 8.6 %all-to-all-start = ((bf16[32,32,512]{2,0,1:T(8,128)(2,1)}), bf16[32,32,512]{2,0,1:T(8,128)(2,1)S(1)}, u32[]{:S(2)}, u32[]{:S(2)}) async-start(bf16[32,32,512]{2,0,1:T(8,128)(2,1)} %copy.20), calls=%async_computation | async-start | bytes 2097152 | tf_op jit(solution)/shard_map/all_to_all | solution.py:75
  72.2 14.6 %all-to-all-done = bf16[32,32,512]{2,0,1:T(8,128)(2,1)S(1)} async-done(((bf16[32,32,512]{2,0,1:T(8,128)(2,1)}), bf16[32,32,512]{2,0,1:T(8,128)(2,1)S(1)}, u32[]{:S(2)}, u32[]{:S(2)}) %all-to-all-start) | async-done | bytes 1048608 | tf_op jit(solution)/shard_map/all_to_all | solution.py:75
  89.2 28.5 %while.23 = (s32[]{:T(128)}, f32[33,4096]{1,0:T(8,128)S(1)}, bf16[8,32,2048]{2,1,0:T(8,128)(2,1)S(1)}, s32[8,2048]{1,0:T(8,128)S(1)}, f32[8,2048]{1,0:T(8,128)S(1)}, /*index=5*/s32[]{:T(128)}, s32[]{:T(128)}) while((s32[]{:T(128)}, f32[33,4096]{1,0:T(8,128)S(1)}, bf16[8,32,2048]{2,1,0:T(8,128)(2,1)S(1)}, s32[8,2048]{1,0:T(8,128)S(1)}, ...), condition=%wide.region_3.4_spmd.clone, body=%wide.region_2.3_spmd.clone.sunk | while | flops 570695680 | bytes 1523811 | solution.py:49
  89.3 3.5 %fusion.108 = f32[33,4096]{1,0:T(8,128)S(1)} fusion(f32[2048]{0:T(1024)S(1)} %bitcast.66, s32[2048]{0:T(1024)S(1)} %bitcast.67, f32[33,4096]{1,0:T(8,128)S(1)} %get-tuple-element.213, pred[]{:T(512)S(6)} %compare.4, bf16[32,2048]{1,0:T(8,128)(2,1)S(1)} %dynamic-slice_bitcast_fusion.2), kind=kOutput, calls=%fused_computation.16.clone.1 | convolution fusion | flops 570695680 | bytes 1228801 | tf_op jit(solution)/shard_map/while/body/eval_jaxpr/dot_general | solution.py:43
  92.9 3.5 %fusion.108 = f32[33,4096]{1,0:T(8,128)S(1)} fusion(f32[2048]{0:T(1024)S(1)} %bitcast.66, s32[2048]{0:T(1024)S(1)} %bitcast.67, f32[33,4096]{1,0:T(8,128)S(1)} %get-tuple-element.213, pred[]{:T(512)S(6)} %compare.4, bf16[32,2048]{1,0:T(8,128)(2,1)S(1)} %dynamic-slice_bitcast_fusion.2), kind=kOutput, calls=%fused_computation.16.clone.1 | convolution fusion | flops 570695680 | bytes 1228801 | tf_op jit(solution)/shard_map/while/body/eval_jaxpr/dot_general | solution.py:43
  96.4 3.5 %fusion.108 = f32[33,4096]{1,0:T(8,128)S(1)} fusion(f32[2048]{0:T(1024)S(1)} %bitcast.66, s32[2048]{0:T(1024)S(1)} %bitcast.67, f32[33,4096]{1,0:T(8,128)S(1)} %get-tuple-element.213, pred[]{:T(512)S(6)} %compare.4, bf16[32,2048]{1,0:T(8,128)(2,1)S(1)} %dynamic-slice_bitcast_fusion.2), kind=kOutput, calls=%fused_computation.16.clone.1 | convolution fusion | flops 570695680 | bytes 1228801 | tf_op jit(solution)/shard_map/while/body/eval_jaxpr/dot_general | solution.py:43
  100.0 3.5 %fusion.108 = f32[33,4096]{1,0:T(8,128)S(1)} fusion(f32[2048]{0:T(1024)S(1)} %bitcast.66, s32[2048]{0:T(1024)S(1)} %bitcast.67, f32[33,4096]{1,0:T(8,128)S(1)} %get-tuple-element.213, pred[]{:T(512)S(6)} %compare.4, bf16[32,2048]{1,0:T(8,128)(2,1)S(1)} %dynamic-slice_bitcast_fusion.2), kind=kOutput, calls=%fused_computation.16.clone.1 | convolution fusion | flops 570695680 | bytes 1228801 | tf_op jit(solution)/shard_map/while/body/eval_jaxpr/dot_general | solution.py:43
  103.5 3.5 %fusion.108 = f32[33,4096]{1,0:T(8,128)S(1)} fusion(f32[2048]{0:T(1024)S(1)} %bitcast.66, s32[2048]{0:T(1024)S(1)} %bitcast.67, f32[33,4096]{1,0:T(8,128)S(1)} %get-tuple-element.213, pred[]{:T(512)S(6)} %compare.4, bf16[32,2048]{1,0:T(8,128)(2,1)S(1)} %dynamic-slice_bitcast_fusion.2), kind=kOutput, calls=%fused_computation.16.clone.1 | convolution fusion | flops 570695680 | bytes 1228801 | tf_op jit(solution)/shard_map/while/body/eval_jaxpr/dot_general | solution.py:43
  107.1 3.5 %fusion.108 = f32[33,4096]{1,0:T(8,128)S(1)} fusion(f32[2048]{0:T(1024)S(1)} %bitcast.66, s32[2048]{0:T(1024)S(1)} %bitcast.67, f32[33,4096]{1,0:T(8,128)S(1)} %get-tuple-element.213, pred[]{:T(512)S(6)} %compare.4, bf16[32,2048]{1,0:T(8,128)(2,1)S(1)} %dynamic-slice_bitcast_fusion.2), kind=kOutput, calls=%fused_computation.16.clone.1 | convolution fusion | flops 570695680 | bytes 1228801 | tf_op jit(solution)/shard_map/while/body/eval_jaxpr/dot_general | solution.py:43
  110.7 3.5 %fusion.108 = f32[33,4096]{1,0:T(8,128)S(1)} fusion(f32[2048]{0:T(1024)S(1)} %bitcast.66, s32[2048]{0:T(1024)S(1)} %bitcast.67, f32[33,4096]{1,0:T(8,128)S(1)} %get-tuple-element.213, pred[]{:T(512)S(6)} %compare.4, bf16[32,2048]{1,0:T(8,128)(2,1)S(1)} %dynamic-slice_bitcast_fusion.2), kind=kOutput, calls=%fused_computation.16.clone.1 | convolution fusion | flops 570695680 | bytes 1228801 | tf_op jit(solution)/shard_map/while/body/eval_jaxpr/dot_general | solution.py:43
  114.2 3.5 %fusion.108 = f32[33,4096]{1,0:T(8,128)S(1)} fusion(f32[2048]{0:T(1024)S(1)} %bitcast.66, s32[2048]{0:T(1024)S(1)} %bitcast.67, f32[33,4096]{1,0:T(8,128)S(1)} %get-tuple-element.213, pred[]{:T(512)S(6)} %compare.4, bf16[32,2048]{1,0:T(8,128)(2,1)S(1)} %dynamic-slice_bitcast_fusion.2), kind=kOutput, calls=%fused_computation.16.clone.1 | convolution fusion | flops 570695680 | bytes 1228801 | tf_op jit(solution)/shard_map/while/body/eval_jaxpr/dot_general | solution.py:43
  118.7 1.6 fusion.88
  120.3 20.2 %all-gather.6.cloned.1.call-done = bf16[128,4096]{1,0:T(8,128)(2,1)} async-done(((bf16[32,4096]{1,0:T(8,128)(2,1)}), bf16[128,4096]{1,0:T(8,128)(2,1)}) %all-gather.6.cloned.1.call-update) | async-done | bytes 1048592 | tf_op jit(solution)/shard_map/all_gather | solution.py:84
  140.5 1.6 fusion.58
  143.5 1.1 reshape.74
  144.6 7.3 %all-to-all-start.1 = ((bf16[32,2,2048]{2,1,0:T(2,128)(2,1)}), bf16[32,2,2048]{2,1,0:T(2,128)(2,1)S(1)}, u32[]{:S(2)}, u32[]{:S(2)}) async-start(bf16[32,2,2048]{2,1,0:T(2,128)(2,1)} %reshape.74), calls=%async_computation.1 | async-start | bytes 524288 | tf_op jit(solution)/shard_map/all_to_all | solution.py:93
  151.9 17.1 %fusion.28 = f32[64,1024]{1,0:T(8,128)S(1)} fusion(bf16[64,4096]{1,0:T(8,128)(2,1)S(1)} %fusion.58, s32[1024]{0:T(1024)S(1)} %bitcast.88, s32[1024]{0:T(1024)S(1)} %bitcast.90, s32[1024]{0:T(1024)S(1)} %bitcast.74, s32[1024]{0:T(1024)S(1)} %bitcast.76, s32[1024]{0:T(1024)S(1)} %bitcast.78, s32[1024]{0:T(1024)S(1)} %bitcast.80, s32[1024]{0:T(1024)S(1)} %bitcast.82, ...), kind=kOutput, calls=%fused_computation.44 | convolution fusion | flops 704643072 | bytes 827392 | tf_op jit(solution)/shard_map/dot_general | solution.py:104
  170.2 8.3 %fusion.81 = bf16[1,64,1024]{2,1,0:T(8,128)(2,1)S(1)} fusion(f32[64,1024]{1,0:T(8,128)S(1)} %fusion.28, bf16[64,2048]{1,0:T(8,128)(2,1)S(1)} %reshape.55, s32[1024]{0:T(1024)S(1)} %bitcast.89, s32[1024]{0:T(1024)S(1)} %bitcast.91, s32[1024]{0:T(1024)S(1)} %bitcast.75, s32[1024]{0:T(1024)S(1)} %bitcast.77, s32[1024]{0:T(1024)S(1)} %bitcast.79, ...), kind=kOutput, calls=%fused_computation.92 | convolution fusion | flops 329449472 | bytes 704512 | tf_op jit(solution)/shard_map/dot_general | solution.py:105
  179.3 24.7 %all-gather.8.cloned.1.call-done = bf16[2,256,1024]{2,1,0:T(8,128)(2,1)} async-done(((bf16[2,64,1024]{2,1,0:T(8,128)(2,1)}), bf16[2,256,1024]{2,1,0:T(8,128)(2,1)}) %all-gather.8.cloned.1.call-update) | async-done | bytes 1048592 | tf_op jit(solution)/shard_map/all_gather | solution.py:108
  204.0 1.3 fusion.84
  205.3 2.0 fusion.77
  (90 shorter events, 10.7 us)
Async XLA Ops:
  6.5 197.4 %copy-start = (bf16[256,256]{1,0:T(8,128)(2,1)S(1)}, bf16[256,256]{1,0:T(8,128)(2,1)}, u32[]{:S(2)}) copy-start(bf16[256,256]{1,0:T(8,128)(2,1)} %param.22) | copy-start | bytes 393220
  61.1 10.1 %copy-start.7 = (s32[32,1]{0,1:T(1,128)S(1)}, s32[32,1]{0,1:T(1,128)}, u32[]{:S(2)}) copy-start(s32[32,1]{0,1:T(1,128)} %param.17) | copy-start | bytes 388
  61.1 10.9 %copy-start.2 = (s32[32,1,512]{2,1,0:T(1,128)S(1)}, s32[32,1,512]{2,1,0:T(1,128)}, u32[]{:S(2)}) copy-start(s32[32,1,512]{2,1,0:T(1,128)} %param.16) | copy-start | bytes 196612
  61.1 25.8 %all-to-all-start = ((bf16[32,32,512]{2,0,1:T(8,128)(2,1)}), bf16[32,32,512]{2,0,1:T(8,128)(2,1)S(1)}, u32[]{:S(2)}, u32[]{:S(2)}) async-start(bf16[32,32,512]{2,0,1:T(8,128)(2,1)} %copy.20), calls=%async_computation | async-start | bytes 2097152 | tf_op jit(solution)/shard_map/all_to_all | solution.py:75
  69.7 49.0 %all-gather.4.cloned.1.call-start = ((), (), s32[]{:S(2)}) async-start(), calls=%async_computation.2 | async-start | bytes 1310720 | tf_op jit(solution)/shard_map/all_gather | solution.py:83
  70.4 70.1 %all-gather.6.cloned.1.call-start = ((), (), s32[]{:S(2)}) async-start(), calls=%async_computation.3 | async-start | bytes 1310720 | tf_op jit(solution)/shard_map/all_gather | solution.py:84
  88.1 1.1 copy-start.1
  117.7 0.8 copy-start.8
  117.7 0.9 copy-start.4
  117.7 0.9 copy-start.5
  118.6 21.9 %copy-start.6 = (bf16[128,256]{1,0:T(8,128)(2,1)S(1)}, bf16[128,256]{1,0:T(8,128)(2,1)}, u32[]{:S(2)}) copy-start(bf16[128,256]{1,0:T(8,128)(2,1)} %param.21) | copy-start | bytes 196612
  144.6 24.5 %all-to-all-start.1 = ((bf16[32,2,2048]{2,1,0:T(2,128)(2,1)}), bf16[32,2,2048]{2,1,0:T(2,128)(2,1)S(1)}, u32[]{:S(2)}, u32[]{:S(2)}) async-start(bf16[32,2,2048]{2,1,0:T(2,128)(2,1)} %reshape.74), calls=%async_computation.1 | async-start | bytes 524288 | tf_op jit(solution)/shard_map/all_to_all | solution.py:93
  151.9 52.1 %all-gather.8.cloned.1.call-start = ((), (), s32[]{:S(2)}) async-start(), calls=%async_computation.4 | async-start | bytes 1310720 | tf_op jit(solution)/shard_map/all_gather | solution.py:108
  178.5 26.8 %copy-start.3 = (bf16[256,256]{1,0:T(8,128)(2,1)S(1)}, bf16[256,256]{1,0:T(8,128)(2,1)}, u32[]{:S(2)}) copy-start(bf16[256,256]{1,0:T(8,128)(2,1)} %param.23) | copy-start | bytes 393220
Sparse Core Ops, SparseCore 0:
  72.1 25.4 all-gather.3
  118.7 21.7 all-gather.5
  179.4 24.5 all-gather.7
where the time goes:
time: 215 us; the launch traced here: 214 us
  matrix products  110 us (51%)
  waiting for transfers between devices  60.3 us (28%)
  starting transfers between devices  16.1 us (7%)
  between operations  13.4 us (6%)
  local copies, waits for them, and re-layouts  10.9 us (5%)
  other arithmetic  2.28 us (1%)
    dot_general x8, matrix products, one_block(): jnp.dot(data, onehot, preferred_element_type=jnp.float32).astype(data.dtype)  50.5 us
    dot_general x8, matrix products, step(): jnp.dot(piece, marks.astype(piece.dtype), preferred_element_type=jnp.floa...  27.7 us
    all_gather x1, waiting for transfers between devices, body(): lax.all_gather(jnp.stack([own_rows, mean_two]), 'feat', axis=1, tiled=True)  24.7 us
    all_gather x1, waiting for transfers between devices, body(): lax.all_gather(mean_one, 'feat', axis=0, tiled=True)  20.2 us
    dot_general x1, matrix products, body(): total = jnp.dot(hidden_one, near_tally, preferred_element_type=jnp.float32)  17.1 us
    all_to_all x1, waiting for transfers between devices, body(): lax.all_to_all(chosen, 'dom', split_axis=1, concat_axis=1, tiled=True)  14.6 us
    all_to_all x1, starting transfers between devices, body(): lax.all_to_all(chosen, 'dom', split_axis=1, concat_axis=1, tiled=True)  8.58 us
    dot_general x1, matrix products, body(): jnp.dot(hub_table, hub_tally, preferred_element_type=jnp.float32)  8.28 us
  transfers between devices with their start and end apart: 5, of which 3 were waited for; matrix products, arithmetic and copies ran while one was open for 24% of the time, Pallas kernels for 0%

commit v1 on v0

--- a/solution.py
+++ b/solution.py
@@ -101,12 +101,16 @@
         picked = second_source[:, column][None, :]
         near_tally = near_tally + (near_places == picked).astype(jnp.bfloat16)
         hub_tally = hub_tally + (hub_places == picked).astype(jnp.bfloat16)
+    near_tally, hub_tally = lax.optimization_barrier((near_tally, hub_tally))
     total = jnp.dot(hidden_one, near_tally, preferred_element_type=jnp.float32)
     total = total + jnp.dot(hub_table, hub_tally, preferred_element_type=jnp.float32)
     mean_two = (total / fanout).astype(jnp.bfloat16)
-    own_rows = hidden_one[:, :tgt_dev]
-    both = lax.all_gather(jnp.stack([own_rows, mean_two]), "feat", axis=1, tiled=True)
-    own_wide, mean_wide = both[0], both[1]
+    own_cols = lax.dynamic_slice_in_dim(own_all, 0, tgt_dev, 1)
+    near_cols = lax.dynamic_slice_in_dim(mean_all, 0, tgt_dev, 1)
+    own_wide = jnp.maximum(
+        left_product(self_one, own_cols) + left_product(neigh_one, near_cols), 0.0
+    ).astype(jnp.bfloat16)
+    mean_wide = lax.all_gather(mean_two, "feat", axis=0, tiled=True)
     v_own = lax.dynamic_slice_in_dim(self_two, column_index * hcols, hcols, 1)
     v_near = lax.dynamic_slice_in_dim(neigh_two, column_index * hcols, hcols, 1)
     result = left_product(v_own, own_wide) + left_product(v_near, mean_wide)

time: 215 us -> 215 us (level)
  waiting for transfers between devices: 60.3 us -> 17.3 us
  other arithmetic: 2.28 us -> 35.9 us
  blocking collectives: 0 us -> 12.9 us
  matrix products: 110 us -> 107 us
    add x0 -> x2, other arithmetic: none -> 32.3 us  [the longest x1 22.4 us: body(): near_tally = near_tally + (near_places == picked).astype(jnp.bfloat16)]
    all_gather x1 -> x0, waiting for transfers between devices: 24.7 us -> none  [body(): lax.all_gather(jnp.stack([own_rows, mean_two]), 'feat', axis=1, tiled=True)]
    all_to_all x1, waiting for transfers between devices: 14.6 us -> 0.01 us  [body(): lax.all_to_all(chosen, 'dom', split_axis=1, concat_axis=1, tiled=True)]
    dot_general x8, matrix products: 27.7 us -> 41.3 us  [step(): jnp.dot(piece, marks.astype(piece.dtype), preferred_element_type=jnp.floa...]
    all_gather x0 -> x1, blocking collectives: none -> 12.9 us  [body(): mean_wide = lax.all_gather(mean_two, 'feat', axis=0, tiled=True)]
    dot_general x1, matrix products: 17.1 us -> 4.94 us  [body(): total = jnp.dot(hidden_one, near_tally, preferred_element_type=jnp.float32)]
    all_gather x1, waiting for transfers between devices: 20.2 us -> 12.7 us  [body(): lax.all_gather(mean_one, 'feat', axis=0, tiled=True)]
    dot_general x1, matrix products: 8.28 us -> 3.04 us  [body(): jnp.dot(hub_table, hub_tally, preferred_element_type=jnp.float32)]
  transfers between devices with their start and end apart: 5 -> 4, of which waited for: 3 -> 2; matrix products, arithmetic and copies ran while one was open for 24% -> 67% of each run, Pallas kernels for 0% -> 0%
where the time goes in v1:
time: 215 us; the launch traced here: 213 us
  matrix products  107 us (50%)
  other arithmetic  35.9 us (17%)
  waiting for transfers between devices  17.3 us (8%)
  starting transfers between devices  15.9 us (7%)
  between operations  13.7 us (6%)
  blocking collectives  12.9 us (6%)
  local copies, waits for them, and re-layouts  10.5 us (5%)
    dot_general x8, matrix products, one_block(): jnp.dot(data, onehot, preferred_element_type=jnp.float32).astype(data.dtype)  50.5 us
    dot_general x8, matrix products, step(): jnp.dot(piece, marks.astype(piece.dtype), preferred_element_type=jnp.floa...  41.3 us
    add x1, other arithmetic, body(): near_tally = near_tally + (near_places == picked).astype(jnp.bfloat16)  22.4 us
    all_gather x1, blocking collectives, body(): mean_wide = lax.all_gather(mean_two, 'feat', axis=0, tiled=True)  12.9 us
    all_gather x1, waiting for transfers between devices, body(): lax.all_gather(mean_one, 'feat', axis=0, tiled=True)  12.7 us
    add x1, other arithmetic, body(): hub_tally = hub_tally + (hub_places == picked).astype(jnp.bfloat16)  9.88 us
    all_to_all x1, starting transfers between devices, body(): lax.all_to_all(chosen, 'dom', split_axis=1, concat_axis=1, tiled=True)  8.45 us
    all_to_all x1, starting transfers between devices, body(): lax.all_to_all(spread, 'dom', split_axis=0, concat_axis=0, tiled=True)  7.26 us
  transfers between devices with their start and end apart: 4, of which 2 were waited for; matrix products, arithmetic and copies ran while one was open for 67% of the time, Pallas kernels for 0%

profile of v1, /device:TPU:0, one launch (start us, length us, event | category | flops | bytes accessed | tf_op | source)
XLA Modules:
  0.0 213.5 jit_solution(8603208562605733341)
XLA Ops:
  8.1 50.8 %while.22 = (s32[]{:T(128)}, bf16[8,32,2048]{2,1,0:T(8,128)(2,1)S(1)}, s32[8,2048]{1,0:T(8,128)S(1)}, bf16[32,4096]{1,0:T(8,128)(2,1)}, s32[]{:T(128)}) while((s32[]{:T(128)}, bf16[8,32,2048]{2,1,0:T(8,128)(2,1)S(1)}, s32[8,2048]{1,0:T(8,128)S(1)}, bf16[32,4096]{1,0:T(8,128)(2,1)}, s32[]{:T(128)}) %tuple.51), condition=%wide.region_1.2_spmd.clone, body=%wide.region_0.1_spmd.clone.sunk | while | flops 545325056 | bytes 417869 | solution.py:26
  8.2 6.3 %fusion.89 = bf16[8,32,2048]{2,1,0:T(8,128)(2,1)S(1)} fusion(bf16[8,32,2048]{2,1,0:T(8,128)(2,1)S(1)} %get-tuple-element.200, s32[]{:T(128)S(6)} %copy.33, bf16[32,4096]{1,0:T(8,128)(2,1)} %get-tuple-element.207, s32[2048]{0:T(1024)S(1)} %bitcast.77), kind=kOutput, calls=%fused_computation.8.clone.1 | convolution fusion | flops 545325056 | bytes 401412 | tf_op jit(solution)/shard_map/while/body/eval_jaxpr/dot_general | solution.py:24
  14.5 6.3 %fusion.89 = bf16[8,32,2048]{2,1,0:T(8,128)(2,1)S(1)} fusion(bf16[8,32,2048]{2,1,0:T(8,128)(2,1)S(1)} %get-tuple-element.200, s32[]{:T(128)S(6)} %copy.33, bf16[32,4096]{1,0:T(8,128)(2,1)} %get-tuple-element.207, s32[2048]{0:T(1024)S(1)} %bitcast.77), kind=kOutput, calls=%fused_computation.8.clone.1 | convolution fusion | flops 545325056 | bytes 401412 | tf_op jit(solution)/shard_map/while/body/eval_jaxpr/dot_general | solution.py:24
  20.9 6.3 %fusion.89 = bf16[8,32,2048]{2,1,0:T(8,128)(2,1)S(1)} fusion(bf16[8,32,2048]{2,1,0:T(8,128)(2,1)S(1)} %get-tuple-element.200, s32[]{:T(128)S(6)} %copy.33, bf16[32,4096]{1,0:T(8,128)(2,1)} %get-tuple-element.207, s32[2048]{0:T(1024)S(1)} %bitcast.77), kind=kOutput, calls=%fused_computation.8.clone.1 | convolution fusion | flops 545325056 | bytes 401412 | tf_op jit(solution)/shard_map/while/body/eval_jaxpr/dot_general | solution.py:24
  27.2 6.3 %fusion.89 = bf16[8,32,2048]{2,1,0:T(8,128)(2,1)S(1)} fusion(bf16[8,32,2048]{2,1,0:T(8,128)(2,1)S(1)} %get-tuple-element.200, s32[]{:T(128)S(6)} %copy.33, bf16[32,4096]{1,0:T(8,128)(2,1)} %get-tuple-element.207, s32[2048]{0:T(1024)S(1)} %bitcast.77), kind=kOutput, calls=%fused_computation.8.clone.1 | convolution fusion | flops 545325056 | bytes 401412 | tf_op jit(solution)/shard_map/while/body/eval_jaxpr/dot_general | solution.py:24
  33.6 6.3 %fusion.89 = bf16[8,32,2048]{2,1,0:T(8,128)(2,1)S(1)} fusion(bf16[8,32,2048]{2,1,0:T(8,128)(2,1)S(1)} %get-tuple-element.200, s32[]{:T(128)S(6)} %copy.33, bf16[32,4096]{1,0:T(8,128)(2,1)} %get-tuple-element.207, s32[2048]{0:T(1024)S(1)} %bitcast.77), kind=kOutput, calls=%fused_computation.8.clone.1 | convolution fusion | flops 545325056 | bytes 401412 | tf_op jit(solution)/shard_map/while/body/eval_jaxpr/dot_general | solution.py:24
  39.9 6.3 %fusion.89 = bf16[8,32,2048]{2,1,0:T(8,128)(2,1)S(1)} fusion(bf16[8,32,2048]{2,1,0:T(8,128)(2,1)S(1)} %get-tuple-element.200, s32[]{:T(128)S(6)} %copy.33, bf16[32,4096]{1,0:T(8,128)(2,1)} %get-tuple-element.207, s32[2048]{0:T(1024)S(1)} %bitcast.77), kind=kOutput, calls=%fused_computation.8.clone.1 | convolution fusion | flops 545325056 | bytes 401412 | tf_op jit(solution)/shard_map/while/body/eval_jaxpr/dot_general | solution.py:24
  46.3 6.3 %fusion.89 = bf16[8,32,2048]{2,1,0:T(8,128)(2,1)S(1)} fusion(bf16[8,32,2048]{2,1,0:T(8,128)(2,1)S(1)} %get-tuple-element.200, s32[]{:T(128)S(6)} %copy.33, bf16[32,4096]{1,0:T(8,128)(2,1)} %get-tuple-element.207, s32[2048]{0:T(1024)S(1)} %bitcast.77), kind=kOutput, calls=%fused_computation.8.clone.1 | convolution fusion | flops 545325056 | bytes 401412 | tf_op jit(solution)/shard_map/while/body/eval_jaxpr/dot_general | solution.py:24
  52.6 6.3 %fusion.89 = bf16[8,32,2048]{2,1,0:T(8,128)(2,1)S(1)} fusion(bf16[8,32,2048]{2,1,0:T(8,128)(2,1)S(1)} %get-tuple-element.200, s32[]{:T(128)S(6)} %copy.33, bf16[32,4096]{1,0:T(8,128)(2,1)} %get-tuple-element.207, s32[2048]{0:T(1024)S(1)} %bitcast.77), kind=kOutput, calls=%fused_computation.8.clone.1 | convolution fusion | flops 545325056 | bytes 401412 | tf_op jit(solution)/shard_map/while/body/eval_jaxpr/dot_general | solution.py:24
  60.3 1.6 copy.20
  61.9 8.4 %all-to-all-start = ((bf16[32,32,512]{2,0,1:T(8,128)(2,1)}), bf16[32,32,512]{2,0,1:T(8,128)(2,1)S(1)}, u32[]{:S(2)}, u32[]{:S(2)}) async-start(bf16[32,32,512]{2,0,1:T(8,128)(2,1)} %copy.20), calls=%async_computation | async-start | bytes 2097152 | tf_op jit(solution)/shard_map/all_to_all | solution.py:75
  70.6 22.4 %fusion.27 = bf16[4096,1024]{1,0:T(8,128)(2,1)} fusion(s32[1024]{0:T(1024)S(1)} %bitcast.96, s32[1024]{0:T(1024)S(1)} %bitcast.98, s32[1024]{0:T(1024)S(1)} %bitcast.82, s32[1024]{0:T(1024)S(1)} %bitcast.84, s32[1024]{0:T(1024)S(1)} %bitcast.86, s32[1024]{0:T(1024)S(1)} %bitcast.88, s32[1024]{0:T(1024)S(1)} %bitcast.90, s32[1024]{0:T(1024)S(1)} %bitcast.92, ...), kind=kLoop, calls=%fused_computation.43 | loop fusion | flops 167772160 | bytes 8429568 | tf_op jit(solution)/shard_map/add | solution.py:102
  96.7 41.8 %while.23 = (s32[]{:T(128)}, f32[33,4096]{1,0:T(8,128)}, bf16[8,32,2048]{2,1,0:T(8,128)(2,1)S(1)}, s32[8,2048]{1,0:T(8,128)S(1)}, f32[8,2048]{1,0:T(8,128)S(1)}, /*index=5*/s32[]{:T(128)}, s32[]{:T(128)}) while((s32[]{:T(128)}, f32[33,4096]{1,0:T(8,128)}, bf16[8,32,2048]{2,1,0:T(8,128)(2,1)S(1)}, s32[8,2048]{1,0:T(8,128)S(1)}, ...), condition=%wide.region_3.4_spmd.clone, body=%wide.region_2.3_spmd.clone.sunk | while | flops 570695680 | bytes 1523819 | solution.py:49
  96.8 4.2 %fusion.91 = f32[33,4096]{1,0:T(8,128)} fusion(f32[2048]{0:T(1024)S(1)} %bitcast.75, s32[2048]{0:T(1024)S(1)} %bitcast.76, f32[33,4096]{1,0:T(8,128)} %get-tuple-element.217, pred[]{:T(512)S(6)} %compare.4, bf16[32,2048]{1,0:T(8,128)(2,1)S(1)} %dynamic-slice_bitcast_fusion.2), kind=kOutput, calls=%fused_computation.16.clone.1 | convolution fusion | flops 570695680 | bytes 1228801 | tf_op jit(solution)/shard_map/while/body/eval_jaxpr/dot_general | solution.py:43
  101.1 5.3 %fusion.91 = f32[33,4096]{1,0:T(8,128)} fusion(f32[2048]{0:T(1024)S(1)} %bitcast.75, s32[2048]{0:T(1024)S(1)} %bitcast.76, f32[33,4096]{1,0:T(8,128)} %get-tuple-element.217, pred[]{:T(512)S(6)} %compare.4, bf16[32,2048]{1,0:T(8,128)(2,1)S(1)} %dynamic-slice_bitcast_fusion.2), kind=kOutput, calls=%fused_computation.16.clone.1 | convolution fusion | flops 570695680 | bytes 1228801 | tf_op jit(solution)/shard_map/while/body/eval_jaxpr/dot_general | solution.py:43
  106.4 5.3 %fusion.91 = f32[33,4096]{1,0:T(8,128)} fusion(f32[2048]{0:T(1024)S(1)} %bitcast.75, s32[2048]{0:T(1024)S(1)} %bitcast.76, f32[33,4096]{1,0:T(8,128)} %get-tuple-element.217, pred[]{:T(512)S(6)} %compare.4, bf16[32,2048]{1,0:T(8,128)(2,1)S(1)} %dynamic-slice_bitcast_fusion.2), kind=kOutput, calls=%fused_computation.16.clone.1 | convolution fusion | flops 570695680 | bytes 1228801 | tf_op jit(solution)/shard_map/while/body/eval_jaxpr/dot_general | solution.py:43
  111.8 5.3 %fusion.91 = f32[33,4096]{1,0:T(8,128)} fusion(f32[2048]{0:T(1024)S(1)} %bitcast.75, s32[2048]{0:T(1024)S(1)} %bitcast.76, f32[33,4096]{1,0:T(8,128)} %get-tuple-element.217, pred[]{:T(512)S(6)} %compare.4, bf16[32,2048]{1,0:T(8,128)(2,1)S(1)} %dynamic-slice_bitcast_fusion.2), kind=kOutput, calls=%fused_computation.16.clone.1 | convolution fusion | flops 570695680 | bytes 1228801 | tf_op jit(solution)/shard_map/while/body/eval_jaxpr/dot_general | solution.py:43
  117.2 5.3 %fusion.91 = f32[33,4096]{1,0:T(8,128)} fusion(f32[2048]{0:T(1024)S(1)} %bitcast.75, s32[2048]{0:T(1024)S(1)} %bitcast.76, f32[33,4096]{1,0:T(8,128)} %get-tuple-element.217, pred[]{:T(512)S(6)} %compare.4, bf16[32,2048]{1,0:T(8,128)(2,1)S(1)} %dynamic-slice_bitcast_fusion.2), kind=kOutput, calls=%fused_computation.16.clone.1 | convolution fusion | flops 570695680 | bytes 1228801 | tf_op jit(solution)/shard_map/while/body/eval_jaxpr/dot_general | solution.py:43
  122.5 5.3 %fusion.91 = f32[33,4096]{1,0:T(8,128)} fusion(f32[2048]{0:T(1024)S(1)} %bitcast.75, s32[2048]{0:T(1024)S(1)} %bitcast.76, f32[33,4096]{1,0:T(8,128)} %get-tuple-element.217, pred[]{:T(512)S(6)} %compare.4, bf16[32,2048]{1,0:T(8,128)(2,1)S(1)} %dynamic-slice_bitcast_fusion.2), kind=kOutput, calls=%fused_computation.16.clone.1 | convolution fusion | flops 570695680 | bytes 1228801 | tf_op jit(solution)/shard_map/while/body/eval_jaxpr/dot_general | solution.py:43
  127.9 5.3 %fusion.91 = f32[33,4096]{1,0:T(8,128)} fusion(f32[2048]{0:T(1024)S(1)} %bitcast.75, s32[2048]{0:T(1024)S(1)} %bitcast.76, f32[33,4096]{1,0:T(8,128)} %get-tuple-element.217, pred[]{:T(512)S(6)} %compare.4, bf16[32,2048]{1,0:T(8,128)(2,1)S(1)} %dynamic-slice_bitcast_fusion.2), kind=kOutput, calls=%fused_computation.16.clone.1 | convolution fusion | flops 570695680 | bytes 1228801 | tf_op jit(solution)/shard_map/while/body/eval_jaxpr/dot_general | solution.py:43
  133.3 5.3 %fusion.91 = f32[33,4096]{1,0:T(8,128)} fusion(f32[2048]{0:T(1024)S(1)} %bitcast.75, s32[2048]{0:T(1024)S(1)} %bitcast.76, f32[33,4096]{1,0:T(8,128)} %get-tuple-element.217, pred[]{:T(512)S(6)} %compare.4, bf16[32,2048]{1,0:T(8,128)(2,1)S(1)} %dynamic-slice_bitcast_fusion.2), kind=kOutput, calls=%fused_computation.16.clone.1 | convolution fusion | flops 570695680 | bytes 1228801 | tf_op jit(solution)/shard_map/while/body/eval_jaxpr/dot_general | solution.py:43
  139.5 1.8 divide_convert_fusion
  141.3 9.9 %fusion.46 = bf16[2048,1024]{1,0:T(8,128)(2,1)} fusion(s32[1024]{0:T(1024)S(1)} %bitcast.97, s32[1024]{0:T(1024)S(1)} %bitcast.99, s32[1024]{0:T(1024)S(1)} %bitcast.83, s32[1024]{0:T(1024)S(1)} %bitcast.85, s32[1024]{0:T(1024)S(1)} %bitcast.87, s32[1024]{0:T(1024)S(1)} %bitcast.89, s32[1024]{0:T(1024)S(1)} %bitcast.91, s32[1024]{0:T(1024)S(1)} %bitcast.93, ...), kind=kLoop, calls=%fused_computation.73 | loop fusion | flops 60817408 | bytes 4243456 | tf_op jit(solution)/shard_map/add | solution.py:103
  152.5 1.7 fusion.64
  154.3 12.7 %all-gather.5.cloned.1.call-done = bf16[128,4096]{1,0:T(8,128)(2,1)} async-done(((bf16[32,4096]{1,0:T(8,128)(2,1)}), bf16[128,4096]{1,0:T(8,128)(2,1)}) %all-gather.5.cloned.1.call-update) | async-done | bytes 1048592 | tf_op jit(solution)/shard_map/all_gather | solution.py:84
  167.0 1.6 fusion.37
  171.1 7.3 %all-to-all-start.1 = ((bf16[32,2,2048]{2,1,0:T(2,128)(2,1)}), bf16[32,2,2048]{2,1,0:T(2,128)(2,1)S(1)}, u32[]{:S(2)}, u32[]{:S(2)}) async-start(bf16[32,2,2048]{2,1,0:T(2,128)(2,1)} %reshape.74), calls=%async_computation.1 | async-start | bytes 524288 | tf_op jit(solution)/shard_map/all_to_all | solution.py:93
  178.4 4.9 %fusion.73 = f32[64,1024]{1,0:T(8,128)S(1)} fusion(bf16[64,4096]{1,0:T(8,128)(2,1)S(1)} %fusion.37, bf16[4096,1024]{1,0:T(8,128)(2,1)} %fusion.27), kind=kOutput, calls=%fused_computation.108 | convolution fusion | flops 536870912 | bytes 9175040 | tf_op jit(solution)/shard_map/dot_general | solution.py:105
  183.3 3.8 %all-to-all-done.1 = bf16[32,2,2048]{2,1,0:T(2,128)(2,1)S(1)} async-done(((bf16[32,2,2048]{2,1,0:T(2,128)(2,1)}), bf16[32,2,2048]{2,1,0:T(2,128)(2,1)S(1)}, u32[]{:S(2)}, u32[]{:S(2)}) %all-to-all-start.1) | async-done | bytes 262176 | tf_op jit(solution)/shard_map/all_to_all | solution.py:93
  188.3 3.0 %fusion.53 = bf16[64,1024]{1,0:T(8,128)(2,1)S(1)} fusion(f32[64,1024]{1,0:T(8,128)S(1)} %fusion.73, bf16[64,2048]{1,0:T(8,128)(2,1)S(1)} %reshape.55, bf16[2048,1024]{1,0:T(8,128)(2,1)} %fusion.46), kind=kOutput, calls=%fused_computation.82 | convolution fusion | flops 268632064 | bytes 4849664 | tf_op jit(solution)/shard_map/dot_general | solution.py:106
  191.3 12.9 %all_gather.11 = bf16[256,1024]{1,0:T(8,128)(2,1)S(1)} all-gather(bf16[64,1024]{1,0:T(8,128)(2,1)S(1)} %fusion.53), channel_id=1, replica_groups=mesh['dom'=32,'feat'=4] {'feat'}, dimensions={0}, use_global_device_ids=true | all-gather | bytes 655360 | tf_op jit(solution)/shard_map/all_gather | solution.py:113
  204.5 2.1 fusion.54
  (87 shorter events, 13.3 us)
Async XLA Ops:
  6.5 197.7 %copy-start = (bf16[256,256]{1,0:T(8,128)(2,1)S(1)}, bf16[256,256]{1,0:T(8,128)(2,1)}, u32[]{:S(2)}) copy-start(bf16[256,256]{1,0:T(8,128)(2,1)} %param.23) | copy-start | bytes 393220
  6.5 144.7 %all-gather.3.cloned.1.call-start = ((), (), s32[]{:S(2)}) async-start(), calls=%async_computation.2 | async-start | bytes 1310720 | tf_op jit(solution)/shard_map/all_gather | solution.py:83
  58.9 11.6 %copy-start.5 = (s32[1024,10]{0,1:T(8,128)S(1)}, s32[1024,10]{0,1:T(8,128)}, u32[]{:S(2)}) copy-start(s32[1024,10]{0,1:T(8,128)} %param.19) | copy-start | bytes 122884
  59.0 34.1 %copy-start.3 = (s32[32,1,512]{2,1,0:T(1,128)S(1)}, s32[32,1,512]{2,1,0:T(1,128)}, u32[]{:S(2)}) copy-start(s32[32,1,512]{2,1,0:T(1,128)} %param.16) | copy-start | bytes 196612
  59.0 34.9 %copy-start.6 = (s32[32,1]{0,1:T(1,128)S(1)}, s32[32,1]{0,1:T(1,128)}, u32[]{:S(2)}) copy-start(s32[32,1]{0,1:T(1,128)} %param.17) | copy-start | bytes 388
  61.9 32.9 %all-to-all-start = ((bf16[32,32,512]{2,0,1:T(8,128)(2,1)}), bf16[32,32,512]{2,0,1:T(8,128)(2,1)S(1)}, u32[]{:S(2)}, u32[]{:S(2)}) async-start(bf16[32,32,512]{2,0,1:T(8,128)(2,1)} %copy.20), calls=%async_computation | async-start | bytes 2097152 | tf_op jit(solution)/shard_map/all_to_all | solution.py:75
  70.3 96.6 %all-gather.5.cloned.1.call-start = ((), (), s32[]{:S(2)}) async-start(), calls=%async_computation.3 | async-start | bytes 1310720 | tf_op jit(solution)/shard_map/all_gather | solution.py:84
  96.7 54.5 %copy-start.7 = (s32[1,64]{1,0:T(1,128)S(1)}, s32[1,64]{1,0:T(1,128)}, u32[]{:S(2)}) copy-start(s32[1,64]{1,0:T(1,128)} %param.18) | copy-start | bytes 772
  96.7 54.6 %copy-start.2 = (bf16[128,256]{1,0:T(8,128)(2,1)S(1)}, bf16[128,256]{1,0:T(8,128)(2,1)}, u32[]{:S(2)}) copy-start(bf16[128,256]{1,0:T(8,128)(2,1)} %param.20) | copy-start | bytes 196612
  138.6 28.4 %copy-start.1 = (bf16[128,256]{1,0:T(8,128)(2,1)S(1)}, bf16[128,256]{1,0:T(8,128)(2,1)}, u32[]{:S(2)}) copy-start(bf16[128,256]{1,0:T(8,128)(2,1)} %param.21) | copy-start | bytes 196612
  171.1 16.1 %all-to-all-start.1 = ((bf16[32,2,2048]{2,1,0:T(2,128)(2,1)}), bf16[32,2,2048]{2,1,0:T(2,128)(2,1)S(1)}, u32[]{:S(2)}, u32[]{:S(2)}) async-start(bf16[32,2,2048]{2,1,0:T(2,128)(2,1)} %reshape.74), calls=%async_computation.1 | async-start | bytes 524288 | tf_op jit(solution)/shard_map/all_to_all | solution.py:93
  183.3 21.2 %copy-start.4 = (bf16[256,256]{1,0:T(8,128)(2,1)S(1)}, bf16[256,256]{1,0:T(8,128)(2,1)}, u32[]{:S(2)}) copy-start(bf16[256,256]{1,0:T(8,128)(2,1)} %param.22) | copy-start | bytes 393220
Sparse Core Ops, SparseCore 0:
  9.0 26.6 all-gather.2
  141.5 25.4 all-gather.4

commit v2 on v1

--- a/solution.py
+++ b/solution.py
@@ -13,40 +13,18 @@
 
 
 def pick_columns(data, index):
-    width, extent = data.shape
-    count = index.shape[0]
-    block = math.gcd(count, 2048)
-    blocks = index.reshape(count // block, block)
+    extent = data.shape[1]
     places = jnp.arange(extent, dtype=jnp.int32)[:, None]
-
-    def one_block(chosen):
-        onehot = (places == chosen[None, :]).astype(data.dtype)
-        return jnp.dot(data, onehot, preferred_element_type=jnp.float32).astype(data.dtype)
-
-    picked = lax.map(one_block, blocks)
-    return picked.transpose(1, 0, 2).reshape(width, count)
+    onehot = (places == index[None, :]).astype(data.dtype)
+    return jnp.dot(data, onehot, preferred_element_type=jnp.float32).astype(data.dtype)
 
 
 def add_columns(values, index, weight, extent):
     width, count = values.shape
-    block = math.gcd(count, 2048)
-    nblocks = count // block
-    value_blocks = values.reshape(width, nblocks, block).transpose(1, 0, 2)
-    index_blocks = index.reshape(nblocks, block)
-    weight_blocks = weight.reshape(nblocks, block)
     places = jnp.arange(extent, dtype=jnp.int32)[None, :]
-
-    def step(total, pieces):
-        piece, chosen, scale = pieces
-        marks = jnp.where(chosen[:, None] == places, scale[:, None], 0.0)
-        piece = jnp.concatenate([piece, jnp.ones((1, block), piece.dtype)], axis=0)
-        total = total + jnp.dot(
-            piece, marks.astype(piece.dtype), preferred_element_type=jnp.float32
-        )
-        return (total, None)
-
-    start = jnp.zeros((width + 1, extent), jnp.float32)
-    total, _ = lax.scan(step, start, (value_blocks, index_blocks, weight_blocks))
+    marks = jnp.where(index[:, None] == places, weight[:, None], 0.0).astype(values.dtype)
+    values = jnp.concatenate([values, jnp.ones((1, count), values.dtype)], axis=0)
+    total = jnp.dot(values, marks, preferred_element_type=jnp.float32)
     return (total[:width], total[width])
 
 

time: 215 us -> 194 us (0.902)
  matrix products: 107 us -> 95.1 us
  local copies, waits for them, and re-layouts: 10.5 us -> 5.81 us
  other arithmetic: 35.9 us -> 32.9 us
    dot_general x16 -> x2, matrix products: 91.8 us -> 80.2 us  [the longest x1 43.8 us: pick_columns(): jnp.dot(data, onehot, preferred_element_type=jnp.float32).astype(data.dtype)]
    another operation x5 -> x0, local copies, waits for them, and re-layouts: 3.89 us -> none  [the longest x2 2.31 us: body(): pick_columns(features, sources.reshape(-1)).reshape(narrow, n_dom, slots)]
  transfers between devices with their start and end apart: 4 -> 4, of which waited for: 2 -> 2; matrix products, arithmetic and copies ran while one was open for 67% -> 64% of each run, Pallas kernels for 0% -> 0%
where the time goes in v2:
time: 194 us
  matrix products  95.1 us (49%)
  other arithmetic  32.9 us (17%)
  waiting for transfers between devices  17.4 us (9%)
  starting transfers between devices  16.2 us (8%)
  between operations  13.6 us (7%)
  blocking collectives  12.9 us (7%)
  local copies, waits for them, and re-layouts  5.81 us (3%)
    dot_general x1, matrix products, pick_columns(): jnp.dot(data, onehot, preferred_element_type=jnp.float32).astype(data.dtype)  43.8 us
    dot_general x1, matrix products, add_columns(): total = jnp.dot(values, marks, preferred_element_type=jnp.float32)  36.3 us
    add x1, other arithmetic, body(): near_tally = near_tally + (near_places == picked).astype(jnp.bfloat16)  22.4 us
    all_gather x1, waiting for transfers between devices, body(): lax.all_gather(mean_one, 'feat', axis=0, tiled=True)  13 us
    all_gather x1, blocking collectives, body(): mean_wide = lax.all_gather(mean_two, 'feat', axis=0, tiled=True)  12.9 us
    add x1, other arithmetic, body(): hub_tally = hub_tally + (hub_places == picked).astype(jnp.bfloat16)  9.65 us
    all_to_all x1, starting transfers between devices, body(): lax.all_to_all(chosen, 'dom', split_axis=1, concat_axis=1, tiled=True)  8.44 us
    all_to_all x1, starting transfers between devices, body(): lax.all_to_all(spread, 'dom', split_axis=0, concat_axis=0, tiled=True)  7.49 us
  transfers between devices with their start and end apart: 4, of which 2 were waited for; matrix products, arithmetic and copies ran while one was open for 64% of the time, Pallas kernels for 0%

profile of v2, /device:TPU:0, one launch (start us, length us, event | category | flops | bytes accessed | tf_op | source)
XLA Modules:
  0.0 193.9 jit_solution(2593924687793645579)
XLA Ops:
  6.5 0.7 all-gather.3.cloned.1.call-update
  7.3 0.9 copy.29
  8.1 43.8 %fusion.6 = bf16[16384,32]{0,1:T(8,128)(2,1)S(1)} fusion(bf16[32,4096]{1,0:T(8,128)(2,1)} %param.10, s32[16384]{0:T(1024)S(1)} %bitcast.62), kind=kOutput, calls=%fused_computation.10 | convolution fusion | flops 4362600448 | bytes 1376256 | tf_op jit(solution)/shard_map/dot_general | solution.py:19
  52.0 1.2 copy.32
  53.2 8.4 %all-to-all-start = ((bf16[32,32,512]{2,0,1:T(8,128)(2,1)}), bf16[32,32,512]{2,0,1:T(8,128)(2,1)S(1)}, u32[]{:S(2)}, u32[]{:S(2)}) async-start(bf16[32,32,512]{2,0,1:T(8,128)(2,1)} %bitcast.54), calls=%async_computation | async-start | bytes 2097152 | tf_op jit(solution)/shard_map/all_to_all | solution.py:53
  61.6 0.2 all-gather.5.cloned.1.call-start
  61.9 22.4 %fusion.17 = bf16[4096,1024]{1,0:T(8,128)(2,1)} fusion(s32[1024]{0:T(1024)S(1)} %bitcast.79, s32[1024]{0:T(1024)S(1)} %bitcast.81, s32[1024]{0:T(1024)S(1)} %bitcast.65, s32[1024]{0:T(1024)S(1)} %bitcast.67, s32[1024]{0:T(1024)S(1)} %bitcast.69, s32[1024]{0:T(1024)S(1)} %bitcast.71, s32[1024]{0:T(1024)S(1)} %bitcast.73, s32[1024]{0:T(1024)S(1)} %bitcast.75, ...), kind=kLoop, calls=%fused_computation.31 | loop fusion | flops 167772160 | bytes 8429568 | tf_op jit(solution)/shard_map/add | solution.py:80
  84.3 0.1 convert_bitcast_fusion
  84.5 0.1 copy.28
  84.6 36.3 %fusion.1 = f32[33,4096]{1,0:T(8,128)S(1)} fusion(bf16[16384]{0:T(1024)(128)(2,1)S(1)} %bitcast.83, s32[16384]{0:T(1024)S(1)} %bitcast.85, bf16[32,16384]{1,0:T(8,128)(2,1)S(1)} %bitcast.57), kind=kOutput, calls=%fused_computation.5 | convolution fusion | flops 4563402752 | bytes 1687552 | tf_op jit(solution)/shard_map/dot_general | solution.py:27
  120.9 0.8 fusion.46
  121.7 9.7 %fusion.36 = bf16[2048,1024]{1,0:T(8,128)(2,1)} fusion(s32[1024]{0:T(1024)S(1)} %bitcast.80, s32[1024]{0:T(1024)S(1)} %bitcast.82, s32[1024]{0:T(1024)S(1)} %bitcast.66, s32[1024]{0:T(1024)S(1)} %bitcast.68, s32[1024]{0:T(1024)S(1)} %bitcast.70, s32[1024]{0:T(1024)S(1)} %bitcast.72, s32[1024]{0:T(1024)S(1)} %bitcast.74, s32[1024]{0:T(1024)S(1)} %bitcast.76, ...), kind=kLoop, calls=%fused_computation.61 | loop fusion | flops 60817408 | bytes 4243456 | tf_op jit(solution)/shard_map/add | solution.py:81
  131.4 0.0 all-gather.3.cloned.1.call-done
  131.4 1.3 fusion.50
  132.7 1.6 fusion.56
  134.4 13.0 %all-gather.5.cloned.1.call-done = bf16[128,4096]{1,0:T(8,128)(2,1)} async-done(((bf16[32,4096]{1,0:T(8,128)(2,1)}), bf16[128,4096]{1,0:T(8,128)(2,1)}) %all-gather.5.cloned.1.call-update) | async-done | bytes 1048592 | tf_op jit(solution)/shard_map/all_gather | solution.py:62
  147.4 1.6 fusion.27
  149.0 0.5 copy.23
  149.5 0.6 gather_fusion
  150.1 0.1 copy.24
  150.2 0.1 broadcast_in_dim.16
  150.4 1.1 reshape.84
  151.5 7.5 %all-to-all-start.1 = ((bf16[32,2,2048]{2,1,0:T(2,128)(2,1)}), bf16[32,2,2048]{2,1,0:T(2,128)(2,1)S(1)}, u32[]{:S(2)}, u32[]{:S(2)}) async-start(bf16[32,2,2048]{2,1,0:T(2,128)(2,1)} %reshape.84), calls=%async_computation.1 | async-start | bytes 524288 | tf_op jit(solution)/shard_map/all_to_all | solution.py:71
  159.0 4.9 %fusion.67 = f32[64,1024]{1,0:T(8,128)S(1)} fusion(bf16[64,4096]{1,0:T(8,128)(2,1)S(1)} %fusion.27, bf16[4096,1024]{1,0:T(8,128)(2,1)} %fusion.17), kind=kOutput, calls=%fused_computation.101 | convolution fusion | flops 536870912 | bytes 9175040 | tf_op jit(solution)/shard_map/dot_general | solution.py:83
  163.9 3.6 %all-to-all-done.1 = bf16[32,2,2048]{2,1,0:T(2,128)(2,1)S(1)} async-done(((bf16[32,2,2048]{2,1,0:T(2,128)(2,1)}), bf16[32,2,2048]{2,1,0:T(2,128)(2,1)S(1)}, u32[]{:S(2)}, u32[]{:S(2)}) %all-to-all-start.1) | async-done | bytes 262176 | tf_op jit(solution)/shard_map/all_to_all | solution.py:71
  167.5 0.4 reshape.85
  167.9 0.3 copy.25
  168.2 0.5 reshape.74
  168.7 3.0 %fusion.44 = bf16[64,1024]{1,0:T(8,128)(2,1)S(1)} fusion(f32[64,1024]{1,0:T(8,128)S(1)} %fusion.67, bf16[64,2048]{1,0:T(8,128)(2,1)S(1)} %reshape.74, bf16[2048,1024]{1,0:T(8,128)(2,1)} %fusion.36), kind=kOutput, calls=%fused_computation.71 | convolution fusion | flops 268632064 | bytes 4849664 | tf_op jit(solution)/shard_map/dot_general | solution.py:84
  171.7 12.9 %all_gather.11 = bf16[256,1024]{1,0:T(8,128)(2,1)S(1)} all-gather(bf16[64,1024]{1,0:T(8,128)(2,1)S(1)} %fusion.44), channel_id=1, replica_groups=mesh['dom'=32,'feat'=4] {'feat'}, dimensions={0}, use_global_device_ids=true | all-gather | bytes 655360 | tf_op jit(solution)/shard_map/all_gather | solution.py:91
  184.6 0.3 fusion.52
  184.9 2.1 %fusion.45 = bf16[64,1024]{1,0:T(8,128)(2,1)} fusion(f32[64,1024]{1,0:T(8,128)S(1)} %fusion.52, f32[256,1024]{1,0:T(8,128)S(1)} %fusion.50, bf16[128,256]{1,0:T(8,128)(2,1)S(1)} %copy-done.1, bf16[128,4096]{1,0:T(8,128)(2,1)} %all-gather.5.cloned.1.call-done, bf16[256,256]{1,0:T(8,128)(2,1)S(1)} %copy-done.3, s32[]{:T(128)S(6)} %select_n.20), kind=kOutput, calls=%fused_computation.72 | convolution fusion | flops 101580800 | bytes 1835012 | tf_op jit(solution)/shard_map/dot_general | solution.py:10
  (25 shorter events, 0.1 us)
Async XLA Ops:
  6.5 178.1 %copy-start = (bf16[256,256]{1,0:T(8,128)(2,1)S(1)}, bf16[256,256]{1,0:T(8,128)(2,1)}, u32[]{:S(2)}) copy-start(bf16[256,256]{1,0:T(8,128)(2,1)} %param.19) | copy-start | bytes 393220
  6.5 124.9 %all-gather.3.cloned.1.call-start = ((), (), s32[]{:S(2)}) async-start(), calls=%async_computation.2 | async-start | bytes 1310720 | tf_op jit(solution)/shard_map/all_gather | solution.py:61
  8.1 53.8 %copy-start.4 = (s32[1024,10]{0,1:T(8,128)S(1)}, s32[1024,10]{0,1:T(8,128)}, u32[]{:S(2)}) copy-start(s32[1024,10]{0,1:T(8,128)} %param.15) | copy-start | bytes 122884
  52.0 32.4 %copy-start.5 = (s32[32,1]{0,1:T(1,128)S(1)}, s32[32,1]{0,1:T(1,128)}, u32[]{:S(2)}) copy-start(s32[32,1]{0,1:T(1,128)} %param.13) | copy-start | bytes 388
  52.0 32.6 %copy-start.6 = (s32[32,1,512]{2,1,0:T(1,128)S(1)}, s32[32,1,512]{2,1,0:T(1,128)}, u32[]{:S(2)}) copy-start(s32[32,1,512]{2,1,0:T(1,128)} %param.12) | copy-start | bytes 196612
  53.2 31.3 %all-to-all-start = ((bf16[32,32,512]{2,0,1:T(8,128)(2,1)}), bf16[32,32,512]{2,0,1:T(8,128)(2,1)S(1)}, u32[]{:S(2)}, u32[]{:S(2)}) async-start(bf16[32,32,512]{2,0,1:T(8,128)(2,1)} %bitcast.54), calls=%async_computation | async-start | bytes 2097152 | tf_op jit(solution)/shard_map/all_to_all | solution.py:53
  61.6 85.7 %all-gather.5.cloned.1.call-start = ((), (), s32[]{:S(2)}) async-start(), calls=%async_computation.3 | async-start | bytes 1310720 | tf_op jit(solution)/shard_map/all_gather | solution.py:62
  84.6 46.8 %copy-start.7 = (s32[1,64]{1,0:T(1,128)S(1)}, s32[1,64]{1,0:T(1,128)}, u32[]{:S(2)}) copy-start(s32[1,64]{1,0:T(1,128)} %param.14) | copy-start | bytes 772
  84.6 46.9 %copy-start.2 = (bf16[128,256]{1,0:T(8,128)(2,1)S(1)}, bf16[128,256]{1,0:T(8,128)(2,1)}, u32[]{:S(2)}) copy-start(bf16[128,256]{1,0:T(8,128)(2,1)} %param.16) | copy-start | bytes 196612
  120.9 26.5 %copy-start.1 = (bf16[128,256]{1,0:T(8,128)(2,1)S(1)}, bf16[128,256]{1,0:T(8,128)(2,1)}, u32[]{:S(2)}) copy-start(bf16[128,256]{1,0:T(8,128)(2,1)} %param.17) | copy-start | bytes 196612
  151.5 16.1 %all-to-all-start.1 = ((bf16[32,2,2048]{2,1,0:T(2,128)(2,1)}), bf16[32,2,2048]{2,1,0:T(2,128)(2,1)S(1)}, u32[]{:S(2)}, u32[]{:S(2)}) async-start(bf16[32,2,2048]{2,1,0:T(2,128)(2,1)} %reshape.84), calls=%async_computation.1 | async-start | bytes 524288 | tf_op jit(solution)/shard_map/all_to_all | solution.py:71
  163.9 21.0 %copy-start.3 = (bf16[256,256]{1,0:T(8,128)(2,1)S(1)}, bf16[256,256]{1,0:T(8,128)(2,1)}, u32[]{:S(2)}) copy-start(bf16[256,256]{1,0:T(8,128)(2,1)} %param.18) | copy-start | bytes 393220
Sparse Core Ops, SparseCore 0:
  9.0 26.6 all-gather.2
  121.8 25.4 all-gather.4

commit v3 on v2

--- a/solution.py
+++ b/solution.py
@@ -13,10 +13,7 @@
 
 
 def pick_columns(data, index):
-    extent = data.shape[1]
-    places = jnp.arange(extent, dtype=jnp.int32)[:, None]
-    onehot = (places == index[None, :]).astype(data.dtype)
-    return jnp.dot(data, onehot, preferred_element_type=jnp.float32).astype(data.dtype)
+    return jnp.take(data.T, index, axis=0, mode="clip").T
 
 
 def add_columns(values, index, weight, extent):

time: 194 us -> 213 us (1.098)
  local copies, waits for them, and re-layouts: 5.81 us -> 68.5 us
  matrix products: 95.1 us -> 51.3 us
    gather x0 -> x1, local copies, waits for them, and re-layouts: none -> 57.8 us  [pick_columns(): return jnp.take(data.T, index, axis=0, mode='clip').T]
    dot_general x1 -> x0, matrix products: 43.8 us -> none  [pick_columns(): jnp.dot(data, onehot, preferred_element_type=jnp.float32).astype(data.dtype)]
    reshape x1, local copies, waits for them, and re-layouts: 1.19 us -> 4.61 us  [body(): pick_columns(features, sources.reshape(-1)).reshape(narrow, n_dom, slots)]
  transfers between devices with their start and end apart: 4 -> 4, of which waited for: 2 -> 2; matrix products, arithmetic and copies ran while one was open for 64% -> 67% of each run, Pallas kernels for 0% -> 0%
where the time goes in v3:
time: 213 us
  local copies, waits for them, and re-layouts  68.5 us (32%)
  matrix products  51.3 us (24%)
  other arithmetic  32.9 us (15%)
  waiting for transfers between devices  17.4 us (8%)
  starting transfers between devices  15.9 us (7%)
  between operations  13.6 us (6%)
  blocking collectives  12.9 us (6%)
    gather x1, local copies, waits for them, and re-layouts, pick_columns(): return jnp.take(data.T, index, axis=0, mode='clip').T  57.8 us
    dot_general x1, matrix products, add_columns(): total = jnp.dot(values, marks, preferred_element_type=jnp.float32)  36.3 us
    add x1, other arithmetic, body(): near_tally = near_tally + (near_places == picked).astype(jnp.bfloat16)  22.4 us
    all_gather x1, waiting for transfers between devices, body(): lax.all_gather(mean_one, 'feat', axis=0, tiled=True)  13 us
    all_gather x1, blocking collectives, body(): mean_wide = lax.all_gather(mean_two, 'feat', axis=0, tiled=True)  12.9 us
    add x1, other arithmetic, body(): hub_tally = hub_tally + (hub_places == picked).astype(jnp.bfloat16)  9.65 us
    all_to_all x1, starting transfers between devices, body(): lax.all_to_all(chosen, 'dom', split_axis=1, concat_axis=1, tiled=True)  8.44 us
    all_to_all x1, starting transfers between devices, body(): lax.all_to_all(spread, 'dom', split_axis=0, concat_axis=0, tiled=True)  7.45 us
  transfers between devices with their start and end apart: 4, of which 2 were waited for; matrix products, arithmetic and copies ran while one was open for 67% of the time, Pallas kernels for 0%

profile of v3, /device:TPU:0, one launch (start us, length us, event | category | flops | bytes accessed | tf_op | source)
XLA Modules:
  0.0 212.5 jit_solution(11585790907825360113)
XLA Ops:
  6.5 0.7 all-gather.3.cloned.1.call-update
  7.3 1.4 copy.23
  8.7 0.9 copy.32
  9.6 57.8 %gather_fusion = bf16[16384,32]{1,0:T(8,128)(2,1)} fusion(bf16[4096,32]{1,0:T(8,128)(2,1)S(1)} %bitcast.53, s32[16384]{0:T(1024)S(1)} %broadcast_clamp_fusion), kind=kCustom, calls=%fused_computation | custom fusion | bytes 2162688 | tf_op jit(solution)/shard_map/jit(_take)/gather | solution.py:16
  67.4 4.6 %copy.24 = bf16[32,32,512]{2,0,1:T(8,128)(2,1)} copy(bf16[32,32,512]{0,2,1:T(8,128)(2,1)} %bitcast.54) | data formatting | bytes 2097152 | tf_op jit(solution)/shard_map/reshape | solution.py:49
  72.0 8.4 %all-to-all-start = ((bf16[32,32,512]{2,0,1:T(8,128)(2,1)}), bf16[32,32,512]{2,0,1:T(8,128)(2,1)S(1)}, u32[]{:S(2)}, u32[]{:S(2)}) async-start(bf16[32,32,512]{2,0,1:T(8,128)(2,1)} %copy.24), calls=%async_computation | async-start | bytes 2097152 | tf_op jit(solution)/shard_map/all_to_all | solution.py:50
  80.5 0.0 all-gather.5.cloned.1.call-start
  80.6 22.4 %fusion.14 = bf16[4096,1024]{1,0:T(8,128)(2,1)} fusion(s32[1024]{0:T(1024)S(1)} %bitcast.78, s32[1024]{0:T(1024)S(1)} %bitcast.80, s32[1024]{0:T(1024)S(1)} %bitcast.64, s32[1024]{0:T(1024)S(1)} %bitcast.66, s32[1024]{0:T(1024)S(1)} %bitcast.68, s32[1024]{0:T(1024)S(1)} %bitcast.70, s32[1024]{0:T(1024)S(1)} %bitcast.72, s32[1024]{0:T(1024)S(1)} %bitcast.74, ...), kind=kLoop, calls=%fused_computation.28 | loop fusion | flops 167772160 | bytes 8429568 | tf_op jit(solution)/shard_map/add | solution.py:77
  103.0 0.1 convert_bitcast_fusion
  103.1 0.1 copy.31
  103.2 36.3 %fusion = f32[33,4096]{1,0:T(8,128)S(1)} fusion(bf16[16384]{0:T(1024)(128)(2,1)S(1)} %bitcast.82, s32[16384]{0:T(1024)S(1)} %bitcast.84, bf16[32,16384]{1,0:T(8,128)(2,1)S(1)} %bitcast.57), kind=kOutput, calls=%fused_computation.4 | convolution fusion | flops 4563402752 | bytes 1687552 | tf_op jit(solution)/shard_map/dot_general | solution.py:24
  139.6 0.8 fusion.43
  140.4 9.7 %fusion.33 = bf16[2048,1024]{1,0:T(8,128)(2,1)} fusion(s32[1024]{0:T(1024)S(1)} %bitcast.79, s32[1024]{0:T(1024)S(1)} %bitcast.81, s32[1024]{0:T(1024)S(1)} %bitcast.65, s32[1024]{0:T(1024)S(1)} %bitcast.67, s32[1024]{0:T(1024)S(1)} %bitcast.69, s32[1024]{0:T(1024)S(1)} %bitcast.71, s32[1024]{0:T(1024)S(1)} %bitcast.73, s32[1024]{0:T(1024)S(1)} %bitcast.75, ...), kind=kLoop, calls=%fused_computation.58 | loop fusion | flops 60817408 | bytes 4243456 | tf_op jit(solution)/shard_map/add | solution.py:78
  150.1 1.3 fusion.47
  151.4 1.6 fusion.53
  153.0 13.0 %all-gather.5.cloned.1.call-done = bf16[128,4096]{1,0:T(8,128)(2,1)} async-done(((bf16[32,4096]{1,0:T(8,128)(2,1)}), bf16[128,4096]{1,0:T(8,128)(2,1)}) %all-gather.5.cloned.1.call-update) | async-done | bytes 1048592 | tf_op jit(solution)/shard_map/all_gather | solution.py:59
  166.0 1.6 fusion.24
  167.7 0.5 copy.27
  168.1 0.6 gather_fusion.1
  168.8 0.1 copy.28
  168.9 0.1 broadcast_in_dim.32
  169.0 1.1 reshape.93
  170.1 7.5 %all-to-all-start.1 = ((bf16[32,2,2048]{2,1,0:T(2,128)(2,1)}), bf16[32,2,2048]{2,1,0:T(2,128)(2,1)S(1)}, u32[]{:S(2)}, u32[]{:S(2)}) async-start(bf16[32,2,2048]{2,1,0:T(2,128)(2,1)} %reshape.93), calls=%async_computation.1 | async-start | bytes 524288 | tf_op jit(solution)/shard_map/all_to_all | solution.py:68
  177.6 4.9 %fusion.64 = f32[64,1024]{1,0:T(8,128)S(1)} fusion(bf16[64,4096]{1,0:T(8,128)(2,1)S(1)} %fusion.24, bf16[4096,1024]{1,0:T(8,128)(2,1)} %fusion.14), kind=kOutput, calls=%fused_computation.98 | convolution fusion | flops 536870912 | bytes 9175040 | tf_op jit(solution)/shard_map/dot_general | solution.py:80
  182.5 3.6 %all-to-all-done.1 = bf16[32,2,2048]{2,1,0:T(2,128)(2,1)S(1)} async-done(((bf16[32,2,2048]{2,1,0:T(2,128)(2,1)}), bf16[32,2,2048]{2,1,0:T(2,128)(2,1)S(1)}, u32[]{:S(2)}, u32[]{:S(2)}) %all-to-all-start.1) | async-done | bytes 262176 | tf_op jit(solution)/shard_map/all_to_all | solution.py:68
  186.2 0.4 reshape.94
  186.5 0.3 copy.29
  186.9 0.5 reshape.74
  187.3 3.0 %fusion.41 = bf16[64,1024]{1,0:T(8,128)(2,1)S(1)} fusion(f32[64,1024]{1,0:T(8,128)S(1)} %fusion.64, bf16[64,2048]{1,0:T(8,128)(2,1)S(1)} %reshape.74, bf16[2048,1024]{1,0:T(8,128)(2,1)} %fusion.33), kind=kOutput, calls=%fused_computation.68 | convolution fusion | flops 268632064 | bytes 4849664 | tf_op jit(solution)/shard_map/dot_general | solution.py:81
  190.4 12.9 %all_gather.11 = bf16[256,1024]{1,0:T(8,128)(2,1)S(1)} all-gather(bf16[64,1024]{1,0:T(8,128)(2,1)S(1)} %fusion.41), channel_id=1, replica_groups=mesh['dom'=32,'feat'=4] {'feat'}, dimensions={0}, use_global_device_ids=true | all-gather | bytes 655360 | tf_op jit(solution)/shard_map/all_gather | solution.py:88
  203.3 0.3 fusion.49
  203.6 2.1 fusion.42
  (27 shorter events, 0.2 us)
Async XLA Ops:
  6.5 196.7 %copy-start = (bf16[256,256]{1,0:T(8,128)(2,1)S(1)}, bf16[256,256]{1,0:T(8,128)(2,1)}, u32[]{:S(2)}) copy-start(bf16[256,256]{1,0:T(8,128)(2,1)} %param.19) | copy-start | bytes 393220
  6.5 143.5 %all-gather.3.cloned.1.call-start = ((), (), s32[]{:S(2)}) async-start(), calls=%async_computation.2 | async-start | bytes 1310720 | tf_op jit(solution)/shard_map/all_gather | solution.py:58
  9.6 70.9 %copy-start.4 = (s32[1024,10]{0,1:T(8,128)S(1)}, s32[1024,10]{0,1:T(8,128)}, u32[]{:S(2)}) copy-start(s32[1024,10]{0,1:T(8,128)} %param.15) | copy-start | bytes 122884
  67.4 35.6 %copy-start.5 = (s32[32,1]{0,1:T(1,128)S(1)}, s32[32,1]{0,1:T(1,128)}, u32[]{:S(2)}) copy-start(s32[32,1]{0,1:T(1,128)} %param.13) | copy-start | bytes 388
  67.4 35.8 %copy-start.6 = (s32[32,1,512]{2,1,0:T(1,128)S(1)}, s32[32,1,512]{2,1,0:T(1,128)}, u32[]{:S(2)}) copy-start(s32[32,1,512]{2,1,0:T(1,128)} %param.12) | copy-start | bytes 196612
  72.0 31.1 %all-to-all-start = ((bf16[32,32,512]{2,0,1:T(8,128)(2,1)}), bf16[32,32,512]{2,0,1:T(8,128)(2,1)S(1)}, u32[]{:S(2)}, u32[]{:S(2)}) async-start(bf16[32,32,512]{2,0,1:T(8,128)(2,1)} %copy.24), calls=%async_computation | async-start | bytes 2097152 | tf_op jit(solution)/shard_map/all_to_all | solution.py:50
  80.5 85.6 %all-gather.5.cloned.1.call-start = ((), (), s32[]{:S(2)}) async-start(), calls=%async_computation.3 | async-start | bytes 1310720 | tf_op jit(solution)/shard_map/all_gather | solution.py:59
  103.2 46.8 %copy-start.7 = (s32[1,64]{1,0:T(1,128)S(1)}, s32[1,64]{1,0:T(1,128)}, u32[]{:S(2)}) copy-start(s32[1,64]{1,0:T(1,128)} %param.14) | copy-start | bytes 772
  103.2 46.9 %copy-start.2 = (bf16[128,256]{1,0:T(8,128)(2,1)S(1)}, bf16[128,256]{1,0:T(8,128)(2,1)}, u32[]{:S(2)}) copy-start(bf16[128,256]{1,0:T(8,128)(2,1)} %param.16) | copy-start | bytes 196612
  139.6 26.5 %copy-start.1 = (bf16[128,256]{1,0:T(8,128)(2,1)S(1)}, bf16[128,256]{1,0:T(8,128)(2,1)}, u32[]{:S(2)}) copy-start(bf16[128,256]{1,0:T(8,128)(2,1)} %param.17) | copy-start | bytes 196612
  170.1 16.1 %all-to-all-start.1 = ((bf16[32,2,2048]{2,1,0:T(2,128)(2,1)}), bf16[32,2,2048]{2,1,0:T(2,128)(2,1)S(1)}, u32[]{:S(2)}, u32[]{:S(2)}) async-start(bf16[32,2,2048]{2,1,0:T(2,128)(2,1)} %reshape.93), calls=%async_computation.1 | async-start | bytes 524288 | tf_op jit(solution)/shard_map/all_to_all | solution.py:68
  182.5 21.0 %copy-start.3 = (bf16[256,256]{1,0:T(8,128)(2,1)S(1)}, bf16[256,256]{1,0:T(8,128)(2,1)}, u32[]{:S(2)}) copy-start(bf16[256,256]{1,0:T(8,128)(2,1)} %param.18) | copy-start | bytes 393220
Sparse Core Ops, SparseCore 0:
  9.0 26.5 all-gather.2
  140.5 25.4 all-gather.4

commit v4 on v2

--- a/solution.py
+++ b/solution.py
@@ -14,15 +14,17 @@
 
 def pick_columns(data, index):
     extent = data.shape[1]
-    places = jnp.arange(extent, dtype=jnp.int32)[:, None]
-    onehot = (places == index[None, :]).astype(data.dtype)
+    places = jnp.arange(extent, dtype=jnp.int16)[:, None]
+    onehot = (places == index.astype(jnp.int16)[None, :]).astype(data.dtype)
     return jnp.dot(data, onehot, preferred_element_type=jnp.float32).astype(data.dtype)
 
 
 def add_columns(values, index, weight, extent):
     width, count = values.shape
-    places = jnp.arange(extent, dtype=jnp.int32)[None, :]
-    marks = jnp.where(index[:, None] == places, weight[:, None], 0.0).astype(values.dtype)
+    places = jnp.arange(extent, dtype=jnp.int16)[None, :]
+    marks = jnp.where(
+        index.astype(jnp.int16)[:, None] == places, weight.astype(values.dtype)[:, None], 0.0
+    ).astype(values.dtype)
     values = jnp.concatenate([values, jnp.ones((1, count), values.dtype)], axis=0)
     total = jnp.dot(values, marks, preferred_element_type=jnp.float32)
     return (total[:width], total[width])
@@ -71,12 +73,12 @@
     landed = lax.all_to_all(spread, "dom", split_axis=0, concat_axis=0, tiled=True)
     hub_table = landed.transpose(1, 0, 2).reshape(hidden_one.shape[0], n_dom * hub_count)
     tgt_dev, fanout = second_source.shape
-    near_places = jnp.arange(node_dev, dtype=jnp.int32)[:, None]
-    hub_places = node_dev + jnp.arange(n_dom * hub_count, dtype=jnp.int32)[:, None]
+    near_places = jnp.arange(node_dev, dtype=jnp.int16)[:, None]
+    hub_places = (node_dev + jnp.arange(n_dom * hub_count, dtype=jnp.int32)).astype(jnp.int16)[:, None]
     near_tally = jnp.zeros((node_dev, tgt_dev), jnp.bfloat16)
     hub_tally = jnp.zeros((n_dom * hub_count, tgt_dev), jnp.bfloat16)
     for column in range(fanout):
-        picked = second_source[:, column][None, :]
+        picked = second_source[:, column].astype(jnp.int16)[None, :]
         near_tally = near_tally + (near_places == picked).astype(jnp.bfloat16)
         hub_tally = hub_tally + (hub_places == picked).astype(jnp.bfloat16)
     near_tally, hub_tally = lax.optimization_barrier((near_tally, hub_tally))

time: 194 us -> 190 us (0.979)
  other arithmetic: 32.9 us -> 29.7 us
    add x1, other arithmetic: 22.4 us -> 18 us  [body(): near_tally = near_tally + (near_places == picked).astype(jnp.bfloat16)]
  transfers between devices with their start and end apart: 4 -> 4, of which waited for: 2 -> 2; matrix products, arithmetic and copies ran while one was open for 64% -> 63% of each run, Pallas kernels for 0% -> 0%
where the time goes in v4:
time: 190 us
  matrix products  95.2 us (50%)
  other arithmetic  29.7 us (16%)
  waiting for transfers between devices  17.1 us (9%)
  starting transfers between devices  16.2 us (9%)
  between operations  13.7 us (7%)
  blocking collectives  12.9 us (7%)
  local copies, waits for them, and re-layouts  5.07 us (3%)
    dot_general x1, matrix products, pick_columns(): jnp.dot(data, onehot, preferred_element_type=jnp.float32).astype(data.dtype)  44.3 us
    dot_general x1, matrix products, add_columns(): total = jnp.dot(values, marks, preferred_element_type=jnp.float32)  35.8 us
    add x1, other arithmetic, body(): near_tally = near_tally + (near_places == picked).astype(jnp.bfloat16)  18 us
    all_gather x1, blocking collectives, body(): mean_wide = lax.all_gather(mean_two, 'feat', axis=0, tiled=True)  12.9 us
    all_gather x1, waiting for transfers between devices, body(): lax.all_gather(mean_one, 'feat', axis=0, tiled=True)  12.7 us
    add x1, other arithmetic, body(): hub_tally = hub_tally + (hub_places == picked).astype(jnp.bfloat16)  9.88 us
    all_to_all x1, starting transfers between devices, body(): lax.all_to_all(chosen, 'dom', split_axis=1, concat_axis=1, tiled=True)  8.45 us
    all_to_all x1, starting transfers between devices, body(): lax.all_to_all(spread, 'dom', split_axis=0, concat_axis=0, tiled=True)  7.48 us
  transfers between devices with their start and end apart: 4, of which 2 were waited for; matrix products, arithmetic and copies ran while one was open for 63% of the time, Pallas kernels for 0%

profile of v4, /device:TPU:0, one launch (start us, length us, event | category | flops | bytes accessed | tf_op | source)
XLA Modules:
  0.0 189.7 jit_solution(7853901094159413932)
XLA Ops:
  6.5 0.7 all-gather.3.cloned.1.call-update
  7.3 0.8 convert_bitcast_fusion
  8.1 44.3 %fusion.9 = bf16[16384,32]{0,1:T(8,128)(2,1)S(1)} fusion(bf16[32,4096]{1,0:T(8,128)(2,1)} %param.10, s16[16384]{0:T(1024)(128)(2,1)S(1)} %bitcast.56), kind=kOutput, calls=%fused_computation.11 | convolution fusion | flops 4362600448 | bytes 1343488 | tf_op jit(solution)/shard_map/dot_general | solution.py:19
  52.5 1.2 copy.33
  53.7 8.4 %all-to-all-start = ((bf16[32,32,512]{2,0,1:T(8,128)(2,1)}), bf16[32,32,512]{2,0,1:T(8,128)(2,1)S(1)}, u32[]{:S(2)}, u32[]{:S(2)}) async-start(bf16[32,32,512]{2,0,1:T(8,128)(2,1)} %bitcast.46), calls=%async_computation | async-start | bytes 2097152 | tf_op jit(solution)/shard_map/all_to_all | solution.py:55
  62.1 0.2 all-gather.5.cloned.1.call-start
  62.4 0.1 slice_reduce_fusion.9
  62.5 18.0 %fusion.20 = bf16[4096,1024]{1,0:T(8,128)(2,1)} fusion(s16[1024]{0:T(1024)(128)(2,1)S(1)} %get-tuple-element.10, s16[1024]{0:T(1024)(128)(2,1)S(1)} %get-tuple-element.11, s16[1024]{0:T(1024)(128)(2,1)S(1)} %get-tuple-element.12, s16[1024]{0:T(1024)(128)(2,1)S(1)} %get-tuple-element.13, s16[1024]{0:T(1024)(128)(2,1)S(1)} %get-tuple-element.14, ...), kind=kLoop, calls=%fused_computation.30 | loop fusion | flops 167772160 | bytes 8409088 | tf_op jit(solution)/shard_map/add | solution.py:82
  80.6 0.1 convert_reduce_fusion
  80.8 0.1 copy.28
  80.9 35.8 %fusion.2 = f32[33,4096]{1,0:T(8,128)S(1)} fusion(bf16[16384]{0:T(1024)(128)(2,1)S(1)} %bitcast.54, s16[16384]{0:T(1024)(128)(2,1)S(1)} %bitcast.55, bf16[32,16384]{1,0:T(8,128)(2,1)S(1)} %bitcast.49), kind=kOutput, calls=%fused_computation.4 | convolution fusion | flops 4563402752 | bytes 1654784 | tf_op jit(solution)/shard_map/dot_general | solution.py:29
  116.8 0.7 fusion.41
  117.6 9.9 %fusion.31 = bf16[2048,1024]{1,0:T(8,128)(2,1)} fusion(s16[1024]{0:T(1024)(128)(2,1)S(1)} %get-tuple-element.10, s16[1024]{0:T(1024)(128)(2,1)S(1)} %get-tuple-element.11, s16[1024]{0:T(1024)(128)(2,1)S(1)} %get-tuple-element.12, s16[1024]{0:T(1024)(128)(2,1)S(1)} %get-tuple-element.13, s16[1024]{0:T(1024)(128)(2,1)S(1)} %get-tuple-element.14, ...), kind=kLoop, calls=%fused_computation.52 | loop fusion | flops 60817408 | bytes 4218880 | tf_op jit(solution)/shard_map/add | solution.py:83
  127.5 1.3 fusion.45
  128.8 1.7 fusion.52
  130.5 12.7 %all-gather.5.cloned.1.call-done = bf16[128,4096]{1,0:T(8,128)(2,1)} async-done(((bf16[32,4096]{1,0:T(8,128)(2,1)}), bf16[128,4096]{1,0:T(8,128)(2,1)}) %all-gather.5.cloned.1.call-update) | async-done | bytes 1048592 | tf_op jit(solution)/shard_map/all_gather | solution.py:64
  143.2 1.6 fusion.22
  144.9 0.5 copy.23
  145.4 0.6 gather_fusion
  146.0 0.1 copy.24
  146.1 0.1 broadcast_in_dim.16
  146.2 1.1 reshape.154
  147.3 7.5 %all-to-all-start.1 = ((bf16[32,2,2048]{2,1,0:T(2,128)(2,1)}), bf16[32,2,2048]{2,1,0:T(2,128)(2,1)S(1)}, u32[]{:S(2)}, u32[]{:S(2)}) async-start(bf16[32,2,2048]{2,1,0:T(2,128)(2,1)} %reshape.154), calls=%async_computation.1 | async-start | bytes 524288 | tf_op jit(solution)/shard_map/all_to_all | solution.py:73
  154.8 4.9 %fusion.62 = f32[64,1024]{1,0:T(8,128)S(1)} fusion(bf16[64,4096]{1,0:T(8,128)(2,1)S(1)} %fusion.22, bf16[4096,1024]{1,0:T(8,128)(2,1)} %fusion.20), kind=kOutput, calls=%fused_computation.104 | convolution fusion | flops 536870912 | bytes 9175040 | tf_op jit(solution)/shard_map/dot_general | solution.py:85
  159.8 3.6 %all-to-all-done.1 = bf16[32,2,2048]{2,1,0:T(2,128)(2,1)S(1)} async-done(((bf16[32,2,2048]{2,1,0:T(2,128)(2,1)}), bf16[32,2,2048]{2,1,0:T(2,128)(2,1)S(1)}, u32[]{:S(2)}, u32[]{:S(2)}) %all-to-all-start.1) | async-done | bytes 262176 | tf_op jit(solution)/shard_map/all_to_all | solution.py:73
  163.4 0.4 reshape.155
  163.7 0.3 copy.25
  164.1 0.5 reshape.134
  164.5 3.0 %fusion.39 = bf16[64,1024]{1,0:T(8,128)(2,1)S(1)} fusion(f32[64,1024]{1,0:T(8,128)S(1)} %fusion.62, bf16[64,2048]{1,0:T(8,128)(2,1)S(1)} %reshape.134, bf16[2048,1024]{1,0:T(8,128)(2,1)} %fusion.31), kind=kOutput, calls=%fused_computation.62 | convolution fusion | flops 268632064 | bytes 4849664 | tf_op jit(solution)/shard_map/dot_general | solution.py:86
  167.6 12.9 %all_gather.11 = bf16[256,1024]{1,0:T(8,128)(2,1)S(1)} all-gather(bf16[64,1024]{1,0:T(8,128)(2,1)S(1)} %fusion.39), channel_id=1, replica_groups=mesh['dom'=32,'feat'=4] {'feat'}, dimensions={0}, use_global_device_ids=true | all-gather | bytes 655360 | tf_op jit(solution)/shard_map/all_gather | solution.py:93
  180.5 0.3 fusion.47
  180.8 2.1 %fusion.40 = bf16[64,1024]{1,0:T(8,128)(2,1)} fusion(f32[64,1024]{1,0:T(8,128)S(1)} %fusion.47, f32[256,1024]{1,0:T(8,128)S(1)} %fusion.45, bf16[128,256]{1,0:T(8,128)(2,1)S(1)} %copy-done.1, bf16[128,4096]{1,0:T(8,128)(2,1)} %all-gather.5.cloned.1.call-done, bf16[256,256]{1,0:T(8,128)(2,1)S(1)} %copy-done.5, s32[]{:T(128)S(6)} %select_n.20), kind=kOutput, calls=%fused_computation.63 | convolution fusion | flops 101580800 | bytes 1835012 | tf_op jit(solution)/shard_map/dot_general | solution.py:10
  (29 shorter events, 0.2 us)
Async XLA Ops:
  6.5 173.9 %copy-start = (bf16[256,256]{1,0:T(8,128)(2,1)S(1)}, bf16[256,256]{1,0:T(8,128)(2,1)}, u32[]{:S(2)}) copy-start(bf16[256,256]{1,0:T(8,128)(2,1)} %param.19) | copy-start | bytes 393220
  6.5 121.0 %all-gather.3.cloned.1.call-start = ((), (), s32[]{:S(2)}) async-start(), calls=%async_computation.2 | async-start | bytes 1310720 | tf_op jit(solution)/shard_map/all_gather | solution.py:63
  8.1 54.3 %copy-start.3 = (s32[1024,10]{0,1:T(8,128)S(1)}, s32[1024,10]{0,1:T(8,128)}, u32[]{:S(2)}) copy-start(s32[1024,10]{0,1:T(8,128)} %param.15) | copy-start | bytes 122884
  52.5 28.0 %copy-start.6 = (s32[32,1]{0,1:T(1,128)S(1)}, s32[32,1]{0,1:T(1,128)}, u32[]{:S(2)}) copy-start(s32[32,1]{0,1:T(1,128)} %param.13) | copy-start | bytes 388
  52.5 28.1 %copy-start.4 = (s32[32,1,512]{2,1,0:T(1,128)S(1)}, s32[32,1,512]{2,1,0:T(1,128)}, u32[]{:S(2)}) copy-start(s32[32,1,512]{2,1,0:T(1,128)} %param.12) | copy-start | bytes 196612
  53.7 27.1 %all-to-all-start = ((bf16[32,32,512]{2,0,1:T(8,128)(2,1)}), bf16[32,32,512]{2,0,1:T(8,128)(2,1)S(1)}, u32[]{:S(2)}, u32[]{:S(2)}) async-start(bf16[32,32,512]{2,0,1:T(8,128)(2,1)} %bitcast.46), calls=%async_computation | async-start | bytes 2097152 | tf_op jit(solution)/shard_map/all_to_all | solution.py:55
  62.1 81.1 %all-gather.5.cloned.1.call-start = ((), (), s32[]{:S(2)}) async-start(), calls=%async_computation.3 | async-start | bytes 1310720 | tf_op jit(solution)/shard_map/all_gather | solution.py:64
  80.9 46.6 %copy-start.7 = (s32[1,64]{1,0:T(1,128)S(1)}, s32[1,64]{1,0:T(1,128)}, u32[]{:S(2)}) copy-start(s32[1,64]{1,0:T(1,128)} %param.14) | copy-start | bytes 772
  80.9 46.6 %copy-start.2 = (bf16[128,256]{1,0:T(8,128)(2,1)S(1)}, bf16[128,256]{1,0:T(8,128)(2,1)}, u32[]{:S(2)}) copy-start(bf16[128,256]{1,0:T(8,128)(2,1)} %param.16) | copy-start | bytes 196612
  116.8 26.5 %copy-start.1 = (bf16[128,256]{1,0:T(8,128)(2,1)S(1)}, bf16[128,256]{1,0:T(8,128)(2,1)}, u32[]{:S(2)}) copy-start(bf16[128,256]{1,0:T(8,128)(2,1)} %param.17) | copy-start | bytes 196612
  147.3 16.1 %all-to-all-start.1 = ((bf16[32,2,2048]{2,1,0:T(2,128)(2,1)}), bf16[32,2,2048]{2,1,0:T(2,128)(2,1)S(1)}, u32[]{:S(2)}, u32[]{:S(2)}) async-start(bf16[32,2,2048]{2,1,0:T(2,128)(2,1)} %reshape.154), calls=%async_computation.1 | async-start | bytes 524288 | tf_op jit(solution)/shard_map/all_to_all | solution.py:73
  159.8 21.0 %copy-start.5 = (bf16[256,256]{1,0:T(8,128)(2,1)S(1)}, bf16[256,256]{1,0:T(8,128)(2,1)}, u32[]{:S(2)}) copy-start(bf16[256,256]{1,0:T(8,128)(2,1)} %param.18) | copy-start | bytes 393220
Sparse Core Ops, SparseCore 0:
  9.0 26.7 all-gather.2
  117.7 25.4 all-gather.4

commit v5 on v4

--- a/solution.py
+++ b/solution.py
@@ -12,21 +12,33 @@
     )
 
 
-def pick_columns(data, index):
-    extent = data.shape[1]
-    places = jnp.arange(extent, dtype=jnp.int16)[:, None]
-    onehot = (places == index.astype(jnp.int16)[None, :]).astype(data.dtype)
-    return jnp.dot(data, onehot, preferred_element_type=jnp.float32).astype(data.dtype)
+def pick_columns(data, index, groups=8):
+    width, extent = data.shape
+    span = extent // groups
+    stacked = data.reshape(width, groups, span).transpose(1, 0, 2).reshape(groups * width, span)
+    low = (index % span).astype(jnp.int16)
+    high = index // span
+    places = jnp.arange(span, dtype=jnp.int16)[:, None]
+    onehot = (places == low[None, :]).astype(data.dtype)
+    rows = jnp.dot(stacked, onehot, preferred_element_type=jnp.float32).astype(data.dtype)
+    rows = rows.reshape(groups, width, index.shape[0])
+    keep = high[None, None, :] == jnp.arange(groups, dtype=jnp.int32)[:, None, None]
+    return jnp.sum(jnp.where(keep, rows, 0), axis=0, dtype=jnp.float32).astype(data.dtype)
 
 
-def add_columns(values, index, weight, extent):
+def add_columns(values, index, weight, extent, groups=8):
     width, count = values.shape
-    places = jnp.arange(extent, dtype=jnp.int16)[None, :]
-    marks = jnp.where(
-        index.astype(jnp.int16)[:, None] == places, weight.astype(values.dtype)[:, None], 0.0
-    ).astype(values.dtype)
+    span = extent // groups
     values = jnp.concatenate([values, jnp.ones((1, count), values.dtype)], axis=0)
-    total = jnp.dot(values, marks, preferred_element_type=jnp.float32)
+    values = values * weight.astype(values.dtype)[None, :]
+    low = (index % span).astype(jnp.int16)
+    high = index // span
+    keep = high[None, None, :] == jnp.arange(groups, dtype=jnp.int32)[:, None, None]
+    spread = jnp.where(keep, values[None], 0).astype(values.dtype).reshape(groups * (width + 1), count)
+    places = jnp.arange(span, dtype=jnp.int16)[None, :]
+    marks = (low[:, None] == places).astype(values.dtype)
+    total = jnp.dot(spread, marks, preferred_element_type=jnp.float32)
+    total = total.reshape(groups, width + 1, span).transpose(1, 0, 2).reshape(width + 1, extent)
     return (total[:width], total[width])
 
 

time: 190 us -> 137 us (0.72)
  matrix products: 95.2 us -> 31.5 us
  other arithmetic: 29.7 us -> 37.7 us
  local copies, waits for them, and re-layouts: 5.07 us -> 7.03 us
    dot_general x2, matrix products: 80.2 us -> 16.5 us  [the longest x1 9.84 us: add_columns(): total = jnp.dot(spread, marks, preferred_element_type=jnp.float32)]
    dot_general x0 -> x1, other arithmetic: none -> 5.57 us  [add_columns(): total = jnp.dot(spread, marks, preferred_element_type=jnp.float32)]
    reduce_sum x0 -> x1, other arithmetic: none -> 2.95 us  [pick_columns(): jnp.sum(jnp.where(keep, rows, 0), axis=0, dtype=jnp.float32)]
    unnamed x21 -> x22, local copies, waits for them, and re-layouts: 1.54 us -> 3.45 us
  transfers between devices with their start and end apart: 4 -> 4, of which waited for: 2 -> 2; matrix products, arithmetic and copies ran while one was open for 63% -> 48% of each run, Pallas kernels for 0% -> 0%
where the time goes in v5:
time: 137 us; the launch traced here: 136 us
  other arithmetic  37.7 us (28%)
  matrix products  31.5 us (23%)
  waiting for transfers between devices  17.3 us (13%)
  starting transfers between devices  15.9 us (12%)
  between operations  13.7 us (10%)
  blocking collectives  12.9 us (9%)
  local copies, waits for them, and re-layouts  7.03 us (5%)
    add x1, other arithmetic, body(): near_tally = near_tally + (near_places == picked).astype(jnp.bfloat16)  18 us
    all_gather x1, blocking collectives, body(): mean_wide = lax.all_gather(mean_two, 'feat', axis=0, tiled=True)  12.9 us
    all_gather x1, waiting for transfers between devices, body(): lax.all_gather(mean_one, 'feat', axis=0, tiled=True)  12.7 us
    add x1, other arithmetic, body(): hub_tally = hub_tally + (hub_places == picked).astype(jnp.bfloat16)  9.89 us
    dot_general x1, matrix products, add_columns(): total = jnp.dot(spread, marks, preferred_element_type=jnp.float32)  9.84 us
    all_to_all x1, starting transfers between devices, body(): lax.all_to_all(chosen, 'dom', split_axis=1, concat_axis=1, tiled=True)  8.45 us
    all_to_all x1, starting transfers between devices, body(): lax.all_to_all(spread, 'dom', split_axis=0, concat_axis=0, tiled=True)  7.27 us
    dot_general x5, matrix products, left_product(): lax.dot_general(weight, columns, (((0,), (0,)), ((), ())), preferred_elem...  7.03 us
  transfers between devices with their start and end apart: 4, of which 2 were waited for; matrix products, arithmetic and copies ran while one was open for 48% of the time, Pallas kernels for 0%

profile of v5, /device:TPU:0, one launch (start us, length us, event | category | flops | bytes accessed | tf_op | source)
XLA Modules:
  0.0 136.0 jit_solution(18419264548953627101)
XLA Ops:
  6.5 0.7 all-gather.3.cloned.1.call-update
  7.3 1.0 copy.40
  8.4 0.9 copy.39
  9.4 6.6 %fusion.5 = bf16[16384,256]{0,1:T(8,128)(2,1)S(1)} fusion(bf16[256,512]{1,0:T(8,128)(2,1)S(1)} %bitcast.76, s16[16384]{0:T(1024)(128)(2,1)S(1)} %get-tuple-element.20), kind=kOutput, calls=%fused_computation.6 | convolution fusion | flops 4307550208 | bytes 8683520 | tf_op jit(solution)/shard_map/dot_general | solution.py:23
  16.1 2.9 %select_reduce_fusion = bf16[32,16384]{1,0:T(8,128)(2,1)S(1)} fusion(bf16[8,32,16384]{2,1,0:T(8,128)(2,1)S(1)} %bitcast.68, pred[8,16384]{1,0:T(8,128)(4,1)S(1)} %iota_compare_fusion), kind=kLoop, calls=%fused_computation.31 | loop fusion | flops 7864320 | bytes 9568256 | tf_op jit(solution)/shard_map/reduce_sum | solution.py:26
  19.0 1.1 copy.43
  20.2 8.5 %all-to-all-start = ((bf16[32,32,512]{2,0,1:T(8,128)(2,1)}), bf16[32,32,512]{2,0,1:T(8,128)(2,1)S(1)}, u32[]{:S(2)}, u32[]{:S(2)}) async-start(bf16[32,32,512]{2,0,1:T(8,128)(2,1)} %bitcast.67), calls=%async_computation | async-start | bytes 2097152 | tf_op jit(solution)/shard_map/all_to_all | solution.py:67
  28.6 0.2 all-gather.5.cloned.1.call-start
  29.0 0.1 slice_reduce_fusion.9
  29.2 18.0 %fusion.20 = bf16[4096,1024]{1,0:T(8,128)(2,1)} fusion(s16[1024]{0:T(1024)(128)(2,1)S(1)} %get-tuple-element.10, s16[1024]{0:T(1024)(128)(2,1)S(1)} %get-tuple-element.11, s16[1024]{0:T(1024)(128)(2,1)S(1)} %get-tuple-element.12, s16[1024]{0:T(1024)(128)(2,1)S(1)} %get-tuple-element.13, s16[1024]{0:T(1024)(128)(2,1)S(1)} %get-tuple-element.14, ...), kind=kLoop, calls=%fused_computation.29 | loop fusion | flops 167772160 | bytes 8409088 | tf_op jit(solution)/shard_map/add | solution.py:94
  47.3 0.2 pad_multiply_fusion
  47.5 5.6 %fusion.91 = bf16[8,33,16384]{2,1,0:T(8,128)(2,1)} fusion(pred[8,16384]{1,0:T(8,128)(4,1)S(1)} %iota_compare_fusion.1, bf16[33,16384]{1,0:T(8,128)(2,1)S(1)} %pad_multiply_fusion), kind=kLoop, calls=%fused_computation.19.clone.clone.clone.2 | loop fusion | flops 4325376 | bytes 9863168 | tf_op jit(solution)/shard_map/dot_general | solution.py:40
  53.1 9.8 %fusion.39 = f32[33,8,512]{2,0,1:T(8,128)S(1)} fusion(s16[16384]{0:T(1024)(128)(2,1)S(1)} %get-tuple-element.22, bf16[8,33,16384]{2,1,0:T(8,128)(2,1)} %fusion.91), kind=kOutput, calls=%fused_computation.62 | convolution fusion | flops 4437573632 | bytes 9224192 | tf_op jit(solution)/shard_map/dot_general | solution.py:40
  63.1 0.8 divide_convert_fusion
  63.9 9.9 %fusion.35 = bf16[2048,1024]{1,0:T(8,128)(2,1)} fusion(s16[1024]{0:T(1024)(128)(2,1)S(1)} %get-tuple-element.10, s16[1024]{0:T(1024)(128)(2,1)S(1)} %get-tuple-element.11, s16[1024]{0:T(1024)(128)(2,1)S(1)} %get-tuple-element.12, s16[1024]{0:T(1024)(128)(2,1)S(1)} %get-tuple-element.13, s16[1024]{0:T(1024)(128)(2,1)S(1)} %get-tuple-element.14, ...), kind=kLoop, calls=%fused_computation.56 | loop fusion | flops 60817408 | bytes 4218880 | tf_op jit(solution)/shard_map/add | solution.py:95
  73.8 1.3 fusion.52
  75.1 1.7 %fusion.65 = f32[64,4096]{1,0:T(8,128)S(1)} fusion(bf16[128,4096]{1,0:T(8,128)(2,1)} %all-gather.3.cloned.1.call-done, bf16[128,256]{1,0:T(8,128)(2,1)S(1)} %copy-done.2, s32[]{:T(128)S(6)} %select_n.61), kind=kOutput, calls=%fused_computation.103 | convolution fusion | flops 67108864 | bytes 2129924 | tf_op jit(solution)/shard_map/dot_general | solution.py:10
  76.8 12.7 %all-gather.5.cloned.1.call-done = bf16[128,4096]{1,0:T(8,128)(2,1)} async-done(((bf16[32,4096]{1,0:T(8,128)(2,1)}), bf16[128,4096]{1,0:T(8,128)(2,1)}) %all-gather.5.cloned.1.call-update) | async-done | bytes 1048592 | tf_op jit(solution)/shard_map/all_gather | solution.py:76
  89.5 1.6 %fusion.26 = bf16[64,4096]{1,0:T(8,128)(2,1)S(1)} fusion(f32[64,4096]{1,0:T(8,128)S(1)} %fusion.65, bf16[128,4096]{1,0:T(8,128)(2,1)} %all-gather.5.cloned.1.call-done, bf16[128,256]{1,0:T(8,128)(2,1)S(1)} %copy-done.1, s32[]{:T(128)S(6)} %select_n.61), kind=kOutput, calls=%fused_computation.47 | convolution fusion | flops 67895296 | bytes 2654212 | tf_op jit(solution)/shard_map/dot_general | solution.py:10
  91.2 0.5 copy.32
  91.6 0.6 gather_fusion
  92.5 1.1 reshape.315
  93.6 7.3 %all-to-all-start.1 = ((bf16[32,2,2048]{2,1,0:T(2,128)(2,1)}), bf16[32,2,2048]{2,1,0:T(2,128)(2,1)S(1)}, u32[]{:S(2)}, u32[]{:S(2)}) async-start(bf16[32,2,2048]{2,1,0:T(2,128)(2,1)} %reshape.315), calls=%async_computation.1 | async-start | bytes 524288 | tf_op jit(solution)/shard_map/all_to_all | solution.py:85
  100.9 4.9 %fusion.74 = f32[64,1024]{1,0:T(8,128)S(1)} fusion(bf16[64,4096]{1,0:T(8,128)(2,1)S(1)} %fusion.26, bf16[4096,1024]{1,0:T(8,128)(2,1)} %fusion.20), kind=kOutput, calls=%fused_computation.126 | convolution fusion | flops 536870912 | bytes 9175040 | tf_op jit(solution)/shard_map/dot_general | solution.py:97
  105.9 3.8 %all-to-all-done.1 = bf16[32,2,2048]{2,1,0:T(2,128)(2,1)S(1)} async-done(((bf16[32,2,2048]{2,1,0:T(2,128)(2,1)}), bf16[32,2,2048]{2,1,0:T(2,128)(2,1)S(1)}, u32[]{:S(2)}, u32[]{:S(2)}) %all-to-all-start.1) | async-done | bytes 262176 | tf_op jit(solution)/shard_map/all_to_all | solution.py:85
  109.7 0.4 reshape.316
  110.0 0.3 copy.34
  110.4 0.5 reshape.295
  110.8 3.0 %fusion.47 = bf16[64,1024]{1,0:T(8,128)(2,1)S(1)} fusion(f32[64,1024]{1,0:T(8,128)S(1)} %fusion.74, bf16[64,2048]{1,0:T(8,128)(2,1)S(1)} %reshape.295, bf16[2048,1024]{1,0:T(8,128)(2,1)} %fusion.35), kind=kOutput, calls=%fused_computation.67 | convolution fusion | flops 268632064 | bytes 4849664 | tf_op jit(solution)/shard_map/dot_general | solution.py:98
  113.9 12.9 %all_gather.11 = bf16[256,1024]{1,0:T(8,128)(2,1)S(1)} all-gather(bf16[64,1024]{1,0:T(8,128)(2,1)S(1)} %fusion.47), channel_id=1, replica_groups=mesh['dom'=32,'feat'=4] {'feat'}, dimensions={0}, use_global_device_ids=true | all-gather | bytes 655360 | tf_op jit(solution)/shard_map/all_gather | solution.py:105
  126.8 0.3 fusion.56
  127.1 2.1 %fusion.48 = bf16[64,1024]{1,0:T(8,128)(2,1)} fusion(f32[64,1024]{1,0:T(8,128)S(1)} %fusion.56, f32[256,1024]{1,0:T(8,128)S(1)} %fusion.52, bf16[128,256]{1,0:T(8,128)(2,1)S(1)} %copy-done.1, bf16[128,4096]{1,0:T(8,128)(2,1)} %all-gather.5.cloned.1.call-done, bf16[256,256]{1,0:T(8,128)(2,1)S(1)} %copy-done.5, s32[]{:T(128)S(6)} %select_n.61), kind=kOutput, calls=%fused_computation.68 | convolution fusion | flops 101580800 | bytes 1835012 | tf_op jit(solution)/shard_map/dot_general | solution.py:10
  (37 shorter events, 0.9 us)
Async XLA Ops:
  6.5 120.2 %copy-start = (bf16[256,256]{1,0:T(8,128)(2,1)S(1)}, bf16[256,256]{1,0:T(8,128)(2,1)}, u32[]{:S(2)}) copy-start(bf16[256,256]{1,0:T(8,128)(2,1)} %param.19) | copy-start | bytes 393220
  6.5 67.3 %all-gather.3.cloned.1.call-start = ((), (), s32[]{:S(2)}) async-start(), calls=%async_computation.2 | async-start | bytes 1310720 | tf_op jit(solution)/shard_map/all_gather | solution.py:75
  16.0 12.8 %copy-start.4 = (s32[32,1,512]{2,1,0:T(1,128)S(1)}, s32[32,1,512]{2,1,0:T(1,128)}, u32[]{:S(2)}) copy-start(s32[32,1,512]{2,1,0:T(1,128)} %param.12) | copy-start | bytes 196612
  16.1 13.0 %copy-start.3 = (s32[1024,10]{0,1:T(8,128)S(1)}, s32[1024,10]{0,1:T(8,128)}, u32[]{:S(2)}) copy-start(s32[1024,10]{0,1:T(8,128)} %param.15) | copy-start | bytes 122884
  19.0 28.1 %copy-start.6 = (s32[32,1]{0,1:T(1,128)S(1)}, s32[32,1]{0,1:T(1,128)}, u32[]{:S(2)}) copy-start(s32[32,1]{0,1:T(1,128)} %param.13) | copy-start | bytes 388
  20.2 27.1 %all-to-all-start = ((bf16[32,32,512]{2,0,1:T(8,128)(2,1)}), bf16[32,32,512]{2,0,1:T(8,128)(2,1)S(1)}, u32[]{:S(2)}, u32[]{:S(2)}) async-start(bf16[32,32,512]{2,0,1:T(8,128)(2,1)} %bitcast.67), calls=%async_computation | async-start | bytes 2097152 | tf_op jit(solution)/shard_map/all_to_all | solution.py:67
  28.6 60.9 %all-gather.5.cloned.1.call-start = ((), (), s32[]{:S(2)}) async-start(), calls=%async_computation.3 | async-start | bytes 1310720 | tf_op jit(solution)/shard_map/all_gather | solution.py:76
  53.1 20.7 %copy-start.7 = (s32[1,64]{1,0:T(1,128)S(1)}, s32[1,64]{1,0:T(1,128)}, u32[]{:S(2)}) copy-start(s32[1,64]{1,0:T(1,128)} %param.14) | copy-start | bytes 772
  53.1 20.7 %copy-start.2 = (bf16[128,256]{1,0:T(8,128)(2,1)S(1)}, bf16[128,256]{1,0:T(8,128)(2,1)}, u32[]{:S(2)}) copy-start(bf16[128,256]{1,0:T(8,128)(2,1)} %param.16) | copy-start | bytes 196612
  63.0 26.6 %copy-start.1 = (bf16[128,256]{1,0:T(8,128)(2,1)S(1)}, bf16[128,256]{1,0:T(8,128)(2,1)}, u32[]{:S(2)}) copy-start(bf16[128,256]{1,0:T(8,128)(2,1)} %param.17) | copy-start | bytes 196612
  93.6 16.1 %all-to-all-start.1 = ((bf16[32,2,2048]{2,1,0:T(2,128)(2,1)}), bf16[32,2,2048]{2,1,0:T(2,128)(2,1)S(1)}, u32[]{:S(2)}, u32[]{:S(2)}) async-start(bf16[32,2,2048]{2,1,0:T(2,128)(2,1)} %reshape.315), calls=%async_computation.1 | async-start | bytes 524288 | tf_op jit(solution)/shard_map/all_to_all | solution.py:85
  105.8 21.2 %copy-start.5 = (bf16[256,256]{1,0:T(8,128)(2,1)S(1)}, bf16[256,256]{1,0:T(8,128)(2,1)}, u32[]{:S(2)}) copy-start(bf16[256,256]{1,0:T(8,128)(2,1)} %param.18) | copy-start | bytes 393220
Sparse Core Ops, SparseCore 0:
  9.0 26.5 all-gather.2
  64.0 25.4 all-gather.4

commit v6 on v5

--- a/solution.py
+++ b/solution.py
@@ -71,10 +71,23 @@
     mean_one = (neighbor_total / jnp.maximum(degree, 1.0)[None, :]).astype(jnp.bfloat16)
     hidden = self_one.shape[1]
     hcols = hidden // n_feat
-    own_all, mean_all = (
-        lax.all_gather(features, "feat", axis=0, tiled=True),
-        lax.all_gather(mean_one, "feat", axis=0, tiled=True),
-    )
+    order = (column_index - jnp.arange(n_feat)) % n_feat
+
+    def ring_gather(x):
+        parts = [x]
+        for shift in range(1, n_feat):
+            pairs = [(j, (j + shift) % n_feat) for j in range(n_feat)]
+            parts.append(lax.ppermute(x, "feat", perm=pairs))
+        return jnp.concatenate(parts, axis=0)
+
+    def ring_rows(weight):
+        blocks = weight.reshape(n_feat, narrow, weight.shape[1])
+        return jnp.take(blocks, order, axis=0).reshape(n_feat * narrow, weight.shape[1])
+
+    self_one = ring_rows(self_one)
+    neigh_one = ring_rows(neigh_one)
+    own_all = ring_gather(features)
+    mean_all = ring_gather(mean_one)
     w_own = lax.dynamic_slice_in_dim(self_one, column_index * hcols, hcols, 1)
     w_near = lax.dynamic_slice_in_dim(neigh_one, column_index * hcols, hcols, 1)
     pre_one = left_product(w_own, own_all) + left_product(w_near, mean_all)

time: 137 us -> 129 us (0.942)
  between operations: 13.7 us -> 0.55 us
  starting transfers between devices: 15.9 us -> 24.6 us
  matrix products: 31.5 us -> 28 us
  local copies, waits for them, and re-layouts: 7.03 us -> 8.5 us
  waiting for transfers between devices: 17.3 us -> 15.9 us
    ppermute x0 -> x6, waiting for transfers between devices: none -> 12.8 us  [ring_gather(): parts.append(lax.ppermute(x, 'feat', perm=pairs))]
    all_gather x2 -> x0, waiting for transfers between devices: 12.7 us -> none  [the longest x1 12.7 us: body(): lax.all_gather(mean_one, 'feat', axis=0, tiled=True)]
    ppermute x0 -> x6, starting transfers between devices: none -> 8.49 us  [ring_gather(): parts.append(lax.ppermute(x, 'feat', perm=pairs))]
    dot_general x5, matrix products: 7.03 us -> 3.44 us  [left_product(): lax.dot_general(weight, columns, (((0,), (0,)), ((), ())), preferred_elem...]
    unnamed x22 -> x49, local copies, waits for them, and re-layouts: 3.45 us -> 3.82 us
  transfers between devices with their start and end apart: 4 -> 8, of which waited for: 2 -> 4; matrix products, arithmetic and copies ran while one was open for 48% -> 50% of each run, Pallas kernels for 0% -> 0%
where the time goes in v6:
time: 129 us; the launch traced here: 128 us
  other arithmetic  37.7 us (29%)
  matrix products  28 us (22%)
  starting transfers between devices  24.6 us (19%)
  waiting for transfers between devices  15.9 us (12%)
  blocking collectives  13.1 us (10%)
  local copies, waits for them, and re-layouts  8.5 us (7%)
    add x1, other arithmetic, body(): near_tally = near_tally + (near_places == picked).astype(jnp.bfloat16)  17.9 us
    all_gather x1, blocking collectives, body(): mean_wide = lax.all_gather(mean_two, 'feat', axis=0, tiled=True)  13.1 us
    ppermute x6, waiting for transfers between devices, ring_gather(): parts.append(lax.ppermute(x, 'feat', perm=pairs))  12.8 us
    add x1, other arithmetic, body(): hub_tally = hub_tally + (hub_places == picked).astype(jnp.bfloat16)  9.88 us
    dot_general x1, matrix products, add_columns(): total = jnp.dot(spread, marks, preferred_element_type=jnp.float32)  9.81 us
    all_to_all x1, starting transfers between devices, body(): lax.all_to_all(chosen, 'dom', split_axis=1, concat_axis=1, tiled=True)  8.65 us
    ppermute x6, starting transfers between devices, ring_gather(): parts.append(lax.ppermute(x, 'feat', perm=pairs))  8.49 us
    all_to_all x1, starting transfers between devices, body(): lax.all_to_all(spread, 'dom', split_axis=0, concat_axis=0, tiled=True)  7.49 us
  transfers between devices with their start and end apart: 8, of which 4 were waited for; matrix products, arithmetic and copies ran while one was open for 50% of the time, Pallas kernels for 0%

profile of v6, /device:TPU:0, one launch (start us, length us, event | category | flops | bytes accessed | tf_op | source)
XLA Modules:
  0.0 128.4 jit_solution(1740597868076968539)
XLA Ops:
  0.0 1.6 %collective-permute-start = (bf16[32,4096]{1,0:T(8,128)(2,1)}, bf16[32,4096]{1,0:T(8,128)(2,1)S(1)}, u32[]{:S(2)}, u32[]{:S(2)}) collective-permute-start(bf16[32,4096]{1,0:T(8,128)(2,1)} %param.12), channel_id=1, source_target_pairs={{0,1},{1,2},{2,3},{3,0},{4,5},{5,6},{6,7},{7,4},{8,9},{9,10},{10,1... | collective-permute-start | bytes 786440 | tf_op jit(solution)/shard_map/ppermute | solution.py:80
  1.6 2.7 %collective-permute-start.1 = (bf16[32,4096]{1,0:T(8,128)(2,1)}, bf16[32,4096]{1,0:T(8,128)(2,1)S(1)}, u32[]{:S(2)}, u32[]{:S(2)}) collective-permute-start(bf16[32,4096]{1,0:T(8,128)(2,1)} %param.12), channel_id=1, source_target_pairs={{0,2},{1,3},{2,0},{3,1},{4,6},{5,7},{6,4},{7,5},{8,10},{9,11},{10,... | collective-permute-start | bytes 786440 | tf_op jit(solution)/shard_map/ppermute | solution.py:80
  4.3 1.4 %collective-permute-start.2 = (bf16[32,4096]{1,0:T(8,128)(2,1)}, bf16[32,4096]{1,0:T(8,128)(2,1)S(1)}, u32[]{:S(2)}, u32[]{:S(2)}) collective-permute-start(bf16[32,4096]{1,0:T(8,128)(2,1)} %param.12), channel_id=1, source_target_pairs={{0,3},{1,0},{2,1},{3,2},{4,7},{5,4},{6,5},{7,6},{8,11},{9,8},{10,9... | collective-permute-start | bytes 786440 | tf_op jit(solution)/shard_map/ppermute | solution.py:80
  5.8 1.1 copy.36
  6.9 0.9 copy.35
  7.9 6.6 %fusion.5 = bf16[16384,256]{0,1:T(8,128)(2,1)S(1)} fusion(bf16[256,512]{1,0:T(8,128)(2,1)S(1)} %bitcast.67, s16[16384]{0:T(1024)(128)(2,1)S(1)} %get-tuple-element.21), kind=kOutput, calls=%fused_computation.8 | convolution fusion | flops 4307550208 | bytes 8683520 | tf_op jit(solution)/shard_map/dot_general | solution.py:23
  14.7 2.9 %select_reduce_fusion = bf16[32,16384]{1,0:T(8,128)(2,1)S(1)} fusion(bf16[8,32,16384]{2,1,0:T(8,128)(2,1)S(1)} %bitcast.57, pred[8,16384]{1,0:T(8,128)(4,1)S(1)} %iota_compare_fusion), kind=kLoop, calls=%fused_computation.33 | loop fusion | flops 7864320 | bytes 9568256 | tf_op jit(solution)/shard_map/reduce_sum | solution.py:26
  17.6 1.1 copy.39
  18.7 8.6 %all-to-all-start = ((bf16[32,32,512]{2,0,1:T(8,128)(2,1)}), bf16[32,32,512]{2,0,1:T(8,128)(2,1)S(1)}, u32[]{:S(2)}, u32[]{:S(2)}) async-start(bf16[32,32,512]{2,0,1:T(8,128)(2,1)} %bitcast.56), calls=%async_computation | async-start | bytes 2097152 | tf_op jit(solution)/shard_map/all_to_all | solution.py:67
  27.5 0.7 add_select_fusion.3
  28.3 0.6 gather_fusion.1
  28.9 0.6 gather_fusion.2
  29.6 17.9 %fusion.20 = bf16[4096,1024]{1,0:T(8,128)(2,1)} fusion(s16[1024]{0:T(1024)(128)(2,1)S(1)} %get-tuple-element.11, s16[1024]{0:T(1024)(128)(2,1)S(1)} %get-tuple-element.12, s16[1024]{0:T(1024)(128)(2,1)S(1)} %get-tuple-element.13, s16[1024]{0:T(1024)(128)(2,1)S(1)} %get-tuple-element.14, s16[1024]{0:T(1024)(128)(2,1)S(1)} %get-tuple-element.15, ...), kind=kLoop, calls=%fused_computation.31 | loop fusion | flops 167772160 | bytes 8409088 | tf_op jit(solution)/shard_map/add | solution.py:107
  47.5 9.9 %fusion.35 = bf16[2048,1024]{1,0:T(8,128)(2,1)} fusion(s16[1024]{0:T(1024)(128)(2,1)S(1)} %get-tuple-element.11, s16[1024]{0:T(1024)(128)(2,1)S(1)} %get-tuple-element.12, s16[1024]{0:T(1024)(128)(2,1)S(1)} %get-tuple-element.13, s16[1024]{0:T(1024)(128)(2,1)S(1)} %get-tuple-element.14, s16[1024]{0:T(1024)(128)(2,1)S(1)} %get-tuple-element.15, ...), kind=kLoop, calls=%fused_computation.58 | loop fusion | flops 60817408 | bytes 4218880 | tf_op jit(solution)/shard_map/add | solution.py:108
  58.0 5.6 %fusion.105 = bf16[8,33,16384]{2,1,0:T(8,128)(2,1)} fusion(pred[8,16384]{1,0:T(8,128)(4,1)S(1)} %iota_compare_fusion.1, bf16[33,16384]{1,0:T(8,128)(2,1)S(1)} %pad_multiply_fusion), kind=kLoop, calls=%fused_computation.21.clone.clone.clone.2 | loop fusion | flops 4325376 | bytes 9863168 | tf_op jit(solution)/shard_map/dot_general | solution.py:40
  63.6 9.8 %fusion.38 = f32[33,8,512]{2,0,1:T(8,128)S(1)} fusion(s16[16384]{0:T(1024)(128)(2,1)S(1)} %copy-done.17, bf16[8,33,16384]{2,1,0:T(8,128)(2,1)} %fusion.105), kind=kOutput, calls=%fused_computation.63 | convolution fusion | flops 4437573632 | bytes 9224192 | tf_op jit(solution)/shard_map/dot_general | solution.py:40
  73.7 2.6 %collective-permute-start.4 = (bf16[32,4096]{1,0:T(8,128)(2,1)S(1)}, bf16[32,4096]{1,0:T(8,128)(2,1)S(1)}, u32[]{:S(2)}, u32[]{:S(2)}) collective-permute-start(bf16[32,4096]{1,0:T(8,128)(2,1)S(1)} %divide_convert_fusion), channel_id=1, source_target_pairs={{0,2},{1,3},{2,0},{3,1},{4,6},{5,7},{6,4},{7,5},{8,10},{9,11},{10,... | collective-permute-start | bytes 786440 | tf_op jit(solution)/shard_map/ppermute | solution.py:80
  76.3 6.5 %collective-permute-done.5 = bf16[32,4096]{1,0:T(8,128)(2,1)S(1)} collective-permute-done((bf16[32,4096]{1,0:T(8,128)(2,1)S(1)}, bf16[32,4096]{1,0:T(8,128)(2,1)S(1)}, u32[]{:S(2)}, u32[]{:S(2)}) %collective-permute-start.5) | collective-permute-done | bytes 262176 | tf_op jit(solution)/shard_map/ppermute | solution.py:80
  82.8 1.6 %collective-permute-done.4 = bf16[32,4096]{1,0:T(8,128)(2,1)S(1)} collective-permute-done((bf16[32,4096]{1,0:T(8,128)(2,1)S(1)}, bf16[32,4096]{1,0:T(8,128)(2,1)S(1)}, u32[]{:S(2)}, u32[]{:S(2)}) %collective-permute-start.4) | collective-permute-done | bytes 262176 | tf_op jit(solution)/shard_map/ppermute | solution.py:80
  84.4 4.7 %collective-permute-done.3 = bf16[32,4096]{1,0:T(8,128)(2,1)S(1)} collective-permute-done((bf16[32,4096]{1,0:T(8,128)(2,1)S(1)}, bf16[32,4096]{1,0:T(8,128)(2,1)S(1)}, u32[]{:S(2)}, u32[]{:S(2)}) %collective-permute-start.3) | collective-permute-done | bytes 262176 | tf_op jit(solution)/shard_map/ppermute | solution.py:80
  89.2 0.4 fusion.48
  89.9 0.4 fusion.26
  90.3 0.5 copy.29
  90.8 0.6 gather_fusion
  91.6 1.1 reshape.358
  92.7 7.5 %all-to-all-start.1 = ((bf16[32,2,2048]{2,1,0:T(2,128)(2,1)}), bf16[32,2,2048]{2,1,0:T(2,128)(2,1)S(1)}, u32[]{:S(2)}, u32[]{:S(2)}) async-start(bf16[32,2,2048]{2,1,0:T(2,128)(2,1)} %reshape.358), calls=%async_computation.1 | async-start | bytes 524288 | tf_op jit(solution)/shard_map/all_to_all | solution.py:98
  100.3 5.0 %fusion.89 = f32[64,1024]{1,0:T(8,128)S(1)} fusion(bf16[64,4096]{1,0:T(8,128)(2,1)S(1)} %fusion.26, bf16[4096,1024]{1,0:T(8,128)(2,1)} %fusion.20), kind=kOutput, calls=%fused_computation.155 | convolution fusion | flops 536870912 | bytes 9175040 | tf_op jit(solution)/shard_map/dot_general | solution.py:110
  105.7 3.1 %all-to-all-done.1 = bf16[32,2,2048]{2,1,0:T(2,128)(2,1)S(1)} async-done(((bf16[32,2,2048]{2,1,0:T(2,128)(2,1)}), bf16[32,2,2048]{2,1,0:T(2,128)(2,1)S(1)}, u32[]{:S(2)}, u32[]{:S(2)}) %all-to-all-start.1) | async-done | bytes 262176 | tf_op jit(solution)/shard_map/all_to_all | solution.py:98
  109.4 0.5 reshape.316
  109.9 3.0 %fusion.46 = bf16[64,1024]{1,0:T(8,128)(2,1)S(1)} fusion(f32[64,1024]{1,0:T(8,128)S(1)} %fusion.89, bf16[64,2048]{1,0:T(8,128)(2,1)S(1)} %reshape.316, bf16[2048,1024]{1,0:T(8,128)(2,1)} %fusion.35), kind=kOutput, calls=%fused_computation.68 | convolution fusion | flops 268632064 | bytes 4849664 | tf_op jit(solution)/shard_map/dot_general | solution.py:111
  112.9 13.1 %all_gather.3 = bf16[256,1024]{1,0:T(8,128)(2,1)S(1)} all-gather(bf16[64,1024]{1,0:T(8,128)(2,1)S(1)} %fusion.46), channel_id=1, replica_groups=mesh['dom'=32,'feat'=4] {'feat'}, dimensions={0}, use_global_device_ids=true | all-gather | bytes 655360 | tf_op jit(solution)/shard_map/all_gather | solution.py:118
  126.4 2.0 %fusion.47 = bf16[64,1024]{1,0:T(8,128)(2,1)} fusion(f32[64,1024]{1,0:T(8,128)S(1)} %fusion.69, f32[256,1024]{1,0:T(8,128)S(1)} %fusion.57, bf16[128,256]{1,0:T(8,128)(2,1)} %bitcast.66, bf16[128,4096]{1,0:T(8,128)(2,1)S(1)} %constant_dynamic-update-slice_fusion, bf16[256,256]{1,0:T(8,128)(2,1)} %param.20, s32[]{:T(128)S(6)} %select_n.74), kind=kOutput, calls=%fused_computation.69 | convolution fusion | flops 101580800 | bytes 1835012 | tf_op jit(solution)/shard_map/dot_general | solution.py:10
  (76 shorter events, 3.1 us)
Async XLA Ops:
  0.0 126.1 %copy-start = (bf16[256,256]{1,0:T(8,128)(2,1)S(1)}, bf16[256,256]{1,0:T(8,128)(2,1)}, u32[]{:S(2)}) copy-start(bf16[256,256]{1,0:T(8,128)(2,1)} %param.21) | copy-start | bytes 393220
  0.0 57.6 %collective-permute-start = (bf16[32,4096]{1,0:T(8,128)(2,1)}, bf16[32,4096]{1,0:T(8,128)(2,1)S(1)}, u32[]{:S(2)}, u32[]{:S(2)}) collective-permute-start(bf16[32,4096]{1,0:T(8,128)(2,1)} %param.12), channel_id=1, source_target_pairs={{0,1},{1,2},{2,3},{3,0},{4,5},{5,6},{6,7},{7,4},{8,9},{9,10},{10,1... | collective-permute-start | bytes 786440 | tf_op jit(solution)/shard_map/ppermute | solution.py:80
  1.6 56.1 %collective-permute-start.1 = (bf16[32,4096]{1,0:T(8,128)(2,1)}, bf16[32,4096]{1,0:T(8,128)(2,1)S(1)}, u32[]{:S(2)}, u32[]{:S(2)}) collective-permute-start(bf16[32,4096]{1,0:T(8,128)(2,1)} %param.12), channel_id=1, source_target_pairs={{0,2},{1,3},{2,0},{3,1},{4,6},{5,7},{6,4},{7,5},{8,10},{9,11},{10,... | collective-permute-start | bytes 786440 | tf_op jit(solution)/shard_map/ppermute | solution.py:80
  4.3 71.9 %collective-permute-start.2 = (bf16[32,4096]{1,0:T(8,128)(2,1)}, bf16[32,4096]{1,0:T(8,128)(2,1)S(1)}, u32[]{:S(2)}, u32[]{:S(2)}) collective-permute-start(bf16[32,4096]{1,0:T(8,128)(2,1)} %param.12), channel_id=1, source_target_pairs={{0,3},{1,0},{2,1},{3,2},{4,7},{5,4},{6,5},{7,6},{8,11},{9,8},{10,9... | collective-permute-start | bytes 786440 | tf_op jit(solution)/shard_map/ppermute | solution.py:80
  14.6 12.8 %copy-start.3 = (bf16[32,4096]{1,0:T(8,128)(2,1)S(1)}, bf16[32,4096]{1,0:T(8,128)(2,1)}, u32[]{:S(2)}) copy-start(bf16[32,4096]{1,0:T(8,128)(2,1)} %param.12) | copy-start | bytes 786436
  14.6 12.9 %copy-start.14 = (s32[32,1,512]{2,1,0:T(1,128)S(1)}, s32[32,1,512]{2,1,0:T(1,128)}, u32[]{:S(2)}) copy-start(s32[32,1,512]{2,1,0:T(1,128)} %param.14) | copy-start | bytes 196612
  14.6 13.6 %copy-start.19 = (s32[1,64]{1,0:T(1,128)S(1)}, s32[1,64]{1,0:T(1,128)}, u32[]{:S(2)}) copy-start(s32[1,64]{1,0:T(1,128)} %param.16) | copy-start | bytes 772
  14.6 13.6 %copy-start.15 = (bf16[128,256]{1,0:T(8,128)(2,1)S(1)}, bf16[128,256]{1,0:T(8,128)(2,1)}, u32[]{:S(2)}) copy-start(bf16[128,256]{1,0:T(8,128)(2,1)} %param.18) | copy-start | bytes 196612
  14.6 14.2 %copy-start.16 = (bf16[128,256]{1,0:T(8,128)(2,1)S(1)}, bf16[128,256]{1,0:T(8,128)(2,1)}, u32[]{:S(2)}) copy-start(bf16[128,256]{1,0:T(8,128)(2,1)} %param.19) | copy-start | bytes 196612
  14.7 14.8 %copy-start.13 = (s32[1024,10]{0,1:T(8,128)S(1)}, s32[1024,10]{0,1:T(8,128)}, u32[]{:S(2)}) copy-start(s32[1024,10]{0,1:T(8,128)} %param.17) | copy-start | bytes 122884
  18.7 38.8 %copy-start.18 = (s32[32,1]{0,1:T(1,128)S(1)}, s32[32,1]{0,1:T(1,128)}, u32[]{:S(2)}) copy-start(s32[32,1]{0,1:T(1,128)} %param.15) | copy-start | bytes 388
  18.7 39.0 %all-to-all-start = ((bf16[32,32,512]{2,0,1:T(8,128)(2,1)}), bf16[32,32,512]{2,0,1:T(8,128)(2,1)S(1)}, u32[]{:S(2)}, u32[]{:S(2)}) async-start(bf16[32,32,512]{2,0,1:T(8,128)(2,1)} %bitcast.56), calls=%async_computation | async-start | bytes 2097152 | tf_op jit(solution)/shard_map/all_to_all | solution.py:67
  57.5 31.7 %copy-start.11 = (bf16[4,32,256]{2,1,0:T(8,128)(2,1)}, bf16[4,32,256]{2,1,0:T(8,128)(2,1)S(1)}, u32[]{:S(2)}) copy-start(bf16[4,32,256]{2,1,0:T(8,128)(2,1)S(1)} %get-tuple-element.25) | copy-start | bytes 196612
  57.5 32.1 %copy-start.4 = (bf16[4,32,256]{2,1,0:T(8,128)(2,1)}, bf16[4,32,256]{2,1,0:T(8,128)(2,1)S(1)}, u32[]{:S(2)}) copy-start(bf16[4,32,256]{2,1,0:T(8,128)(2,1)S(1)} %get-tuple-element.24) | copy-start | bytes 196612
  57.7 5.9 %copy-start.17 = (s16[16384]{0:T(1024)(128)(2,1)S(1)}, s16[16384]{0:T(1024)(128)(2,1)}, u32[]{:S(2)}) copy-start(s16[16384]{0:T(1024)(128)(2,1)} %get-tuple-element.23) | copy-start | bytes 98308
  73.5 16.0 %copy-start.1 = (bf16[32,4096]{1,0:T(8,128)(2,1)}, bf16[32,4096]{1,0:T(8,128)(2,1)S(1)}, u32[]{:S(2)}) copy-start(bf16[32,4096]{1,0:T(8,128)(2,1)S(1)} %divide_convert_fusion) | copy-start | bytes 786436
  73.6 9.2 %collective-permute-start.5 = (bf16[32,4096]{1,0:T(8,128)(2,1)S(1)}, bf16[32,4096]{1,0:T(8,128)(2,1)S(1)}, u32[]{:S(2)}, u32[]{:S(2)}) collective-permute-start(bf16[32,4096]{1,0:T(8,128)(2,1)S(1)} %divide_convert_fusion), channel_id=1, source_target_pairs={{0,3},{1,0},{2,1},{3,2},{4,7},{5,4},{6,5},{7,6},{8,11},{9,8},{10,9... | collective-permute-start | bytes 786440 | tf_op jit(solution)/shard_map/ppermute | solution.py:80
  73.7 10.8 %collective-permute-start.4 = (bf16[32,4096]{1,0:T(8,128)(2,1)S(1)}, bf16[32,4096]{1,0:T(8,128)(2,1)S(1)}, u32[]{:S(2)}, u32[]{:S(2)}) collective-permute-start(bf16[32,4096]{1,0:T(8,128)(2,1)S(1)} %divide_convert_fusion), channel_id=1, source_target_pairs={{0,2},{1,3},{2,0},{3,1},{4,6},{5,7},{6,4},{7,5},{8,10},{9,11},{10,... | collective-permute-start | bytes 786440 | tf_op jit(solution)/shard_map/ppermute | solution.py:80
  76.3 12.9 %collective-permute-start.3 = (bf16[32,4096]{1,0:T(8,128)(2,1)S(1)}, bf16[32,4096]{1,0:T(8,128)(2,1)S(1)}, u32[]{:S(2)}, u32[]{:S(2)}) collective-permute-start(bf16[32,4096]{1,0:T(8,128)(2,1)S(1)} %divide_convert_fusion), channel_id=1, source_target_pairs={{0,1},{1,2},{2,3},{3,0},{4,5},{5,6},{6,7},{7,4},{8,9},{9,10},{10,1... | collective-permute-start | bytes 786440 | tf_op jit(solution)/shard_map/ppermute | solution.py:80
  82.8 6.8 %copy-start.5 = (bf16[32,4096]{1,0:T(8,128)(2,1)}, bf16[32,4096]{1,0:T(8,128)(2,1)S(1)}, u32[]{:S(2)}) copy-start(bf16[32,4096]{1,0:T(8,128)(2,1)S(1)} %collective-permute-done.5) | copy-start | bytes 786436
  84.4 5.2 %copy-start.7 = (bf16[32,4096]{1,0:T(8,128)(2,1)}, bf16[32,4096]{1,0:T(8,128)(2,1)S(1)}, u32[]{:S(2)}) copy-start(bf16[32,4096]{1,0:T(8,128)(2,1)S(1)} %collective-permute-done.4) | copy-start | bytes 786436
  89.2 0.7 copy-start.9
  92.7 16.0 %all-to-all-start.1 = ((bf16[32,2,2048]{2,1,0:T(2,128)(2,1)}), bf16[32,2,2048]{2,1,0:T(2,128)(2,1)S(1)}, u32[]{:S(2)}, u32[]{:S(2)}) async-start(bf16[32,2,2048]{2,1,0:T(2,128)(2,1)} %reshape.358), calls=%async_computation.1 | async-start | bytes 524288 | tf_op jit(solution)/shard_map/all_to_all | solution.py:98
  100.2 5.1 %copy-start.2 = (bf16[32,4096]{1,0:T(8,128)(2,1)S(1)}, bf16[32,4096]{1,0:T(8,128)(2,1)}, u32[]{:S(2)}) copy-start(bf16[32,4096]{1,0:T(8,128)(2,1)} %copy-done.1) | copy-start | bytes 786436
  100.2 5.1 %copy-start.6 = (bf16[32,4096]{1,0:T(8,128)(2,1)S(1)}, bf16[32,4096]{1,0:T(8,128)(2,1)}, u32[]{:S(2)}) copy-start(bf16[32,4096]{1,0:T(8,128)(2,1)} %copy-done.5) | copy-start | bytes 786436
  100.2 5.1 %copy-start.8 = (bf16[32,4096]{1,0:T(8,128)(2,1)S(1)}, bf16[32,4096]{1,0:T(8,128)(2,1)}, u32[]{:S(2)}) copy-start(bf16[32,4096]{1,0:T(8,128)(2,1)} %copy-done.7) | copy-start | bytes 786436
  100.2 5.1 %copy-start.10 = (bf16[32,4096]{1,0:T(8,128)(2,1)S(1)}, bf16[32,4096]{1,0:T(8,128)(2,1)}, u32[]{:S(2)}) copy-start(bf16[32,4096]{1,0:T(8,128)(2,1)} %copy-done.9) | copy-start | bytes 786436
  100.2 5.1 %copy-start.12 = (bf16[4,32,256]{2,1,0:T(8,128)(2,1)S(1)}, bf16[4,32,256]{2,1,0:T(8,128)(2,1)}, u32[]{:S(2)}) copy-start(bf16[4,32,256]{2,1,0:T(8,128)(2,1)} %copy-done.11) | copy-start | bytes 196612

commit v7 on v6

--- a/solution.py
+++ b/solution.py
@@ -69,6 +69,7 @@
         received.reshape(narrow, -1), targets.reshape(-1), live.reshape(-1), node_dev
     )
     mean_one = (neighbor_total / jnp.maximum(degree, 1.0)[None, :]).astype(jnp.bfloat16)
+    late_source, mean_one = lax.optimization_barrier((second_source, mean_one))
     hidden = self_one.shape[1]
     hcols = hidden // n_feat
     order = (column_index - jnp.arange(n_feat)) % n_feat
@@ -105,8 +106,10 @@
     for column in range(fanout):
         picked = second_source[:, column].astype(jnp.int16)[None, :]
         near_tally = near_tally + (near_places == picked).astype(jnp.bfloat16)
-        hub_tally = hub_tally + (hub_places == picked).astype(jnp.bfloat16)
-    near_tally, hub_tally = lax.optimization_barrier((near_tally, hub_tally))
+        late = late_source[:, column].astype(jnp.int16)[None, :]
+        hub_tally = hub_tally + (hub_places == late).astype(jnp.bfloat16)
+    near_tally = lax.optimization_barrier(near_tally)
+    hub_tally = lax.optimization_barrier(hub_tally)
     total = jnp.dot(hidden_one, near_tally, preferred_element_type=jnp.float32)
     total = total + jnp.dot(hub_table, hub_tally, preferred_element_type=jnp.float32)
     mean_two = (total / fanout).astype(jnp.bfloat16)
@@ -115,9 +118,10 @@
     own_wide = jnp.maximum(
         left_product(self_one, own_cols) + left_product(neigh_one, near_cols), 0.0
     ).astype(jnp.bfloat16)
-    mean_wide = lax.all_gather(mean_two, "feat", axis=0, tiled=True)
+    mean_wide = ring_gather(mean_two)
     v_own = lax.dynamic_slice_in_dim(self_two, column_index * hcols, hcols, 1)
     v_near = lax.dynamic_slice_in_dim(neigh_two, column_index * hcols, hcols, 1)
+    v_near = jnp.take(v_near.reshape(n_feat, hidden // n_feat, hcols), order, axis=0).reshape(hidden, hcols)
     result = left_product(v_own, own_wide) + left_product(v_near, mean_wide)
     return result.astype(jnp.bfloat16)
 

time: 129 us -> 123 us (0.953)
  blocking collectives: 13.1 us -> 0 us
  local copies, waits for them, and re-layouts: 8.5 us -> 12.4 us
  starting transfers between devices: 24.6 us -> 28.4 us
  waiting for transfers between devices: 15.9 us -> 13.3 us
  matrix products: 28 us -> 29.4 us
    all_gather x1 -> x0, blocking collectives: 13.1 us -> none  [body(): mean_wide = lax.all_gather(mean_two, 'feat', axis=0, tiled=True)]
    ppermute x6 -> x9, starting transfers between devices: 8.49 us -> 12.7 us  [ring_gather(): parts.append(lax.ppermute(x, 'feat', perm=pairs))]
    ppermute x6 -> x9, waiting for transfers between devices: 12.8 us -> 9.46 us  [ring_gather(): parts.append(lax.ppermute(x, 'feat', perm=pairs))]
    dot_general x5, matrix products: 3.44 us -> 5.01 us  [left_product(): lax.dot_general(weight, columns, (((0,), (0,)), ((), ())), preferred_elem...]
    gather x2, local copies, waits for them, and re-layouts: 0.73 us -> 2.05 us  [body(): hub_rows = hidden_one[:, hub_local[0]]]
    unnamed x49 -> x34, local copies, waits for them, and re-layouts: 3.82 us -> 4.58 us
  transfers between devices with their start and end apart: 8 -> 11, of which waited for: 4 -> 6; matrix products, arithmetic and copies ran while one was open for 50% -> 42% of each run, Pallas kernels for 0% -> 0%
where the time goes in v7:
time: 123 us; the launch traced here: 122 us
  other arithmetic  38.1 us (31%)
  matrix products  29.4 us (24%)
  starting transfers between devices  28.4 us (23%)
  waiting for transfers between devices  13.3 us (11%)
  local copies, waits for them, and re-layouts  12.4 us (10%)
    add x1, other arithmetic, body(): near_tally = near_tally + (near_places == picked).astype(jnp.bfloat16)  17.9 us
    ppermute x9, starting transfers between devices, ring_gather(): parts.append(lax.ppermute(x, 'feat', perm=pairs))  12.7 us
    add x1, other arithmetic, body(): hub_tally = hub_tally + (hub_places == late).astype(jnp.bfloat16)  10.1 us
    dot_general x1, matrix products, add_columns(): total = jnp.dot(spread, marks, preferred_element_type=jnp.float32)  9.81 us
    ppermute x9, waiting for transfers between devices, ring_gather(): parts.append(lax.ppermute(x, 'feat', perm=pairs))  9.46 us
    all_to_all x1, starting transfers between devices, body(): lax.all_to_all(chosen, 'dom', split_axis=1, concat_axis=1, tiled=True)  8.52 us
    all_to_all x1, starting transfers between devices, body(): lax.all_to_all(spread, 'dom', split_axis=0, concat_axis=0, tiled=True)  7.23 us
    dot_general x1, matrix products, pick_columns(): jnp.dot(stacked, onehot, preferred_element_type=jnp.float32)  6.64 us
  transfers between devices with their start and end apart: 11, of which 6 were waited for; matrix products, arithmetic and copies ran while one was open for 42% of the time, Pallas kernels for 0%

profile of v7, /device:TPU:0, one launch (start us, length us, event | category | flops | bytes accessed | tf_op | source)
XLA Modules:
  0.0 122.2 jit_solution(14761085072109548741)
XLA Ops:
  0.0 1.6 %collective-permute-start = (bf16[32,4096]{1,0:T(8,128)(2,1)}, bf16[32,4096]{1,0:T(8,128)(2,1)}, u32[]{:S(2)}, u32[]{:S(2)}) collective-permute-start(bf16[32,4096]{1,0:T(8,128)(2,1)} %param.12), channel_id=1, source_target_pairs={{0,1},{1,2},{2,3},{3,0},{4,5},{5,6},{6,7},{7,4},{8,9},{9,10},{10,1... | collective-permute-start | bytes 786440 | tf_op jit(solution)/shard_map/ppermute | solution.py:81
  1.6 2.7 %collective-permute-start.1 = (bf16[32,4096]{1,0:T(8,128)(2,1)}, bf16[32,4096]{1,0:T(8,128)(2,1)S(1)}, u32[]{:S(2)}, u32[]{:S(2)}) collective-permute-start(bf16[32,4096]{1,0:T(8,128)(2,1)} %param.12), channel_id=1, source_target_pairs={{0,2},{1,3},{2,0},{3,1},{4,6},{5,7},{6,4},{7,5},{8,10},{9,11},{10,... | collective-permute-start | bytes 786440 | tf_op jit(solution)/shard_map/ppermute | solution.py:81
  4.3 1.4 %collective-permute-start.2 = (bf16[32,4096]{1,0:T(8,128)(2,1)}, bf16[32,4096]{1,0:T(8,128)(2,1)S(1)}, u32[]{:S(2)}, u32[]{:S(2)}) collective-permute-start(bf16[32,4096]{1,0:T(8,128)(2,1)} %param.12), channel_id=1, source_target_pairs={{0,3},{1,0},{2,1},{3,2},{4,7},{5,4},{6,5},{7,6},{8,11},{9,8},{10,9... | collective-permute-start | bytes 786440 | tf_op jit(solution)/shard_map/ppermute | solution.py:81
  5.8 1.1 copy.36
  6.9 0.9 copy.35
  7.9 6.6 %fusion.5 = bf16[16384,256]{0,1:T(8,128)(2,1)S(1)} fusion(bf16[256,512]{1,0:T(8,128)(2,1)S(1)} %bitcast.75, s16[16384]{0:T(1024)(128)(2,1)S(1)} %get-tuple-element.31), kind=kOutput, calls=%fused_computation.9 | convolution fusion | flops 4307550208 | bytes 8683520 | tf_op jit(solution)/shard_map/dot_general | solution.py:23
  14.7 2.9 %select_reduce_fusion = bf16[32,16384]{1,0:T(8,128)(2,1)S(1)} fusion(bf16[8,32,16384]{2,1,0:T(8,128)(2,1)S(1)} %bitcast.63, pred[8,16384]{1,0:T(8,128)(4,1)S(1)} %iota_compare_fusion), kind=kLoop, calls=%fused_computation.34 | loop fusion | flops 7864320 | bytes 9568256 | tf_op jit(solution)/shard_map/reduce_sum | solution.py:26
  17.6 1.1 copy.39
  18.8 8.5 %all-to-all-start = ((bf16[32,32,512]{2,0,1:T(8,128)(2,1)}), bf16[32,32,512]{2,0,1:T(8,128)(2,1)S(1)}, u32[]{:S(2)}, u32[]{:S(2)}) async-start(bf16[32,32,512]{2,0,1:T(8,128)(2,1)} %bitcast.62), calls=%async_computation | async-start | bytes 2097152 | tf_op jit(solution)/shard_map/all_to_all | solution.py:67
  29.4 17.9 %fusion.20 = bf16[4096,1024]{1,0:T(8,128)(2,1)} fusion(s16[1024]{0:T(1024)(128)(2,1)S(1)} %get-tuple-element.21, s16[1024]{0:T(1024)(128)(2,1)S(1)} %get-tuple-element.22, s16[1024]{0:T(1024)(128)(2,1)S(1)} %get-tuple-element.23, s16[1024]{0:T(1024)(128)(2,1)S(1)} %get-tuple-element.24, s16[1024]{0:T(1024)(128)(2,1)S(1)} %get-tuple-element.25, ...), kind=kLoop, calls=%fused_computation.32 | loop fusion | flops 167772160 | bytes 8409088 | tf_op jit(solution)/shard_map/add | solution.py:108
  48.6 1.0 constant_dynamic-update-slice_fusion.2
  50.0 5.6 %fusion.99 = bf16[8,33,16384]{2,1,0:T(8,128)(2,1)} fusion(pred[8,16384]{1,0:T(8,128)(4,1)S(1)} %iota_compare_fusion.1, bf16[33,16384]{1,0:T(8,128)(2,1)S(1)} %pad_multiply_fusion), kind=kLoop, calls=%fused_computation.22.clone.clone.clone.2 | loop fusion | flops 4325376 | bytes 9863168 | tf_op jit(solution)/shard_map/dot_general | solution.py:40
  55.6 9.8 %fusion.38 = f32[33,8,512]{2,0,1:T(8,128)S(1)} fusion(s16[16384]{0:T(1024)(128)(2,1)S(1)} %get-tuple-element.33, bf16[8,33,16384]{2,1,0:T(8,128)(2,1)} %fusion.99), kind=kOutput, calls=%fused_computation.64 | convolution fusion | flops 4437573632 | bytes 9224192 | tf_op jit(solution)/shard_map/dot_general | solution.py:40
  66.2 0.9 collective-permute-start.4
  67.1 1.9 %collective-permute-start.5 = (bf16[32,4096]{1,0:T(8,128)(2,1)S(1)}, bf16[32,4096]{1,0:T(8,128)(2,1)S(1)}, u32[]{:S(2)}, u32[]{:S(2)}) collective-permute-start(bf16[32,4096]{1,0:T(8,128)(2,1)S(1)} %divide_convert_fusion), channel_id=1, source_target_pairs={{0,3},{1,0},{2,1},{3,2},{4,7},{5,4},{6,5},{7,6},{8,11},{9,8},{10,9... | collective-permute-start | bytes 786440 | tf_op jit(solution)/shard_map/ppermute | solution.py:81
  69.1 10.1 %fusion.35 = bf16[2048,1024]{1,0:T(8,128)(2,1)} fusion(s16[1024]{0:T(1024)(128)(2,1)S(1)} %get-tuple-element.11, s16[1024]{0:T(1024)(128)(2,1)S(1)} %get-tuple-element.12, s16[1024]{0:T(1024)(128)(2,1)S(1)} %get-tuple-element.13, s16[1024]{0:T(1024)(128)(2,1)S(1)} %get-tuple-element.14, s16[1024]{0:T(1024)(128)(2,1)S(1)} %get-tuple-element.15, ...), kind=kLoop, calls=%fused_computation.59 | loop fusion | flops 60817408 | bytes 4218880 | tf_op jit(solution)/shard_map/add | solution.py:110
  79.3 1.5 %collective-permute-done.3 = bf16[32,4096]{1,0:T(8,128)(2,1)S(1)} collective-permute-done((bf16[32,4096]{1,0:T(8,128)(2,1)S(1)}, bf16[32,4096]{1,0:T(8,128)(2,1)S(1)}, u32[]{:S(2)}, u32[]{:S(2)}) %collective-permute-start.3) | collective-permute-done | bytes 262176 | tf_op jit(solution)/shard_map/ppermute | solution.py:81
  82.3 1.3 %copy.29 = bf16[64,4096]{0,1:T(8,128)(2,1)} copy(bf16[64,4096]{1,0:T(8,128)(2,1)S(1)} %fusion.26) | data formatting | bytes 1048576 | tf_op jit(solution)/shard_map/convert_element_type | solution.py:95
  83.6 2.0 %gather_fusion.1 = bf16[64,64]{1,0:T(8,128)(2,1)S(1)} fusion(bf16[64,4096]{0,1:T(8,128)(2,1)} %copy.29, s32[1024]{0:T(1024)S(1)} %get-tuple-element.36), kind=kCustom, calls=%fused_computation.3 | custom fusion | bytes 16640 | tf_op jit(solution)/shard_map/gather | solution.py:96
  85.8 1.1 reshape.497
  86.9 7.2 %all-to-all-start.1 = ((bf16[32,2,2048]{2,1,0:T(2,128)(2,1)}), bf16[32,2,2048]{2,1,0:T(2,128)(2,1)S(1)}, u32[]{:S(2)}, u32[]{:S(2)}) async-start(bf16[32,2,2048]{2,1,0:T(2,128)(2,1)} %reshape.497), calls=%async_computation.1 | async-start | bytes 524288 | tf_op jit(solution)/shard_map/all_to_all | solution.py:99
  94.1 4.9 %fusion.82 = f32[64,1024]{1,0:T(8,128)S(1)} fusion(bf16[64,4096]{1,0:T(8,128)(2,1)S(1)} %fusion.26, bf16[4096,1024]{1,0:T(8,128)(2,1)} %fusion.20), kind=kOutput, calls=%fused_computation.170 | convolution fusion | flops 536870912 | bytes 9175040 | tf_op jit(solution)/shard_map/dot_general | solution.py:113
  99.1 3.8 %all-to-all-done.1 = bf16[32,2,2048]{2,1,0:T(2,128)(2,1)S(1)} async-done(((bf16[32,2,2048]{2,1,0:T(2,128)(2,1)}), bf16[32,2,2048]{2,1,0:T(2,128)(2,1)S(1)}, u32[]{:S(2)}, u32[]{:S(2)}) %all-to-all-start.1) | async-done | bytes 262176 | tf_op jit(solution)/shard_map/all_to_all | solution.py:99
  104.0 3.0 %fusion.46 = bf16[64,1024]{1,0:T(8,128)(2,1)S(1)} fusion(f32[64,1024]{1,0:T(8,128)S(1)} %fusion.82, bf16[64,2048]{1,0:T(8,128)(2,1)S(1)} %reshape.437, bf16[2048,1024]{1,0:T(8,128)(2,1)} %fusion.35), kind=kOutput, calls=%fused_computation.69 | convolution fusion | flops 268632064 | bytes 4849664 | tf_op jit(solution)/shard_map/dot_general | solution.py:114
  107.1 2.5 %collective-permute-start.8 = (bf16[64,1024]{1,0:T(8,128)(2,1)S(1)}, bf16[64,1024]{1,0:T(8,128)(2,1)S(1)}, u32[]{:S(2)}, u32[]{:S(2)}) collective-permute-start(bf16[64,1024]{1,0:T(8,128)(2,1)S(1)} %fusion.46), channel_id=1, source_target_pairs={{0,3},{1,0},{2,1},{3,2},{4,7},{5,4},{6,5},{7,6},{8,11},{9,8},{10,9... | collective-permute-start | bytes 393224 | tf_op jit(solution)/shard_map/ppermute | solution.py:81
  109.6 0.9 collective-permute-start.6
  110.6 1.1 fusion.57
  111.7 4.0 %collective-permute-done.8 = bf16[64,1024]{1,0:T(8,128)(2,1)S(1)} collective-permute-done((bf16[64,1024]{1,0:T(8,128)(2,1)S(1)}, bf16[64,1024]{1,0:T(8,128)(2,1)S(1)}, u32[]{:S(2)}, u32[]{:S(2)}) %collective-permute-start.8) | collective-permute-done | bytes 131104 | tf_op jit(solution)/shard_map/ppermute | solution.py:81
  115.7 1.8 %collective-permute-done.7 = bf16[64,1024]{1,0:T(8,128)(2,1)S(1)} collective-permute-done((bf16[64,1024]{1,0:T(8,128)(2,1)S(1)}, bf16[64,1024]{1,0:T(8,128)(2,1)S(1)}, u32[]{:S(2)}, u32[]{:S(2)}) %collective-permute-start.7) | collective-permute-done | bytes 131104 | tf_op jit(solution)/shard_map/ppermute | solution.py:81
  117.5 1.6 %collective-permute-done.6 = bf16[64,1024]{1,0:T(8,128)(2,1)S(1)} collective-permute-done((bf16[64,1024]{1,0:T(8,128)(2,1)S(1)}, bf16[64,1024]{1,0:T(8,128)(2,1)S(1)}, u32[]{:S(2)}, u32[]{:S(2)}) %collective-permute-start.6) | collective-permute-done | bytes 131104 | tf_op jit(solution)/shard_map/ppermute | solution.py:81
  119.1 1.1 fusion.48
  120.2 2.0 %fusion.47 = bf16[64,1024]{1,0:T(8,128)(2,1)} fusion(f32[64,1024]{1,0:T(8,128)S(1)} %fusion.48, f32[256,1024]{1,0:T(8,128)S(1)} %fusion.57, bf16[128,256]{1,0:T(8,128)(2,1)} %bitcast.72, bf16[128,4096]{1,0:T(8,128)(2,1)S(1)} %constant_dynamic-update-slice_fusion, bf16[256,256]{1,0:T(8,128)(2,1)S(1)} %copy-done, s32[]{:T(128)S(6)} %select_n.105), kind=kOutput, calls=%fused_computation.70 | convolution fusion | flops 101580800 | bytes 1835012 | tf_op jit(solution)/shard_map/dot_general | solution.py:10
  (76 shorter events, 7.6 us)
Async XLA Ops:
  0.0 120.2 %copy-start = (bf16[256,256]{1,0:T(8,128)(2,1)S(1)}, bf16[256,256]{1,0:T(8,128)(2,1)}, u32[]{:S(2)}) copy-start(bf16[256,256]{1,0:T(8,128)(2,1)} %param.20) | copy-start | bytes 393220
  0.0 48.6 %collective-permute-start = (bf16[32,4096]{1,0:T(8,128)(2,1)}, bf16[32,4096]{1,0:T(8,128)(2,1)}, u32[]{:S(2)}, u32[]{:S(2)}) collective-permute-start(bf16[32,4096]{1,0:T(8,128)(2,1)} %param.12), channel_id=1, source_target_pairs={{0,1},{1,2},{2,3},{3,0},{4,5},{5,6},{6,7},{7,4},{8,9},{9,10},{10,1... | collective-permute-start | bytes 786440 | tf_op jit(solution)/shard_map/ppermute | solution.py:81
  1.6 48.0 %collective-permute-start.1 = (bf16[32,4096]{1,0:T(8,128)(2,1)}, bf16[32,4096]{1,0:T(8,128)(2,1)S(1)}, u32[]{:S(2)}, u32[]{:S(2)}) collective-permute-start(bf16[32,4096]{1,0:T(8,128)(2,1)} %param.12), channel_id=1, source_target_pairs={{0,2},{1,3},{2,0},{3,1},{4,6},{5,7},{6,4},{7,5},{8,10},{9,11},{10,... | collective-permute-start | bytes 786440 | tf_op jit(solution)/shard_map/ppermute | solution.py:81
  4.3 45.3 %collective-permute-start.2 = (bf16[32,4096]{1,0:T(8,128)(2,1)}, bf16[32,4096]{1,0:T(8,128)(2,1)S(1)}, u32[]{:S(2)}, u32[]{:S(2)}) collective-permute-start(bf16[32,4096]{1,0:T(8,128)(2,1)} %param.12), channel_id=1, source_target_pairs={{0,3},{1,0},{2,1},{3,2},{4,7},{5,4},{6,5},{7,6},{8,11},{9,8},{10,9... | collective-permute-start | bytes 786440 | tf_op jit(solution)/shard_map/ppermute | solution.py:81
  14.6 12.8 %copy-start.1 = (bf16[32,4096]{1,0:T(8,128)(2,1)S(1)}, bf16[32,4096]{1,0:T(8,128)(2,1)}, u32[]{:S(2)}) copy-start(bf16[32,4096]{1,0:T(8,128)(2,1)} %param.12) | copy-start | bytes 786436
  14.6 12.8 %copy-start.10 = (s32[1,64]{1,0:T(1,128)S(1)}, s32[1,64]{1,0:T(1,128)}, u32[]{:S(2)}) copy-start(s32[1,64]{1,0:T(1,128)} %param.16) | copy-start | bytes 772
  14.6 13.0 %copy-start.5 = (s32[32,1,512]{2,1,0:T(1,128)S(1)}, s32[32,1,512]{2,1,0:T(1,128)}, u32[]{:S(2)}) copy-start(s32[32,1,512]{2,1,0:T(1,128)} %param.14) | copy-start | bytes 196612
  14.6 13.1 %copy-start.9 = (s32[32,1]{0,1:T(1,128)S(1)}, s32[32,1]{0,1:T(1,128)}, u32[]{:S(2)}) copy-start(s32[32,1]{0,1:T(1,128)} %param.15) | copy-start | bytes 388
  14.6 13.2 %copy-start.4 = (s32[1024,10]{0,1:T(8,128)S(1)}, s32[1024,10]{0,1:T(8,128)}, u32[]{:S(2)}) copy-start(s32[1024,10]{0,1:T(8,128)} %param.17) | copy-start | bytes 122884
  14.7 13.3 %copy-start.8 = (bf16[256,256]{1,0:T(8,128)(2,1)S(1)}, bf16[256,256]{1,0:T(8,128)(2,1)}, u32[]{:S(2)}) copy-start(bf16[256,256]{1,0:T(8,128)(2,1)} %param.21) | copy-start | bytes 393220
  17.6 29.7 %copy-start.6 = (bf16[128,256]{1,0:T(8,128)(2,1)S(1)}, bf16[128,256]{1,0:T(8,128)(2,1)}, u32[]{:S(2)}) copy-start(bf16[128,256]{1,0:T(8,128)(2,1)} %param.18) | copy-start | bytes 196612
  17.6 30.3 %copy-start.7 = (bf16[128,256]{1,0:T(8,128)(2,1)S(1)}, bf16[128,256]{1,0:T(8,128)(2,1)}, u32[]{:S(2)}) copy-start(bf16[128,256]{1,0:T(8,128)(2,1)} %param.19) | copy-start | bytes 196612
  18.8 30.9 %all-to-all-start = ((bf16[32,32,512]{2,0,1:T(8,128)(2,1)}), bf16[32,32,512]{2,0,1:T(8,128)(2,1)S(1)}, u32[]{:S(2)}, u32[]{:S(2)}) async-start(bf16[32,32,512]{2,0,1:T(8,128)(2,1)} %bitcast.62), calls=%async_computation | async-start | bytes 2097152 | tf_op jit(solution)/shard_map/all_to_all | solution.py:67
  48.6 32.8 %copy-start.3 = (bf16[4,32,256]{2,1,0:T(8,128)(2,1)}, bf16[4,32,256]{2,1,0:T(8,128)(2,1)S(1)}, u32[]{:S(2)}) copy-start(bf16[4,32,256]{2,1,0:T(8,128)(2,1)S(1)} %get-tuple-element.35) | copy-start | bytes 196612
  48.6 33.2 %copy-start.2 = (bf16[4,32,256]{2,1,0:T(8,128)(2,1)}, bf16[4,32,256]{2,1,0:T(8,128)(2,1)S(1)}, u32[]{:S(2)}) copy-start(bf16[4,32,256]{2,1,0:T(8,128)(2,1)S(1)} %get-tuple-element.34) | copy-start | bytes 196612
  65.6 15.2 %collective-permute-start.3 = (bf16[32,4096]{1,0:T(8,128)(2,1)S(1)}, bf16[32,4096]{1,0:T(8,128)(2,1)S(1)}, u32[]{:S(2)}, u32[]{:S(2)}) collective-permute-start(bf16[32,4096]{1,0:T(8,128)(2,1)S(1)} %divide_convert_fusion), channel_id=1, source_target_pairs={{0,1},{1,2},{2,3},{3,0},{4,5},{5,6},{6,7},{7,4},{8,9},{9,10},{10,1... | collective-permute-start | bytes 786440 | tf_op jit(solution)/shard_map/ppermute | solution.py:81
  66.2 14.6 %collective-permute-start.4 = (bf16[32,4096]{1,0:T(8,128)(2,1)S(1)}, bf16[32,4096]{1,0:T(8,128)(2,1)S(1)}, u32[]{:S(2)}, u32[]{:S(2)}) collective-permute-start(bf16[32,4096]{1,0:T(8,128)(2,1)S(1)} %divide_convert_fusion), channel_id=1, source_target_pairs={{0,2},{1,3},{2,0},{3,1},{4,6},{5,7},{6,4},{7,5},{8,10},{9,11},{10,... | collective-permute-start | bytes 786440 | tf_op jit(solution)/shard_map/ppermute | solution.py:81
  67.1 14.3 %collective-permute-start.5 = (bf16[32,4096]{1,0:T(8,128)(2,1)S(1)}, bf16[32,4096]{1,0:T(8,128)(2,1)S(1)}, u32[]{:S(2)}, u32[]{:S(2)}) collective-permute-start(bf16[32,4096]{1,0:T(8,128)(2,1)S(1)} %divide_convert_fusion), channel_id=1, source_target_pairs={{0,3},{1,0},{2,1},{3,2},{4,7},{5,4},{6,5},{7,6},{8,11},{9,8},{10,9... | collective-permute-start | bytes 786440 | tf_op jit(solution)/shard_map/ppermute | solution.py:81
  86.9 16.0 %all-to-all-start.1 = ((bf16[32,2,2048]{2,1,0:T(2,128)(2,1)}), bf16[32,2,2048]{2,1,0:T(2,128)(2,1)S(1)}, u32[]{:S(2)}, u32[]{:S(2)}) async-start(bf16[32,2,2048]{2,1,0:T(2,128)(2,1)} %reshape.497), calls=%async_computation.1 | async-start | bytes 524288 | tf_op jit(solution)/shard_map/all_to_all | solution.py:99
  107.1 8.6 %collective-permute-start.8 = (bf16[64,1024]{1,0:T(8,128)(2,1)S(1)}, bf16[64,1024]{1,0:T(8,128)(2,1)S(1)}, u32[]{:S(2)}, u32[]{:S(2)}) collective-permute-start(bf16[64,1024]{1,0:T(8,128)(2,1)S(1)} %fusion.46), channel_id=1, source_target_pairs={{0,3},{1,0},{2,1},{3,2},{4,7},{5,4},{6,5},{7,6},{8,11},{9,8},{10,9... | collective-permute-start | bytes 393224 | tf_op jit(solution)/shard_map/ppermute | solution.py:81
  109.6 7.9 %collective-permute-start.7 = (bf16[64,1024]{1,0:T(8,128)(2,1)S(1)}, bf16[64,1024]{1,0:T(8,128)(2,1)S(1)}, u32[]{:S(2)}, u32[]{:S(2)}) collective-permute-start(bf16[64,1024]{1,0:T(8,128)(2,1)S(1)} %fusion.46), channel_id=1, source_target_pairs={{0,2},{1,3},{2,0},{3,1},{4,6},{5,7},{6,4},{7,5},{8,10},{9,11},{10,... | collective-permute-start | bytes 393224 | tf_op jit(solution)/shard_map/ppermute | solution.py:81
  109.6 9.5 %collective-permute-start.6 = (bf16[64,1024]{1,0:T(8,128)(2,1)S(1)}, bf16[64,1024]{1,0:T(8,128)(2,1)S(1)}, u32[]{:S(2)}, u32[]{:S(2)}) collective-permute-start(bf16[64,1024]{1,0:T(8,128)(2,1)S(1)} %fusion.46), channel_id=1, source_target_pairs={{0,1},{1,2},{2,3},{3,0},{4,5},{5,6},{6,7},{7,4},{8,9},{9,10},{10,1... | collective-permute-start | bytes 393224 | tf_op jit(solution)/shard_map/ppermute | solution.py:81

commit v8 on v7

--- a/solution.py
+++ b/solution.py
@@ -93,7 +93,8 @@
     w_near = lax.dynamic_slice_in_dim(neigh_one, column_index * hcols, hcols, 1)
     pre_one = left_product(w_own, own_all) + left_product(w_near, mean_all)
     hidden_one = jnp.maximum(pre_one, 0.0).astype(jnp.bfloat16)
-    hub_rows = hidden_one[:, hub_local[0]]
+    hub_marks = (jnp.arange(node_dev, dtype=jnp.int32)[:, None] == hub_local[0][None, :]).astype(jnp.bfloat16)
+    hub_rows = jnp.dot(hidden_one, hub_marks, preferred_element_type=jnp.float32).astype(jnp.bfloat16)
     hub_count = hub_rows.shape[1]
     spread = jnp.broadcast_to(hub_rows[None], (n_dom,) + hub_rows.shape)
     landed = lax.all_to_all(spread, "dom", split_axis=0, concat_axis=0, tiled=True)

time: 123 us -> 121 us (0.984)
  local copies, waits for them, and re-layouts: 12.4 us -> 9.01 us
    gather x2 -> x0, local copies, waits for them, and re-layouts: 2.05 us -> none  [body(): hub_rows = hidden_one[:, hub_local[0]]]
    convert_element_type x1 -> x0, local copies, waits for them, and re-layouts: 1.32 us -> none  [body(): hidden_one = jnp.maximum(pre_one, 0.0).astype(jnp.bfloat16)]
  transfers between devices with their start and end apart: 11 -> 11, of which waited for: 6 -> 6; matrix products, arithmetic and copies ran while one was open for 42% -> 43% of each run, Pallas kernels for 0% -> 0%
where the time goes in v8:
time: 121 us; the launch traced here: 119 us
  other arithmetic  38.1 us (31%)
  matrix products  30 us (25%)
  starting transfers between devices  28.4 us (23%)
  waiting for transfers between devices  13.3 us (11%)
  local copies, waits for them, and re-layouts  9.01 us (7%)
    add x1, other arithmetic, body(): near_tally = near_tally + (near_places == picked).astype(jnp.bfloat16)  17.9 us
    ppermute x9, starting transfers between devices, ring_gather(): parts.append(lax.ppermute(x, 'feat', perm=pairs))  12.7 us
    add x1, other arithmetic, body(): hub_tally = hub_tally + (hub_places == late).astype(jnp.bfloat16)  10.1 us
    dot_general x1, matrix products, add_columns(): total = jnp.dot(spread, marks, preferred_element_type=jnp.float32)  9.81 us
    ppermute x9, waiting for transfers between devices, ring_gather(): parts.append(lax.ppermute(x, 'feat', perm=pairs))  9.47 us
    all_to_all x1, starting transfers between devices, body(): lax.all_to_all(chosen, 'dom', split_axis=1, concat_axis=1, tiled=True)  8.51 us
    all_to_all x1, starting transfers between devices, body(): lax.all_to_all(spread, 'dom', split_axis=0, concat_axis=0, tiled=True)  7.24 us
    dot_general x1, matrix products, pick_columns(): jnp.dot(stacked, onehot, preferred_element_type=jnp.float32)  6.64 us
  transfers between devices with their start and end apart: 11, of which 6 were waited for; matrix products, arithmetic and copies ran while one was open for 43% of the time, Pallas kernels for 0%

profile of v8, /device:TPU:0, one launch (start us, length us, event | category | flops | bytes accessed | tf_op | source)
XLA Modules:
  0.0 119.3 jit_solution(8610393653327970427)
XLA Ops:
  0.0 1.6 %collective-permute-start = (bf16[32,4096]{1,0:T(8,128)(2,1)}, bf16[32,4096]{1,0:T(8,128)(2,1)}, u32[]{:S(2)}, u32[]{:S(2)}) collective-permute-start(bf16[32,4096]{1,0:T(8,128)(2,1)} %param.12), channel_id=1, source_target_pairs={{0,1},{1,2},{2,3},{3,0},{4,5},{5,6},{6,7},{7,4},{8,9},{9,10},{10,1... | collective-permute-start | bytes 786440 | tf_op jit(solution)/shard_map/ppermute | solution.py:81
  1.6 2.7 %collective-permute-start.1 = (bf16[32,4096]{1,0:T(8,128)(2,1)}, bf16[32,4096]{1,0:T(8,128)(2,1)S(1)}, u32[]{:S(2)}, u32[]{:S(2)}) collective-permute-start(bf16[32,4096]{1,0:T(8,128)(2,1)} %param.12), channel_id=1, source_target_pairs={{0,2},{1,3},{2,0},{3,1},{4,6},{5,7},{6,4},{7,5},{8,10},{9,11},{10,... | collective-permute-start | bytes 786440 | tf_op jit(solution)/shard_map/ppermute | solution.py:81
  4.3 1.4 %collective-permute-start.2 = (bf16[32,4096]{1,0:T(8,128)(2,1)}, bf16[32,4096]{1,0:T(8,128)(2,1)S(1)}, u32[]{:S(2)}, u32[]{:S(2)}) collective-permute-start(bf16[32,4096]{1,0:T(8,128)(2,1)} %param.12), channel_id=1, source_target_pairs={{0,3},{1,0},{2,1},{3,2},{4,7},{5,4},{6,5},{7,6},{8,11},{9,8},{10,9... | collective-permute-start | bytes 786440 | tf_op jit(solution)/shard_map/ppermute | solution.py:81
  5.8 1.1 copy.26
  6.9 0.9 copy.25
  7.9 6.6 %fusion.5 = bf16[16384,256]{0,1:T(8,128)(2,1)S(1)} fusion(bf16[256,512]{1,0:T(8,128)(2,1)S(1)} %bitcast.72, s16[16384]{0:T(1024)(128)(2,1)S(1)} %get-tuple-element.31), kind=kOutput, calls=%fused_computation.8 | convolution fusion | flops 4307550208 | bytes 8683520 | tf_op jit(solution)/shard_map/dot_general | solution.py:23
  14.7 2.9 %select_reduce_fusion = bf16[32,16384]{1,0:T(8,128)(2,1)S(1)} fusion(bf16[8,32,16384]{2,1,0:T(8,128)(2,1)S(1)} %bitcast.60, pred[8,16384]{1,0:T(8,128)(4,1)S(1)} %iota_compare_fusion.4), kind=kLoop, calls=%fused_computation.33 | loop fusion | flops 7864320 | bytes 9568256 | tf_op jit(solution)/shard_map/reduce_sum | solution.py:26
  17.6 1.1 copy.29
  18.8 8.5 %all-to-all-start = ((bf16[32,32,512]{2,0,1:T(8,128)(2,1)}), bf16[32,32,512]{2,0,1:T(8,128)(2,1)S(1)}, u32[]{:S(2)}, u32[]{:S(2)}) async-start(bf16[32,32,512]{2,0,1:T(8,128)(2,1)} %bitcast.59), calls=%async_computation | async-start | bytes 2097152 | tf_op jit(solution)/shard_map/all_to_all | solution.py:67
  28.6 0.7 bitcast_select_fusion
  29.4 17.9 %fusion.20 = bf16[4096,1024]{1,0:T(8,128)(2,1)} fusion(s16[1024]{0:T(1024)(128)(2,1)S(1)} %get-tuple-element.21, s16[1024]{0:T(1024)(128)(2,1)S(1)} %get-tuple-element.22, s16[1024]{0:T(1024)(128)(2,1)S(1)} %get-tuple-element.23, s16[1024]{0:T(1024)(128)(2,1)S(1)} %get-tuple-element.24, s16[1024]{0:T(1024)(128)(2,1)S(1)} %get-tuple-element.25, ...), kind=kLoop, calls=%fused_computation.31 | loop fusion | flops 167772160 | bytes 8409088 | tf_op jit(solution)/shard_map/add | solution.py:109
  48.6 1.0 constant_dynamic-update-slice_fusion.2
  50.0 5.6 %fusion.102 = bf16[8,33,16384]{2,1,0:T(8,128)(2,1)} fusion(pred[8,16384]{1,0:T(8,128)(4,1)S(1)} %iota_compare_fusion.5, bf16[33,16384]{1,0:T(8,128)(2,1)S(1)} %pad_multiply_fusion), kind=kLoop, calls=%fused_computation.21.clone.clone.clone.2 | loop fusion | flops 4325376 | bytes 9863168 | tf_op jit(solution)/shard_map/dot_general | solution.py:40
  55.5 9.8 %fusion.39 = f32[33,8,512]{2,0,1:T(8,128)S(1)} fusion(s16[16384]{0:T(1024)(128)(2,1)S(1)} %get-tuple-element.33, bf16[8,33,16384]{2,1,0:T(8,128)(2,1)} %fusion.102), kind=kOutput, calls=%fused_computation.65 | convolution fusion | flops 4437573632 | bytes 9224192 | tf_op jit(solution)/shard_map/dot_general | solution.py:40
  65.5 0.7 collective-permute-start.3
  66.2 0.9 collective-permute-start.4
  67.1 1.9 %collective-permute-start.5 = (bf16[32,4096]{1,0:T(8,128)(2,1)S(1)}, bf16[32,4096]{1,0:T(8,128)(2,1)S(1)}, u32[]{:S(2)}, u32[]{:S(2)}) collective-permute-start(bf16[32,4096]{1,0:T(8,128)(2,1)S(1)} %divide_convert_fusion), channel_id=1, source_target_pairs={{0,3},{1,0},{2,1},{3,2},{4,7},{5,4},{6,5},{7,6},{8,11},{9,8},{10,9... | collective-permute-start | bytes 786440 | tf_op jit(solution)/shard_map/ppermute | solution.py:81
  69.1 10.1 %fusion.35 = bf16[2048,1024]{1,0:T(8,128)(2,1)} fusion(s16[1024]{0:T(1024)(128)(2,1)S(1)} %get-tuple-element.11, s16[1024]{0:T(1024)(128)(2,1)S(1)} %get-tuple-element.12, s16[1024]{0:T(1024)(128)(2,1)S(1)} %get-tuple-element.13, s16[1024]{0:T(1024)(128)(2,1)S(1)} %get-tuple-element.14, s16[1024]{0:T(1024)(128)(2,1)S(1)} %get-tuple-element.15, ...), kind=kLoop, calls=%fused_computation.58 | loop fusion | flops 60817408 | bytes 4218880 | tf_op jit(solution)/shard_map/add | solution.py:111
  79.2 1.5 %collective-permute-done.3 = bf16[32,4096]{1,0:T(8,128)(2,1)S(1)} collective-permute-done((bf16[32,4096]{1,0:T(8,128)(2,1)S(1)}, bf16[32,4096]{1,0:T(8,128)(2,1)S(1)}, u32[]{:S(2)}, u32[]{:S(2)}) %collective-permute-start.3) | collective-permute-done | bytes 262176 | tf_op jit(solution)/shard_map/ppermute | solution.py:81
  82.9 1.1 reshape.461
  84.0 7.2 %all-to-all-start.1 = ((bf16[32,2,2048]{2,1,0:T(2,128)(2,1)}), bf16[32,2,2048]{2,1,0:T(2,128)(2,1)S(1)}, u32[]{:S(2)}, u32[]{:S(2)}) async-start(bf16[32,2,2048]{2,1,0:T(2,128)(2,1)} %reshape.461), calls=%async_computation.1 | async-start | bytes 524288 | tf_op jit(solution)/shard_map/all_to_all | solution.py:100
  91.2 4.9 %fusion.84 = f32[64,1024]{1,0:T(8,128)S(1)} fusion(bf16[64,4096]{1,0:T(8,128)(2,1)S(1)} %fusion.26, bf16[4096,1024]{1,0:T(8,128)(2,1)} %fusion.20), kind=kOutput, calls=%fused_computation.170 | convolution fusion | flops 536870912 | bytes 9175040 | tf_op jit(solution)/shard_map/dot_general | solution.py:114
  96.2 3.8 %all-to-all-done.1 = bf16[32,2,2048]{2,1,0:T(2,128)(2,1)S(1)} async-done(((bf16[32,2,2048]{2,1,0:T(2,128)(2,1)}), bf16[32,2,2048]{2,1,0:T(2,128)(2,1)S(1)}, u32[]{:S(2)}, u32[]{:S(2)}) %all-to-all-start.1) | async-done | bytes 262176 | tf_op jit(solution)/shard_map/all_to_all | solution.py:100
  101.2 3.0 %fusion.47 = bf16[64,1024]{1,0:T(8,128)(2,1)S(1)} fusion(f32[64,1024]{1,0:T(8,128)S(1)} %fusion.84, bf16[64,2048]{1,0:T(8,128)(2,1)S(1)} %reshape.409, bf16[2048,1024]{1,0:T(8,128)(2,1)} %fusion.35), kind=kOutput, calls=%fused_computation.70 | convolution fusion | flops 268632064 | bytes 4849664 | tf_op jit(solution)/shard_map/dot_general | solution.py:115
  104.2 2.5 %collective-permute-start.8 = (bf16[64,1024]{1,0:T(8,128)(2,1)S(1)}, bf16[64,1024]{1,0:T(8,128)(2,1)S(1)}, u32[]{:S(2)}, u32[]{:S(2)}) collective-permute-start(bf16[64,1024]{1,0:T(8,128)(2,1)S(1)} %fusion.47), channel_id=1, source_target_pairs={{0,3},{1,0},{2,1},{3,2},{4,7},{5,4},{6,5},{7,6},{8,11},{9,8},{10,9... | collective-permute-start | bytes 393224 | tf_op jit(solution)/shard_map/ppermute | solution.py:81
  106.7 0.9 collective-permute-start.6
  107.7 1.1 fusion.60
  108.8 4.0 %collective-permute-done.8 = bf16[64,1024]{1,0:T(8,128)(2,1)S(1)} collective-permute-done((bf16[64,1024]{1,0:T(8,128)(2,1)S(1)}, bf16[64,1024]{1,0:T(8,128)(2,1)S(1)}, u32[]{:S(2)}, u32[]{:S(2)}) %collective-permute-start.8) | collective-permute-done | bytes 131104 | tf_op jit(solution)/shard_map/ppermute | solution.py:81
  112.9 1.8 %collective-permute-done.7 = bf16[64,1024]{1,0:T(8,128)(2,1)S(1)} collective-permute-done((bf16[64,1024]{1,0:T(8,128)(2,1)S(1)}, bf16[64,1024]{1,0:T(8,128)(2,1)S(1)}, u32[]{:S(2)}, u32[]{:S(2)}) %collective-permute-start.7) | collective-permute-done | bytes 131104 | tf_op jit(solution)/shard_map/ppermute | solution.py:81
  114.7 1.6 %collective-permute-done.6 = bf16[64,1024]{1,0:T(8,128)(2,1)S(1)} collective-permute-done((bf16[64,1024]{1,0:T(8,128)(2,1)S(1)}, bf16[64,1024]{1,0:T(8,128)(2,1)S(1)}, u32[]{:S(2)}, u32[]{:S(2)}) %collective-permute-start.6) | collective-permute-done | bytes 131104 | tf_op jit(solution)/shard_map/ppermute | solution.py:81
  116.3 1.1 fusion.51
  117.3 2.0 %fusion.48 = bf16[64,1024]{1,0:T(8,128)(2,1)} fusion(f32[64,1024]{1,0:T(8,128)S(1)} %fusion.51, f32[256,1024]{1,0:T(8,128)S(1)} %fusion.60, bf16[128,256]{1,0:T(8,128)(2,1)} %bitcast.69, bf16[128,4096]{1,0:T(8,128)(2,1)S(1)} %constant_dynamic-update-slice_fusion, bf16[256,256]{1,0:T(8,128)(2,1)S(1)} %copy-done, s32[]{:T(128)S(6)} %select_n.95), kind=kOutput, calls=%fused_computation.71 | convolution fusion | flops 101580800 | bytes 1835012 | tf_op jit(solution)/shard_map/dot_general | solution.py:10
  (72 shorter events, 6.6 us)
Async XLA Ops:
  0.0 117.3 %copy-start = (bf16[256,256]{1,0:T(8,128)(2,1)S(1)}, bf16[256,256]{1,0:T(8,128)(2,1)}, u32[]{:S(2)}) copy-start(bf16[256,256]{1,0:T(8,128)(2,1)} %param.20) | copy-start | bytes 393220
  0.0 48.6 %collective-permute-start = (bf16[32,4096]{1,0:T(8,128)(2,1)}, bf16[32,4096]{1,0:T(8,128)(2,1)}, u32[]{:S(2)}, u32[]{:S(2)}) collective-permute-start(bf16[32,4096]{1,0:T(8,128)(2,1)} %param.12), channel_id=1, source_target_pairs={{0,1},{1,2},{2,3},{3,0},{4,5},{5,6},{6,7},{7,4},{8,9},{9,10},{10,1... | collective-permute-start | bytes 786440 | tf_op jit(solution)/shard_map/ppermute | solution.py:81
  1.6 48.0 %collective-permute-start.1 = (bf16[32,4096]{1,0:T(8,128)(2,1)}, bf16[32,4096]{1,0:T(8,128)(2,1)S(1)}, u32[]{:S(2)}, u32[]{:S(2)}) collective-permute-start(bf16[32,4096]{1,0:T(8,128)(2,1)} %param.12), channel_id=1, source_target_pairs={{0,2},{1,3},{2,0},{3,1},{4,6},{5,7},{6,4},{7,5},{8,10},{9,11},{10,... | collective-permute-start | bytes 786440 | tf_op jit(solution)/shard_map/ppermute | solution.py:81
  4.3 45.3 %collective-permute-start.2 = (bf16[32,4096]{1,0:T(8,128)(2,1)}, bf16[32,4096]{1,0:T(8,128)(2,1)S(1)}, u32[]{:S(2)}, u32[]{:S(2)}) collective-permute-start(bf16[32,4096]{1,0:T(8,128)(2,1)} %param.12), channel_id=1, source_target_pairs={{0,3},{1,0},{2,1},{3,2},{4,7},{5,4},{6,5},{7,6},{8,11},{9,8},{10,9... | collective-permute-start | bytes 786440 | tf_op jit(solution)/shard_map/ppermute | solution.py:81
  14.6 12.7 %copy-start.1 = (bf16[32,4096]{1,0:T(8,128)(2,1)S(1)}, bf16[32,4096]{1,0:T(8,128)(2,1)}, u32[]{:S(2)}) copy-start(bf16[32,4096]{1,0:T(8,128)(2,1)} %param.12) | copy-start | bytes 786436
  14.6 12.9 %copy-start.5 = (s32[32,1,512]{2,1,0:T(1,128)S(1)}, s32[32,1,512]{2,1,0:T(1,128)}, u32[]{:S(2)}) copy-start(s32[32,1,512]{2,1,0:T(1,128)} %param.14) | copy-start | bytes 196612
  14.6 13.1 %copy-start.9 = (s32[32,1]{0,1:T(1,128)S(1)}, s32[32,1]{0,1:T(1,128)}, u32[]{:S(2)}) copy-start(s32[32,1]{0,1:T(1,128)} %param.15) | copy-start | bytes 388
  14.6 13.2 %copy-start.4 = (s32[1024,10]{0,1:T(8,128)S(1)}, s32[1024,10]{0,1:T(8,128)}, u32[]{:S(2)}) copy-start(s32[1024,10]{0,1:T(8,128)} %param.17) | copy-start | bytes 122884
  14.6 13.3 %copy-start.8 = (bf16[256,256]{1,0:T(8,128)(2,1)S(1)}, bf16[256,256]{1,0:T(8,128)(2,1)}, u32[]{:S(2)}) copy-start(bf16[256,256]{1,0:T(8,128)(2,1)} %param.21) | copy-start | bytes 393220
  17.6 29.7 %copy-start.6 = (bf16[128,256]{1,0:T(8,128)(2,1)S(1)}, bf16[128,256]{1,0:T(8,128)(2,1)}, u32[]{:S(2)}) copy-start(bf16[128,256]{1,0:T(8,128)(2,1)} %param.18) | copy-start | bytes 196612
  17.6 30.3 %copy-start.7 = (bf16[128,256]{1,0:T(8,128)(2,1)S(1)}, bf16[128,256]{1,0:T(8,128)(2,1)}, u32[]{:S(2)}) copy-start(bf16[128,256]{1,0:T(8,128)(2,1)} %param.19) | copy-start | bytes 196612
  18.8 30.9 %all-to-all-start = ((bf16[32,32,512]{2,0,1:T(8,128)(2,1)}), bf16[32,32,512]{2,0,1:T(8,128)(2,1)S(1)}, u32[]{:S(2)}, u32[]{:S(2)}) async-start(bf16[32,32,512]{2,0,1:T(8,128)(2,1)} %bitcast.59), calls=%async_computation | async-start | bytes 2097152 | tf_op jit(solution)/shard_map/all_to_all | solution.py:67
  48.5 32.8 %copy-start.3 = (bf16[4,32,256]{2,1,0:T(8,128)(2,1)}, bf16[4,32,256]{2,1,0:T(8,128)(2,1)S(1)}, u32[]{:S(2)}) copy-start(bf16[4,32,256]{2,1,0:T(8,128)(2,1)S(1)} %get-tuple-element.35) | copy-start | bytes 196612
  48.5 33.3 %copy-start.2 = (bf16[4,32,256]{2,1,0:T(8,128)(2,1)}, bf16[4,32,256]{2,1,0:T(8,128)(2,1)S(1)}, u32[]{:S(2)}) copy-start(bf16[4,32,256]{2,1,0:T(8,128)(2,1)S(1)} %get-tuple-element.34) | copy-start | bytes 196612
  65.3 16.9 %copy-start.10 = (s32[1,64]{1,0:T(1,128)S(1)}, s32[1,64]{1,0:T(1,128)}, u32[]{:S(2)}) copy-start(s32[1,64]{1,0:T(1,128)} %param.16) | copy-start | bytes 772
  65.5 15.2 %collective-permute-start.3 = (bf16[32,4096]{1,0:T(8,128)(2,1)S(1)}, bf16[32,4096]{1,0:T(8,128)(2,1)S(1)}, u32[]{:S(2)}, u32[]{:S(2)}) collective-permute-start(bf16[32,4096]{1,0:T(8,128)(2,1)S(1)} %divide_convert_fusion), channel_id=1, source_target_pairs={{0,1},{1,2},{2,3},{3,0},{4,5},{5,6},{6,7},{7,4},{8,9},{9,10},{10,1... | collective-permute-start | bytes 786440 | tf_op jit(solution)/shard_map/ppermute | solution.py:81
  66.2 14.6 %collective-permute-start.4 = (bf16[32,4096]{1,0:T(8,128)(2,1)S(1)}, bf16[32,4096]{1,0:T(8,128)(2,1)S(1)}, u32[]{:S(2)}, u32[]{:S(2)}) collective-permute-start(bf16[32,4096]{1,0:T(8,128)(2,1)S(1)} %divide_convert_fusion), channel_id=1, source_target_pairs={{0,2},{1,3},{2,0},{3,1},{4,6},{5,7},{6,4},{7,5},{8,10},{9,11},{10,... | collective-permute-start | bytes 786440 | tf_op jit(solution)/shard_map/ppermute | solution.py:81
  67.1 14.3 %collective-permute-start.5 = (bf16[32,4096]{1,0:T(8,128)(2,1)S(1)}, bf16[32,4096]{1,0:T(8,128)(2,1)S(1)}, u32[]{:S(2)}, u32[]{:S(2)}) collective-permute-start(bf16[32,4096]{1,0:T(8,128)(2,1)S(1)} %divide_convert_fusion), channel_id=1, source_target_pairs={{0,3},{1,0},{2,1},{3,2},{4,7},{5,4},{6,5},{7,6},{8,11},{9,8},{10,9... | collective-permute-start | bytes 786440 | tf_op jit(solution)/shard_map/ppermute | solution.py:81
  84.0 16.0 %all-to-all-start.1 = ((bf16[32,2,2048]{2,1,0:T(2,128)(2,1)}), bf16[32,2,2048]{2,1,0:T(2,128)(2,1)S(1)}, u32[]{:S(2)}, u32[]{:S(2)}) async-start(bf16[32,2,2048]{2,1,0:T(2,128)(2,1)} %reshape.461), calls=%async_computation.1 | async-start | bytes 524288 | tf_op jit(solution)/shard_map/all_to_all | solution.py:100
  104.2 8.6 %collective-permute-start.8 = (bf16[64,1024]{1,0:T(8,128)(2,1)S(1)}, bf16[64,1024]{1,0:T(8,128)(2,1)S(1)}, u32[]{:S(2)}, u32[]{:S(2)}) collective-permute-start(bf16[64,1024]{1,0:T(8,128)(2,1)S(1)} %fusion.47), channel_id=1, source_target_pairs={{0,3},{1,0},{2,1},{3,2},{4,7},{5,4},{6,5},{7,6},{8,11},{9,8},{10,9... | collective-permute-start | bytes 393224 | tf_op jit(solution)/shard_map/ppermute | solution.py:81
  106.7 7.9 %collective-permute-start.7 = (bf16[64,1024]{1,0:T(8,128)(2,1)S(1)}, bf16[64,1024]{1,0:T(8,128)(2,1)S(1)}, u32[]{:S(2)}, u32[]{:S(2)}) collective-permute-start(bf16[64,1024]{1,0:T(8,128)(2,1)S(1)} %fusion.47), channel_id=1, source_target_pairs={{0,2},{1,3},{2,0},{3,1},{4,6},{5,7},{6,4},{7,5},{8,10},{9,11},{10,... | collective-permute-start | bytes 393224 | tf_op jit(solution)/shard_map/ppermute | solution.py:81
  106.7 9.5 %collective-permute-start.6 = (bf16[64,1024]{1,0:T(8,128)(2,1)S(1)}, bf16[64,1024]{1,0:T(8,128)(2,1)S(1)}, u32[]{:S(2)}, u32[]{:S(2)}) collective-permute-start(bf16[64,1024]{1,0:T(8,128)(2,1)S(1)} %fusion.47), channel_id=1, source_target_pairs={{0,1},{1,2},{2,3},{3,0},{4,5},{5,6},{6,7},{7,4},{8,9},{9,10},{10,1... | collective-permute-start | bytes 393224 | tf_op jit(solution)/shard_map/ppermute | solution.py:81

commit v9 on v8

--- a/solution.py
+++ b/solution.py
@@ -94,7 +94,11 @@
     pre_one = left_product(w_own, own_all) + left_product(w_near, mean_all)
     hidden_one = jnp.maximum(pre_one, 0.0).astype(jnp.bfloat16)
     hub_marks = (jnp.arange(node_dev, dtype=jnp.int32)[:, None] == hub_local[0][None, :]).astype(jnp.bfloat16)
-    hub_rows = jnp.dot(hidden_one, hub_marks, preferred_element_type=jnp.float32).astype(jnp.bfloat16)
+    hub_own = jnp.dot(own_all, hub_marks, preferred_element_type=jnp.float32).astype(jnp.bfloat16)
+    hub_near = jnp.dot(mean_all, hub_marks, preferred_element_type=jnp.float32).astype(jnp.bfloat16)
+    hub_rows = jnp.maximum(
+        left_product(w_own, hub_own) + left_product(w_near, hub_near), 0.0
+    ).astype(jnp.bfloat16)
     hub_count = hub_rows.shape[1]
     spread = jnp.broadcast_to(hub_rows[None], (n_dom,) + hub_rows.shape)
     landed = lax.all_to_all(spread, "dom", split_axis=0, concat_axis=0, tiled=True)

time: 121 us -> 132 us (1.091)
  local copies, waits for them, and re-layouts: 9.01 us -> 14.9 us
  matrix products: 30 us -> 32.7 us
  waiting for transfers between devices: 13.3 us -> 15.3 us
    all_to_all x1, waiting for transfers between devices: 3.83 us -> 7.61 us  [body(): lax.all_to_all(spread, 'dom', split_axis=0, concat_axis=0, tiled=True)]
    dot_general x5 -> x6, matrix products: 5.01 us -> 7.21 us  [left_product(): lax.dot_general(weight, columns, (((0,), (0,)), ((), ())), preferred_elem...]
    transpose x1, local copies, waits for them, and re-layouts: 0.34 us -> 2.18 us  [body(): landed.transpose(1, 0, 2).reshape(hidden_one.shape[0], n_dom * hub_count)]
    ppermute x9, waiting for transfers between devices: 9.47 us -> 7.71 us  [ring_gather(): parts.append(lax.ppermute(x, 'feat', perm=pairs))]
    reshape x1, local copies, waits for them, and re-layouts: 0.45 us -> 2.2 us  [body(): landed.transpose(1, 0, 2).reshape(hidden_one.shape[0], n_dom * hub_count)]
    gather x2, local copies, waits for them, and re-layouts: 1.1 us -> 2.78 us  [ring_rows(): jnp.take(blocks, order, axis=0).reshape(n_feat * narrow, weight.shape[1])]
    unnamed x34 -> x28, local copies, waits for them, and re-layouts: 4.58 us -> 4.38 us
  transfers between devices with their start and end apart: 11 -> 11, of which waited for: 6 -> 5; matrix products, arithmetic and copies ran while one was open for 43% -> 38% of each run, Pallas kernels for 0% -> 0%
where the time goes in v9:
time: 132 us; the launch traced here: 130 us
  other arithmetic  38.1 us (29%)
  matrix products  32.7 us (25%)
  starting transfers between devices  28.8 us (22%)
  waiting for transfers between devices  15.3 us (12%)
  local copies, waits for them, and re-layouts  14.9 us (11%)
    add x1, other arithmetic, body(): near_tally = near_tally + (near_places == picked).astype(jnp.bfloat16)  17.9 us
    ppermute x9, starting transfers between devices, ring_gather(): parts.append(lax.ppermute(x, 'feat', perm=pairs))  13.1 us
    add x1, other arithmetic, body(): hub_tally = hub_tally + (hub_places == late).astype(jnp.bfloat16)  10.1 us
    dot_general x1, matrix products, add_columns(): total = jnp.dot(spread, marks, preferred_element_type=jnp.float32)  9.81 us
    all_to_all x1, starting transfers between devices, body(): lax.all_to_all(chosen, 'dom', split_axis=1, concat_axis=1, tiled=True)  8.52 us
    ppermute x9, waiting for transfers between devices, ring_gather(): parts.append(lax.ppermute(x, 'feat', perm=pairs))  7.71 us
    all_to_all x1, waiting for transfers between devices, body(): lax.all_to_all(spread, 'dom', split_axis=0, concat_axis=0, tiled=True)  7.61 us
    all_to_all x1, starting transfers between devices, body(): lax.all_to_all(spread, 'dom', split_axis=0, concat_axis=0, tiled=True)  7.23 us
  transfers between devices with their start and end apart: 11, of which 5 were waited for; matrix products, arithmetic and copies ran while one was open for 38% of the time, Pallas kernels for 0%

profile of v9, /device:TPU:0, one launch (start us, length us, event | category | flops | bytes accessed | tf_op | source)
XLA Modules:
  0.0 130.3 jit_solution(3692996240772353977)
XLA Ops:
  0.0 1.6 %collective-permute-start = (bf16[32,4096]{1,0:T(8,128)(2,1)}, bf16[32,4096]{1,0:T(8,128)(2,1)S(1)}, u32[]{:S(2)}, u32[]{:S(2)}) collective-permute-start(bf16[32,4096]{1,0:T(8,128)(2,1)} %param.12), channel_id=1, source_target_pairs={{0,1},{1,2},{2,3},{3,0},{4,5},{5,6},{6,7},{7,4},{8,9},{9,10},{10,1... | collective-permute-start | bytes 786440 | tf_op jit(solution)/shard_map/ppermute | solution.py:81
  1.6 2.7 %collective-permute-start.1 = (bf16[32,4096]{1,0:T(8,128)(2,1)}, bf16[32,4096]{1,0:T(8,128)(2,1)S(1)}, u32[]{:S(2)}, u32[]{:S(2)}) collective-permute-start(bf16[32,4096]{1,0:T(8,128)(2,1)} %param.12), channel_id=1, source_target_pairs={{0,2},{1,3},{2,0},{3,1},{4,6},{5,7},{6,4},{7,5},{8,10},{9,11},{10,... | collective-permute-start | bytes 786440 | tf_op jit(solution)/shard_map/ppermute | solution.py:81
  4.3 1.4 %collective-permute-start.2 = (bf16[32,4096]{1,0:T(8,128)(2,1)}, bf16[32,4096]{1,0:T(8,128)(2,1)S(1)}, u32[]{:S(2)}, u32[]{:S(2)}) collective-permute-start(bf16[32,4096]{1,0:T(8,128)(2,1)} %param.12), channel_id=1, source_target_pairs={{0,3},{1,0},{2,1},{3,2},{4,7},{5,4},{6,5},{7,6},{8,11},{9,8},{10,9... | collective-permute-start | bytes 786440 | tf_op jit(solution)/shard_map/ppermute | solution.py:81
  6.7 1.0 copy.26
  7.9 6.6 %fusion.5 = bf16[16384,256]{0,1:T(8,128)(2,1)S(1)} fusion(bf16[256,512]{1,0:T(8,128)(2,1)S(1)} %bitcast.74, s16[16384]{0:T(1024)(128)(2,1)S(1)} %get-tuple-element.31), kind=kOutput, calls=%fused_computation.8 | convolution fusion | flops 4307550208 | bytes 8683520 | tf_op jit(solution)/shard_map/dot_general | solution.py:23
  14.6 2.9 %select_reduce_fusion = bf16[32,16384]{1,0:T(8,128)(2,1)S(1)} fusion(bf16[8,32,16384]{2,1,0:T(8,128)(2,1)S(1)} %bitcast.60, pred[8,16384]{1,0:T(8,128)(4,1)S(1)} %iota_compare_fusion.11), kind=kLoop, calls=%fused_computation.33 | loop fusion | flops 7864320 | bytes 9568256 | tf_op jit(solution)/shard_map/reduce_sum | solution.py:26
  17.6 1.1 copy.29
  18.7 8.5 %all-to-all-start = ((bf16[32,32,512]{2,0,1:T(8,128)(2,1)}), bf16[32,32,512]{2,0,1:T(8,128)(2,1)S(1)}, u32[]{:S(2)}, u32[]{:S(2)}) async-start(bf16[32,32,512]{2,0,1:T(8,128)(2,1)} %bitcast.59), calls=%async_computation | async-start | bytes 2097152 | tf_op jit(solution)/shard_map/all_to_all | solution.py:67
  27.9 0.9 constant_dynamic-slice_fusion
  30.1 17.9 %fusion.20 = bf16[4096,1024]{1,0:T(8,128)(2,1)} fusion(s16[1024]{0:T(1024)(128)(2,1)S(1)} %get-tuple-element.11, s16[1024]{0:T(1024)(128)(2,1)S(1)} %get-tuple-element.12, s16[1024]{0:T(1024)(128)(2,1)S(1)} %get-tuple-element.13, s16[1024]{0:T(1024)(128)(2,1)S(1)} %get-tuple-element.14, s16[1024]{0:T(1024)(128)(2,1)S(1)} %get-tuple-element.15, ...), kind=kLoop, calls=%fused_computation.31 | loop fusion | flops 167772160 | bytes 8409088 | tf_op jit(solution)/shard_map/add | solution.py:113
  48.1 1.4 %gather_fusion.1 = bf16[4,32,256]{2,1,0:T(8,128)(2,1)S(1)} fusion(bf16[4,32,256]{2,1,0:T(8,128)(2,1)} %bitcast.81, s32[1024]{0:T(1024)S(1)} %pad_clamp_fusion.1), kind=kCustom, calls=%fused_computation.clone | custom fusion | bytes 131088 | tf_op jit(solution)/shard_map/jit(_take)/gather | solution.py:86
  49.5 1.4 %gather_fusion.2 = bf16[4,32,256]{2,1,0:T(8,128)(2,1)S(1)} fusion(bf16[4,32,256]{2,1,0:T(8,128)(2,1)} %bitcast.82, s32[1024]{0:T(1024)S(1)} %pad_clamp_fusion.1), kind=kCustom, calls=%fused_computation.1.clone | custom fusion | bytes 131088 | tf_op jit(solution)/shard_map/jit(_take)/gather | solution.py:86
  52.3 5.6 %fusion.120 = bf16[8,33,16384]{2,1,0:T(8,128)(2,1)} fusion(pred[8,16384]{1,0:T(8,128)(4,1)S(1)} %iota_compare_fusion.12, bf16[33,16384]{1,0:T(8,128)(2,1)S(1)} %pad_multiply_fusion), kind=kLoop, calls=%fused_computation.21.clone.clone.clone.2 | loop fusion | flops 4325376 | bytes 9863168 | tf_op jit(solution)/shard_map/dot_general | solution.py:40
  57.9 9.8 %fusion.40 = f32[33,8,512]{2,0,1:T(8,128)S(1)} fusion(s16[16384]{0:T(1024)(128)(2,1)S(1)} %get-tuple-element.33, bf16[8,33,16384]{2,1,0:T(8,128)(2,1)} %fusion.120), kind=kOutput, calls=%fused_computation.66 | convolution fusion | flops 4437573632 | bytes 9224192 | tf_op jit(solution)/shard_map/dot_general | solution.py:40
  69.4 1.9 %collective-permute-start.5 = (bf16[32,4096]{1,0:T(8,128)(2,1)S(1)}, bf16[32,4096]{1,0:T(8,128)(2,1)S(1)}, u32[]{:S(2)}, u32[]{:S(2)}) collective-permute-start(bf16[32,4096]{1,0:T(8,128)(2,1)S(1)} %divide_convert_fusion), channel_id=1, source_target_pairs={{0,3},{1,0},{2,1},{3,2},{4,7},{5,4},{6,5},{7,6},{8,11},{9,8},{10,9... | collective-permute-start | bytes 786440 | tf_op jit(solution)/shard_map/ppermute | solution.py:81
  71.4 10.1 %fusion.35 = bf16[2048,1024]{1,0:T(8,128)(2,1)} fusion(s16[1024]{0:T(1024)(128)(2,1)S(1)} %get-tuple-element.21, s16[1024]{0:T(1024)(128)(2,1)S(1)} %get-tuple-element.22, s16[1024]{0:T(1024)(128)(2,1)S(1)} %get-tuple-element.23, s16[1024]{0:T(1024)(128)(2,1)S(1)} %get-tuple-element.24, s16[1024]{0:T(1024)(128)(2,1)S(1)} %get-tuple-element.25, ...), kind=kLoop, calls=%fused_computation.58 | loop fusion | flops 60817408 | bytes 4218880 | tf_op jit(solution)/shard_map/add | solution.py:115
  81.5 1.5 %collective-permute-done.3 = bf16[32,4096]{1,0:T(8,128)(2,1)S(1)} collective-permute-done((bf16[32,4096]{1,0:T(8,128)(2,1)S(1)}, bf16[32,4096]{1,0:T(8,128)(2,1)S(1)}, u32[]{:S(2)}, u32[]{:S(2)}) %collective-permute-start.3) | collective-permute-done | bytes 262176 | tf_op jit(solution)/shard_map/ppermute | solution.py:81
  84.7 1.1 reshape.461
  85.8 7.2 %all-to-all-start.1 = ((bf16[32,2,2048]{2,1,0:T(2,128)(2,1)}), bf16[32,2,2048]{2,1,0:T(2,128)(2,1)S(1)}, u32[]{:S(2)}, u32[]{:S(2)}) async-start(bf16[32,2,2048]{2,1,0:T(2,128)(2,1)} %reshape.461), calls=%async_computation.1 | async-start | bytes 524288 | tf_op jit(solution)/shard_map/all_to_all | solution.py:104
  93.1 1.2 fusion.84
  94.2 7.6 %all-to-all-done.1 = bf16[32,2,2048]{2,1,0:T(2,128)(2,1)S(1)} async-done(((bf16[32,2,2048]{2,1,0:T(2,128)(2,1)}), bf16[32,2,2048]{2,1,0:T(2,128)(2,1)S(1)}, u32[]{:S(2)}, u32[]{:S(2)}) %all-to-all-start.1) | async-done | bytes 262176 | tf_op jit(solution)/shard_map/all_to_all | solution.py:104
  101.8 1.2 reshape.462
  103.0 2.2 %copy.21 = bf16[64,32,64]{2,1,0:T(8,128)(2,1)} copy(bf16[64,32,64]{2,0,1:T(8,128)(2,1)} %bitcast.65) | data formatting | bytes 524288 | tf_op jit(solution)/shard_map/transpose | solution.py:105
  105.2 2.2 %reshape.409 = bf16[64,2048]{1,0:T(8,128)(2,1)} reshape(bf16[64,32,64]{2,1,0:T(8,128)(2,1)} %copy.21) | data formatting | bytes 524288 | tf_op jit(solution)/shard_map/reshape | solution.py:105
  107.4 3.1 %fusion.102 = f32[64,1024]{1,0:T(8,128)S(1)} fusion(bf16[64,2048]{1,0:T(8,128)(2,1)} %reshape.409, bf16[2048,1024]{1,0:T(8,128)(2,1)} %fusion.35), kind=kOutput, calls=%fused_computation.184 | convolution fusion | flops 268435456 | bytes 4718592 | tf_op jit(solution)/shard_map/dot_general | solution.py:119
  110.5 5.9 %fusion.51 = bf16[64,1024]{1,0:T(8,128)(2,1)} fusion(f32[64,1024]{1,0:T(8,128)S(1)} %fusion.102, bf16[4096,1024]{1,0:T(8,128)(2,1)} %fusion.20, f32[64,4096]{1,0:T(8,128)S(1)} %fusion.84, bf16[128,4096]{1,0:T(8,128)(2,1)S(1)} %constant_dynamic-update-slice_fusion, bf16[128,256]{1,0:T(8,128)(2,1)} %bitcast.69, s32[]{:T(128)S(6)} %select_n.95), kind=kOutput, calls=%fused_computation.73 | convolution fusion | flops 604962816 | bytes 10911748 | tf_op jit(solution)/shard_map/dot_general | solution.py:118
  116.8 3.6 %collective-permute-start.7 = (bf16[64,1024]{1,0:T(8,128)(2,1)}, bf16[64,1024]{1,0:T(8,128)(2,1)S(1)}, u32[]{:S(2)}, u32[]{:S(2)}) collective-permute-start(bf16[64,1024]{1,0:T(8,128)(2,1)} %fusion.51), channel_id=1, source_target_pairs={{0,2},{1,3},{2,0},{3,1},{4,6},{5,7},{6,4},{7,5},{8,10},{9,11},{10,... | collective-permute-start | bytes 393224 | tf_op jit(solution)/shard_map/ppermute | solution.py:81
  120.4 1.2 fusion.71
  121.6 2.1 %collective-permute-done.6 = bf16[64,1024]{1,0:T(8,128)(2,1)S(1)} collective-permute-done((bf16[64,1024]{1,0:T(8,128)(2,1)}, bf16[64,1024]{1,0:T(8,128)(2,1)S(1)}, u32[]{:S(2)}, u32[]{:S(2)}) %collective-permute-start.6) | collective-permute-done | bytes 131104 | tf_op jit(solution)/shard_map/ppermute | solution.py:81
  123.7 3.5 %collective-permute-done.7 = bf16[64,1024]{1,0:T(8,128)(2,1)S(1)} collective-permute-done((bf16[64,1024]{1,0:T(8,128)(2,1)}, bf16[64,1024]{1,0:T(8,128)(2,1)S(1)}, u32[]{:S(2)}, u32[]{:S(2)}) %collective-permute-start.7) | collective-permute-done | bytes 131104 | tf_op jit(solution)/shard_map/ppermute | solution.py:81
  127.2 1.2 fusion.61
  128.3 2.0 %fusion.50 = bf16[64,1024]{1,0:T(8,128)(2,1)} fusion(f32[64,1024]{1,0:T(8,128)S(1)} %fusion.61, f32[256,1024]{1,0:T(8,128)S(1)} %fusion.71, bf16[128,256]{1,0:T(8,128)(2,1)} %bitcast.70, bf16[128,4096]{1,0:T(8,128)(2,1)S(1)} %constant_dynamic-update-slice_fusion, bf16[256,256]{1,0:T(8,128)(2,1)S(1)} %copy-done, s32[]{:T(128)S(6)} %select_n.95), kind=kOutput, calls=%fused_computation.72 | convolution fusion | flops 101580800 | bytes 1835012 | tf_op jit(solution)/shard_map/dot_general | solution.py:10
  (67 shorter events, 8.1 us)
Async XLA Ops:
  0.0 128.3 %copy-start = (bf16[256,256]{1,0:T(8,128)(2,1)S(1)}, bf16[256,256]{1,0:T(8,128)(2,1)}, u32[]{:S(2)}) copy-start(bf16[256,256]{1,0:T(8,128)(2,1)} %param.20) | copy-start | bytes 393220
  0.0 51.0 %collective-permute-start = (bf16[32,4096]{1,0:T(8,128)(2,1)}, bf16[32,4096]{1,0:T(8,128)(2,1)S(1)}, u32[]{:S(2)}, u32[]{:S(2)}) collective-permute-start(bf16[32,4096]{1,0:T(8,128)(2,1)} %param.12), channel_id=1, source_target_pairs={{0,1},{1,2},{2,3},{3,0},{4,5},{5,6},{6,7},{7,4},{8,9},{9,10},{10,1... | collective-permute-start | bytes 786440 | tf_op jit(solution)/shard_map/ppermute | solution.py:81
  1.6 49.4 %collective-permute-start.1 = (bf16[32,4096]{1,0:T(8,128)(2,1)}, bf16[32,4096]{1,0:T(8,128)(2,1)S(1)}, u32[]{:S(2)}, u32[]{:S(2)}) collective-permute-start(bf16[32,4096]{1,0:T(8,128)(2,1)} %param.12), channel_id=1, source_target_pairs={{0,2},{1,3},{2,0},{3,1},{4,6},{5,7},{6,4},{7,5},{8,10},{9,11},{10,... | collective-permute-start | bytes 786440 | tf_op jit(solution)/shard_map/ppermute | solution.py:81
  4.3 46.7 %collective-permute-start.2 = (bf16[32,4096]{1,0:T(8,128)(2,1)}, bf16[32,4096]{1,0:T(8,128)(2,1)S(1)}, u32[]{:S(2)}, u32[]{:S(2)}) collective-permute-start(bf16[32,4096]{1,0:T(8,128)(2,1)} %param.12), channel_id=1, source_target_pairs={{0,3},{1,0},{2,1},{3,2},{4,7},{5,4},{6,5},{7,6},{8,11},{9,8},{10,9... | collective-permute-start | bytes 786440 | tf_op jit(solution)/shard_map/ppermute | solution.py:81
  14.6 12.7 %copy-start.1 = (bf16[32,4096]{1,0:T(8,128)(2,1)S(1)}, bf16[32,4096]{1,0:T(8,128)(2,1)}, u32[]{:S(2)}) copy-start(bf16[32,4096]{1,0:T(8,128)(2,1)} %param.12) | copy-start | bytes 786436
  14.6 12.8 %copy-start.6 = (s32[32,1]{0,1:T(1,128)S(1)}, s32[32,1]{0,1:T(1,128)}, u32[]{:S(2)}) copy-start(s32[32,1]{0,1:T(1,128)} %param.15) | copy-start | bytes 388
  14.6 12.8 %copy-start.5 = (s32[32,1,512]{2,1,0:T(1,128)S(1)}, s32[32,1,512]{2,1,0:T(1,128)}, u32[]{:S(2)}) copy-start(s32[32,1,512]{2,1,0:T(1,128)} %param.14) | copy-start | bytes 196612
  14.6 13.0 %copy-start.4 = (s32[1024,10]{0,1:T(8,128)S(1)}, s32[1024,10]{0,1:T(8,128)}, u32[]{:S(2)}) copy-start(s32[1024,10]{0,1:T(8,128)} %param.17) | copy-start | bytes 122884
  17.6 33.5 %copy-start.7 = (s32[1,64]{1,0:T(1,128)S(1)}, s32[1,64]{1,0:T(1,128)}, u32[]{:S(2)}) copy-start(s32[1,64]{1,0:T(1,128)} %param.16) | copy-start | bytes 772
  18.7 33.3 %all-to-all-start = ((bf16[32,32,512]{2,0,1:T(8,128)(2,1)}), bf16[32,32,512]{2,0,1:T(8,128)(2,1)S(1)}, u32[]{:S(2)}, u32[]{:S(2)}) async-start(bf16[32,32,512]{2,0,1:T(8,128)(2,1)} %bitcast.59), calls=%async_computation | async-start | bytes 2097152 | tf_op jit(solution)/shard_map/all_to_all | solution.py:67
  51.0 6.9 %copy-start.2 = (bf16[4,32,256]{2,1,0:T(8,128)(2,1)}, bf16[4,32,256]{2,1,0:T(8,128)(2,1)S(1)}, u32[]{:S(2)}) copy-start(bf16[4,32,256]{2,1,0:T(8,128)(2,1)S(1)} %get-tuple-element.35) | copy-start | bytes 196612
  51.0 32.7 %copy-start.3 = (bf16[4,32,256]{2,1,0:T(8,128)(2,1)}, bf16[4,32,256]{2,1,0:T(8,128)(2,1)S(1)}, u32[]{:S(2)}) copy-start(bf16[4,32,256]{2,1,0:T(8,128)(2,1)S(1)} %get-tuple-element.34) | copy-start | bytes 196612
  67.8 15.2 %collective-permute-start.3 = (bf16[32,4096]{1,0:T(8,128)(2,1)S(1)}, bf16[32,4096]{1,0:T(8,128)(2,1)S(1)}, u32[]{:S(2)}, u32[]{:S(2)}) collective-permute-start(bf16[32,4096]{1,0:T(8,128)(2,1)S(1)} %divide_convert_fusion), channel_id=1, source_target_pairs={{0,1},{1,2},{2,3},{3,0},{4,5},{5,6},{6,7},{7,4},{8,9},{9,10},{10,1... | collective-permute-start | bytes 786440 | tf_op jit(solution)/shard_map/ppermute | solution.py:81
  68.5 14.6 %collective-permute-start.4 = (bf16[32,4096]{1,0:T(8,128)(2,1)S(1)}, bf16[32,4096]{1,0:T(8,128)(2,1)S(1)}, u32[]{:S(2)}, u32[]{:S(2)}) collective-permute-start(bf16[32,4096]{1,0:T(8,128)(2,1)S(1)} %divide_convert_fusion), channel_id=1, source_target_pairs={{0,2},{1,3},{2,0},{3,1},{4,6},{5,7},{6,4},{7,5},{8,10},{9,11},{10,... | collective-permute-start | bytes 786440 | tf_op jit(solution)/shard_map/ppermute | solution.py:81
  69.4 14.3 %collective-permute-start.5 = (bf16[32,4096]{1,0:T(8,128)(2,1)S(1)}, bf16[32,4096]{1,0:T(8,128)(2,1)S(1)}, u32[]{:S(2)}, u32[]{:S(2)}) collective-permute-start(bf16[32,4096]{1,0:T(8,128)(2,1)S(1)} %divide_convert_fusion), channel_id=1, source_target_pairs={{0,3},{1,0},{2,1},{3,2},{4,7},{5,4},{6,5},{7,6},{8,11},{9,8},{10,9... | collective-permute-start | bytes 786440 | tf_op jit(solution)/shard_map/ppermute | solution.py:81
  85.8 16.0 %all-to-all-start.1 = ((bf16[32,2,2048]{2,1,0:T(2,128)(2,1)}), bf16[32,2,2048]{2,1,0:T(2,128)(2,1)S(1)}, u32[]{:S(2)}, u32[]{:S(2)}) async-start(bf16[32,2,2048]{2,1,0:T(2,128)(2,1)} %reshape.461), calls=%async_computation.1 | async-start | bytes 524288 | tf_op jit(solution)/shard_map/all_to_all | solution.py:104
  116.5 7.2 %collective-permute-start.6 = (bf16[64,1024]{1,0:T(8,128)(2,1)}, bf16[64,1024]{1,0:T(8,128)(2,1)S(1)}, u32[]{:S(2)}, u32[]{:S(2)}) collective-permute-start(bf16[64,1024]{1,0:T(8,128)(2,1)} %fusion.51), channel_id=1, source_target_pairs={{0,1},{1,2},{2,3},{3,0},{4,5},{5,6},{6,7},{7,4},{8,9},{9,10},{10,1... | collective-permute-start | bytes 393224 | tf_op jit(solution)/shard_map/ppermute | solution.py:81
  116.8 10.3 %collective-permute-start.7 = (bf16[64,1024]{1,0:T(8,128)(2,1)}, bf16[64,1024]{1,0:T(8,128)(2,1)S(1)}, u32[]{:S(2)}, u32[]{:S(2)}) collective-permute-start(bf16[64,1024]{1,0:T(8,128)(2,1)} %fusion.51), channel_id=1, source_target_pairs={{0,2},{1,3},{2,0},{3,1},{4,6},{5,7},{6,4},{7,5},{8,10},{9,11},{10,... | collective-permute-start | bytes 393224 | tf_op jit(solution)/shard_map/ppermute | solution.py:81
  120.4 6.8 %collective-permute-start.8 = (bf16[64,1024]{1,0:T(8,128)(2,1)}, bf16[64,1024]{1,0:T(8,128)(2,1)S(1)}, u32[]{:S(2)}, u32[]{:S(2)}) collective-permute-start(bf16[64,1024]{1,0:T(8,128)(2,1)} %fusion.51), channel_id=1, source_target_pairs={{0,3},{1,0},{2,1},{3,2},{4,7},{5,4},{6,5},{7,6},{8,11},{9,8},{10,9... | collective-permute-start | bytes 393224 | tf_op jit(solution)/shard_map/ppermute | solution.py:81

commit v10 on v8

--- a/solution.py
+++ b/solution.py
@@ -87,7 +87,10 @@
 
     self_one = ring_rows(self_one)
     neigh_one = ring_rows(neigh_one)
-    own_all = ring_gather(features)
+    half = lax.ppermute(features, "feat", perm=[(j, (j + 1) % n_feat) for j in range(n_feat)])
+    pair = jnp.concatenate([features, half], axis=0)
+    far = lax.ppermute(pair, "feat", perm=[(j, (j + 2) % n_feat) for j in range(n_feat)])
+    own_all = jnp.concatenate([pair, far], axis=0)
     mean_all = ring_gather(mean_one)
     w_own = lax.dynamic_slice_in_dim(self_one, column_index * hcols, hcols, 1)
     w_near = lax.dynamic_slice_in_dim(neigh_one, column_index * hcols, hcols, 1)

time: 121 us -> 131 us (1.083)
  waiting for transfers between devices: 13.3 us -> 23.6 us
    ppermute x0 -> x2, waiting for transfers between devices: none -> 12.7 us  [the longest x1 12.7 us: body(): lax.ppermute(pair, 'feat', perm=[(j, (j + 2) % n_feat) for j in range(n_f...]
    ppermute x0 -> x2, starting transfers between devices: none -> 4.64 us  [the longest x1 3.03 us: body(): lax.ppermute(pair, 'feat', perm=[(j, (j + 2) % n_feat) for j in range(n_f...]
    ppermute x9 -> x6, starting transfers between devices: 12.7 us -> 9.09 us  [ring_gather(): parts.append(lax.ppermute(x, 'feat', perm=pairs))]
    ppermute x9 -> x6, waiting for transfers between devices: 9.47 us -> 7.13 us  [ring_gather(): parts.append(lax.ppermute(x, 'feat', perm=pairs))]
    unnamed x34 -> x33, local copies, waits for them, and re-layouts: 4.58 us -> 3.58 us
  transfers between devices with their start and end apart: 11 -> 10, of which waited for: 6 -> 5; matrix products, arithmetic and copies ran while one was open for 43% -> 39% of each run, Pallas kernels for 0% -> 0%
where the time goes in v10:
time: 131 us; the launch traced here: 129 us
  other arithmetic  37.9 us (29%)
  matrix products  30 us (23%)
  starting transfers between devices  29.5 us (23%)
  waiting for transfers between devices  23.6 us (18%)
  local copies, waits for them, and re-layouts  8.03 us (6%)
    add x1, other arithmetic, body(): near_tally = near_tally + (near_places == picked).astype(jnp.bfloat16)  17.9 us
    ppermute x1, waiting for transfers between devices, body(): lax.ppermute(pair, 'feat', perm=[(j, (j + 2) % n_feat) for j in range(n_f...  12.7 us
    add x1, other arithmetic, body(): hub_tally = hub_tally + (hub_places == late).astype(jnp.bfloat16)  9.89 us
    dot_general x1, matrix products, add_columns(): total = jnp.dot(spread, marks, preferred_element_type=jnp.float32)  9.81 us
    ppermute x6, starting transfers between devices, ring_gather(): parts.append(lax.ppermute(x, 'feat', perm=pairs))  9.09 us
    all_to_all x1, starting transfers between devices, body(): lax.all_to_all(chosen, 'dom', split_axis=1, concat_axis=1, tiled=True)  8.51 us
    all_to_all x1, starting transfers between devices, body(): lax.all_to_all(spread, 'dom', split_axis=0, concat_axis=0, tiled=True)  7.24 us
    ppermute x6, waiting for transfers between devices, ring_gather(): parts.append(lax.ppermute(x, 'feat', perm=pairs))  7.13 us
  transfers between devices with their start and end apart: 10, of which 5 were waited for; matrix products, arithmetic and copies ran while one was open for 39% of the time, Pallas kernels for 0%

profile of v10, /device:TPU:0, one launch (start us, length us, event | category | flops | bytes accessed | tf_op | source)
XLA Modules:
  0.0 129.5 jit_solution(1243174152652922107)
XLA Ops:
  0.0 1.6 %collective-permute-start = (bf16[32,4096]{1,0:T(8,128)(2,1)}, bf16[32,4096]{1,0:T(8,128)(2,1)S(1)}, u32[]{:S(2)}, u32[]{:S(2)}) collective-permute-start(bf16[32,4096]{1,0:T(8,128)(2,1)} %param.12), channel_id=1, source_target_pairs={{0,1},{1,2},{2,3},{3,0},{4,5},{5,6},{6,7},{7,4},{8,9},{9,10},{10,1... | collective-permute-start | bytes 786440 | tf_op jit(solution)/shard_map/ppermute | solution.py:90
  1.6 1.1 copy.26
  2.8 0.9 copy.25
  3.8 6.6 %fusion.5 = bf16[16384,256]{0,1:T(8,128)(2,1)S(1)} fusion(bf16[256,512]{1,0:T(8,128)(2,1)S(1)} %bitcast.72, s16[16384]{0:T(1024)(128)(2,1)S(1)} %get-tuple-element.31), kind=kOutput, calls=%fused_computation.8 | convolution fusion | flops 4307550208 | bytes 8683520 | tf_op jit(solution)/shard_map/dot_general | solution.py:23
  10.5 2.9 %select_reduce_fusion = bf16[32,16384]{1,0:T(8,128)(2,1)S(1)} fusion(bf16[8,32,16384]{2,1,0:T(8,128)(2,1)S(1)} %bitcast.60, pred[8,16384]{1,0:T(8,128)(4,1)S(1)} %iota_compare_fusion.4), kind=kLoop, calls=%fused_computation.33 | loop fusion | flops 7864320 | bytes 9568256 | tf_op jit(solution)/shard_map/reduce_sum | solution.py:26
  13.5 1.1 copy.29
  14.6 8.5 %all-to-all-start = ((bf16[32,32,512]{2,0,1:T(8,128)(2,1)}), bf16[32,32,512]{2,0,1:T(8,128)(2,1)S(1)}, u32[]{:S(2)}, u32[]{:S(2)}) async-start(bf16[32,32,512]{2,0,1:T(8,128)(2,1)} %bitcast.59), calls=%async_computation | async-start | bytes 2097152 | tf_op jit(solution)/shard_map/all_to_all | solution.py:67
  23.8 0.6 gather_fusion
  24.4 0.7 bitcast_select_fusion
  25.1 17.9 %fusion.20 = bf16[4096,1024]{1,0:T(8,128)(2,1)} fusion(s16[1024]{0:T(1024)(128)(2,1)S(1)} %get-tuple-element.21, s16[1024]{0:T(1024)(128)(2,1)S(1)} %get-tuple-element.22, s16[1024]{0:T(1024)(128)(2,1)S(1)} %get-tuple-element.23, s16[1024]{0:T(1024)(128)(2,1)S(1)} %get-tuple-element.24, s16[1024]{0:T(1024)(128)(2,1)S(1)} %get-tuple-element.25, ...), kind=kLoop, calls=%fused_computation.31 | loop fusion | flops 167772160 | bytes 8409088 | tf_op jit(solution)/shard_map/add | solution.py:112
  43.1 0.6 gather_fusion.1
  44.4 3.0 %collective-permute-start.1 = (bf16[64,4096]{1,0:T(8,128)(2,1)S(1)}, bf16[64,4096]{1,0:T(8,128)(2,1)S(1)}, u32[]{:S(2)}, u32[]{:S(2)}) collective-permute-start(bf16[64,4096]{1,0:T(8,128)(2,1)S(1)} %pad_maximum_fusion), channel_id=1, source_target_pairs={{0,2},{1,3},{2,0},{3,1},{4,6},{5,7},{6,4},{7,5},{8,10},{9,11},{10,... | collective-permute-start | bytes 1572872 | tf_op jit(solution)/shard_map/ppermute | solution.py:92
  47.5 12.7 %collective-permute-done.1 = bf16[64,4096]{1,0:T(8,128)(2,1)S(1)} collective-permute-done((bf16[64,4096]{1,0:T(8,128)(2,1)S(1)}, bf16[64,4096]{1,0:T(8,128)(2,1)S(1)}, u32[]{:S(2)}, u32[]{:S(2)}) %collective-permute-start.1) | collective-permute-done | bytes 524320 | tf_op jit(solution)/shard_map/ppermute | solution.py:92
  60.5 5.6 %fusion.102 = bf16[8,33,16384]{2,1,0:T(8,128)(2,1)} fusion(pred[8,16384]{1,0:T(8,128)(4,1)S(1)} %iota_compare_fusion.5, bf16[33,16384]{1,0:T(8,128)(2,1)S(1)} %pad_multiply_fusion), kind=kLoop, calls=%fused_computation.21.clone.clone.clone.2 | loop fusion | flops 4325376 | bytes 9863168 | tf_op jit(solution)/shard_map/dot_general | solution.py:40
  66.1 9.8 %fusion.39 = f32[33,8,512]{2,0,1:T(8,128)S(1)} fusion(s16[16384]{0:T(1024)(128)(2,1)S(1)} %get-tuple-element.33, bf16[8,33,16384]{2,1,0:T(8,128)(2,1)} %fusion.102), kind=kOutput, calls=%fused_computation.65 | convolution fusion | flops 4437573632 | bytes 9224192 | tf_op jit(solution)/shard_map/dot_general | solution.py:40
  76.1 1.6 %collective-permute-start.2 = (bf16[32,4096]{1,0:T(8,128)(2,1)S(1)}, bf16[32,4096]{1,0:T(8,128)(2,1)S(1)}, u32[]{:S(2)}, u32[]{:S(2)}) collective-permute-start(bf16[32,4096]{1,0:T(8,128)(2,1)S(1)} %divide_convert_fusion), channel_id=1, source_target_pairs={{0,1},{1,2},{2,3},{3,0},{4,5},{5,6},{6,7},{7,4},{8,9},{9,10},{10,1... | collective-permute-start | bytes 786440 | tf_op jit(solution)/shard_map/ppermute | solution.py:81
  77.6 1.7 %collective-permute-start.3 = (bf16[32,4096]{1,0:T(8,128)(2,1)S(1)}, bf16[32,4096]{1,0:T(8,128)(2,1)S(1)}, u32[]{:S(2)}, u32[]{:S(2)}) collective-permute-start(bf16[32,4096]{1,0:T(8,128)(2,1)S(1)} %divide_convert_fusion), channel_id=1, source_target_pairs={{0,2},{1,3},{2,0},{3,1},{4,6},{5,7},{6,4},{7,5},{8,10},{9,11},{10,... | collective-permute-start | bytes 786440 | tf_op jit(solution)/shard_map/ppermute | solution.py:81
  79.4 2.2 %collective-permute-start.4 = (bf16[32,4096]{1,0:T(8,128)(2,1)S(1)}, bf16[32,4096]{1,0:T(8,128)(2,1)S(1)}, u32[]{:S(2)}, u32[]{:S(2)}) collective-permute-start(bf16[32,4096]{1,0:T(8,128)(2,1)S(1)} %divide_convert_fusion), channel_id=1, source_target_pairs={{0,3},{1,0},{2,1},{3,2},{4,7},{5,4},{6,5},{7,6},{8,11},{9,8},{10,9... | collective-permute-start | bytes 786440 | tf_op jit(solution)/shard_map/ppermute | solution.py:81
  81.6 9.9 %fusion.35 = bf16[2048,1024]{1,0:T(8,128)(2,1)} fusion(s16[1024]{0:T(1024)(128)(2,1)S(1)} %get-tuple-element.11, s16[1024]{0:T(1024)(128)(2,1)S(1)} %get-tuple-element.12, s16[1024]{0:T(1024)(128)(2,1)S(1)} %get-tuple-element.13, s16[1024]{0:T(1024)(128)(2,1)S(1)} %get-tuple-element.14, s16[1024]{0:T(1024)(128)(2,1)S(1)} %get-tuple-element.15, ...), kind=kLoop, calls=%fused_computation.58 | loop fusion | flops 60817408 | bytes 4218880 | tf_op jit(solution)/shard_map/add | solution.py:114
  93.2 1.1 reshape.461
  94.3 7.2 %all-to-all-start.1 = ((bf16[32,2,2048]{2,1,0:T(2,128)(2,1)}), bf16[32,2,2048]{2,1,0:T(2,128)(2,1)S(1)}, u32[]{:S(2)}, u32[]{:S(2)}) async-start(bf16[32,2,2048]{2,1,0:T(2,128)(2,1)} %reshape.461), calls=%async_computation.1 | async-start | bytes 524288 | tf_op jit(solution)/shard_map/all_to_all | solution.py:103
  101.5 4.9 %fusion.84 = f32[64,1024]{1,0:T(8,128)S(1)} fusion(bf16[64,4096]{1,0:T(8,128)(2,1)S(1)} %fusion.26, bf16[4096,1024]{1,0:T(8,128)(2,1)} %fusion.20), kind=kOutput, calls=%fused_computation.170 | convolution fusion | flops 536870912 | bytes 9175040 | tf_op jit(solution)/shard_map/dot_general | solution.py:117
  106.5 3.8 %all-to-all-done.1 = bf16[32,2,2048]{2,1,0:T(2,128)(2,1)S(1)} async-done(((bf16[32,2,2048]{2,1,0:T(2,128)(2,1)}), bf16[32,2,2048]{2,1,0:T(2,128)(2,1)S(1)}, u32[]{:S(2)}, u32[]{:S(2)}) %all-to-all-start.1) | async-done | bytes 262176 | tf_op jit(solution)/shard_map/all_to_all | solution.py:103
  111.5 3.0 %fusion.47 = bf16[64,1024]{1,0:T(8,128)(2,1)S(1)} fusion(f32[64,1024]{1,0:T(8,128)S(1)} %fusion.84, bf16[64,2048]{1,0:T(8,128)(2,1)S(1)} %reshape.409, bf16[2048,1024]{1,0:T(8,128)(2,1)} %fusion.35), kind=kOutput, calls=%fused_computation.70 | convolution fusion | flops 268632064 | bytes 4849664 | tf_op jit(solution)/shard_map/dot_general | solution.py:118
  114.5 2.1 %collective-permute-start.7 = (bf16[64,1024]{1,0:T(8,128)(2,1)S(1)}, bf16[64,1024]{1,0:T(8,128)(2,1)S(1)}, u32[]{:S(2)}, u32[]{:S(2)}) collective-permute-start(bf16[64,1024]{1,0:T(8,128)(2,1)S(1)} %fusion.47), channel_id=1, source_target_pairs={{0,3},{1,0},{2,1},{3,2},{4,7},{5,4},{6,5},{7,6},{8,11},{9,8},{10,9... | collective-permute-start | bytes 393224 | tf_op jit(solution)/shard_map/ppermute | solution.py:81
  116.6 1.1 collective-permute-start.6
  118.2 1.2 fusion.60
  119.3 3.4 %collective-permute-done.7 = bf16[64,1024]{1,0:T(8,128)(2,1)S(1)} collective-permute-done((bf16[64,1024]{1,0:T(8,128)(2,1)S(1)}, bf16[64,1024]{1,0:T(8,128)(2,1)S(1)}, u32[]{:S(2)}, u32[]{:S(2)}) %collective-permute-start.7) | collective-permute-done | bytes 131104 | tf_op jit(solution)/shard_map/ppermute | solution.py:81
  122.8 1.7 %collective-permute-done.6 = bf16[64,1024]{1,0:T(8,128)(2,1)S(1)} collective-permute-done((bf16[64,1024]{1,0:T(8,128)(2,1)S(1)}, bf16[64,1024]{1,0:T(8,128)(2,1)S(1)}, u32[]{:S(2)}, u32[]{:S(2)}) %collective-permute-start.6) | collective-permute-done | bytes 131104 | tf_op jit(solution)/shard_map/ppermute | solution.py:81
  124.5 1.9 %collective-permute-done.5 = bf16[64,1024]{1,0:T(8,128)(2,1)S(1)} collective-permute-done((bf16[64,1024]{1,0:T(8,128)(2,1)S(1)}, bf16[64,1024]{1,0:T(8,128)(2,1)S(1)}, u32[]{:S(2)}, u32[]{:S(2)}) %collective-permute-start.5) | collective-permute-done | bytes 131104 | tf_op jit(solution)/shard_map/ppermute | solution.py:81
  126.4 1.1 fusion.51
  127.5 2.0 %fusion.48 = bf16[64,1024]{1,0:T(8,128)(2,1)} fusion(f32[64,1024]{1,0:T(8,128)S(1)} %fusion.51, f32[256,1024]{1,0:T(8,128)S(1)} %fusion.60, bf16[128,256]{1,0:T(8,128)(2,1)} %bitcast.69, bf16[128,4096]{1,0:T(8,128)(2,1)S(1)} %constant_dynamic-update-slice_fusion, bf16[256,256]{1,0:T(8,128)(2,1)S(1)} %copy-done, s32[]{:T(128)S(6)} %select_n.95), kind=kOutput, calls=%fused_computation.71 | convolution fusion | flops 101580800 | bytes 1835012 | tf_op jit(solution)/shard_map/dot_general | solution.py:10
  (70 shorter events, 5.3 us)
Async XLA Ops:
  0.0 127.5 %copy-start = (bf16[256,256]{1,0:T(8,128)(2,1)S(1)}, bf16[256,256]{1,0:T(8,128)(2,1)}, u32[]{:S(2)}) copy-start(bf16[256,256]{1,0:T(8,128)(2,1)} %param.20) | copy-start | bytes 393220
  0.0 44.4 %collective-permute-start = (bf16[32,4096]{1,0:T(8,128)(2,1)}, bf16[32,4096]{1,0:T(8,128)(2,1)S(1)}, u32[]{:S(2)}, u32[]{:S(2)}) collective-permute-start(bf16[32,4096]{1,0:T(8,128)(2,1)} %param.12), channel_id=1, source_target_pairs={{0,1},{1,2},{2,3},{3,0},{4,5},{5,6},{6,7},{7,4},{8,9},{9,10},{10,1... | collective-permute-start | bytes 786440 | tf_op jit(solution)/shard_map/ppermute | solution.py:90
  10.4 12.7 %copy-start.1 = (bf16[32,4096]{1,0:T(8,128)(2,1)S(1)}, bf16[32,4096]{1,0:T(8,128)(2,1)}, u32[]{:S(2)}) copy-start(bf16[32,4096]{1,0:T(8,128)(2,1)} %param.12) | copy-start | bytes 786436
  10.4 12.9 %copy-start.5 = (s32[32,1,512]{2,1,0:T(1,128)S(1)}, s32[32,1,512]{2,1,0:T(1,128)}, u32[]{:S(2)}) copy-start(s32[32,1,512]{2,1,0:T(1,128)} %param.14) | copy-start | bytes 196612
  10.5 13.1 %copy-start.4 = (s32[1024,10]{0,1:T(8,128)S(1)}, s32[1024,10]{0,1:T(8,128)}, u32[]{:S(2)}) copy-start(s32[1024,10]{0,1:T(8,128)} %param.17) | copy-start | bytes 122884
  10.5 13.2 %copy-start.8 = (bf16[256,256]{1,0:T(8,128)(2,1)S(1)}, bf16[256,256]{1,0:T(8,128)(2,1)}, u32[]{:S(2)}) copy-start(bf16[256,256]{1,0:T(8,128)(2,1)} %param.21) | copy-start | bytes 393220
  13.4 29.6 %copy-start.9 = (s32[32,1]{0,1:T(1,128)S(1)}, s32[32,1]{0,1:T(1,128)}, u32[]{:S(2)}) copy-start(s32[32,1]{0,1:T(1,128)} %param.15) | copy-start | bytes 388
  13.4 29.7 %copy-start.6 = (bf16[128,256]{1,0:T(8,128)(2,1)S(1)}, bf16[128,256]{1,0:T(8,128)(2,1)}, u32[]{:S(2)}) copy-start(bf16[128,256]{1,0:T(8,128)(2,1)} %param.18) | copy-start | bytes 196612
  13.5 30.3 %copy-start.7 = (bf16[128,256]{1,0:T(8,128)(2,1)S(1)}, bf16[128,256]{1,0:T(8,128)(2,1)}, u32[]{:S(2)}) copy-start(bf16[128,256]{1,0:T(8,128)(2,1)} %param.19) | copy-start | bytes 196612
  14.6 45.6 %all-to-all-start = ((bf16[32,32,512]{2,0,1:T(8,128)(2,1)}), bf16[32,32,512]{2,0,1:T(8,128)(2,1)S(1)}, u32[]{:S(2)}, u32[]{:S(2)}) async-start(bf16[32,32,512]{2,0,1:T(8,128)(2,1)} %bitcast.59), calls=%async_computation | async-start | bytes 2097152 | tf_op jit(solution)/shard_map/all_to_all | solution.py:67
  44.4 47.3 %copy-start.3 = (bf16[4,32,256]{2,1,0:T(8,128)(2,1)}, bf16[4,32,256]{2,1,0:T(8,128)(2,1)S(1)}, u32[]{:S(2)}) copy-start(bf16[4,32,256]{2,1,0:T(8,128)(2,1)S(1)} %get-tuple-element.35) | copy-start | bytes 196612
  44.4 47.7 %copy-start.2 = (bf16[4,32,256]{2,1,0:T(8,128)(2,1)}, bf16[4,32,256]{2,1,0:T(8,128)(2,1)S(1)}, u32[]{:S(2)}) copy-start(bf16[4,32,256]{2,1,0:T(8,128)(2,1)S(1)} %get-tuple-element.34) | copy-start | bytes 196612
  44.4 15.7 %collective-permute-start.1 = (bf16[64,4096]{1,0:T(8,128)(2,1)S(1)}, bf16[64,4096]{1,0:T(8,128)(2,1)S(1)}, u32[]{:S(2)}, u32[]{:S(2)}) collective-permute-start(bf16[64,4096]{1,0:T(8,128)(2,1)S(1)} %pad_maximum_fusion), channel_id=1, source_target_pairs={{0,2},{1,3},{2,0},{3,1},{4,6},{5,7},{6,4},{7,5},{8,10},{9,11},{10,... | collective-permute-start | bytes 1572872 | tf_op jit(solution)/shard_map/ppermute | solution.py:92
  75.9 16.6 %copy-start.10 = (s32[1,64]{1,0:T(1,128)S(1)}, s32[1,64]{1,0:T(1,128)}, u32[]{:S(2)}) copy-start(s32[1,64]{1,0:T(1,128)} %param.16) | copy-start | bytes 772
  76.1 15.5 %collective-permute-start.2 = (bf16[32,4096]{1,0:T(8,128)(2,1)S(1)}, bf16[32,4096]{1,0:T(8,128)(2,1)S(1)}, u32[]{:S(2)}, u32[]{:S(2)}) collective-permute-start(bf16[32,4096]{1,0:T(8,128)(2,1)S(1)} %divide_convert_fusion), channel_id=1, source_target_pairs={{0,1},{1,2},{2,3},{3,0},{4,5},{5,6},{6,7},{7,4},{8,9},{9,10},{10,1... | collective-permute-start | bytes 786440 | tf_op jit(solution)/shard_map/ppermute | solution.py:81
  77.6 14.0 %collective-permute-start.3 = (bf16[32,4096]{1,0:T(8,128)(2,1)S(1)}, bf16[32,4096]{1,0:T(8,128)(2,1)S(1)}, u32[]{:S(2)}, u32[]{:S(2)}) collective-permute-start(bf16[32,4096]{1,0:T(8,128)(2,1)S(1)} %divide_convert_fusion), channel_id=1, source_target_pairs={{0,2},{1,3},{2,0},{3,1},{4,6},{5,7},{6,4},{7,5},{8,10},{9,11},{10,... | collective-permute-start | bytes 786440 | tf_op jit(solution)/shard_map/ppermute | solution.py:81
  79.4 12.3 %collective-permute-start.4 = (bf16[32,4096]{1,0:T(8,128)(2,1)S(1)}, bf16[32,4096]{1,0:T(8,128)(2,1)S(1)}, u32[]{:S(2)}, u32[]{:S(2)}) collective-permute-start(bf16[32,4096]{1,0:T(8,128)(2,1)S(1)} %divide_convert_fusion), channel_id=1, source_target_pairs={{0,3},{1,0},{2,1},{3,2},{4,7},{5,4},{6,5},{7,6},{8,11},{9,8},{10,9... | collective-permute-start | bytes 786440 | tf_op jit(solution)/shard_map/ppermute | solution.py:81
  94.3 16.0 %all-to-all-start.1 = ((bf16[32,2,2048]{2,1,0:T(2,128)(2,1)}), bf16[32,2,2048]{2,1,0:T(2,128)(2,1)S(1)}, u32[]{:S(2)}, u32[]{:S(2)}) async-start(bf16[32,2,2048]{2,1,0:T(2,128)(2,1)} %reshape.461), calls=%async_computation.1 | async-start | bytes 524288 | tf_op jit(solution)/shard_map/all_to_all | solution.py:103
  114.5 8.3 %collective-permute-start.7 = (bf16[64,1024]{1,0:T(8,128)(2,1)S(1)}, bf16[64,1024]{1,0:T(8,128)(2,1)S(1)}, u32[]{:S(2)}, u32[]{:S(2)}) collective-permute-start(bf16[64,1024]{1,0:T(8,128)(2,1)S(1)} %fusion.47), channel_id=1, source_target_pairs={{0,3},{1,0},{2,1},{3,2},{4,7},{5,4},{6,5},{7,6},{8,11},{9,8},{10,9... | collective-permute-start | bytes 393224 | tf_op jit(solution)/shard_map/ppermute | solution.py:81
  116.6 7.9 %collective-permute-start.6 = (bf16[64,1024]{1,0:T(8,128)(2,1)S(1)}, bf16[64,1024]{1,0:T(8,128)(2,1)S(1)}, u32[]{:S(2)}, u32[]{:S(2)}) collective-permute-start(bf16[64,1024]{1,0:T(8,128)(2,1)S(1)} %fusion.47), channel_id=1, source_target_pairs={{0,2},{1,3},{2,0},{3,1},{4,6},{5,7},{6,4},{7,5},{8,10},{9,11},{10,... | collective-permute-start | bytes 393224 | tf_op jit(solution)/shard_map/ppermute | solution.py:81
  117.8 8.7 %collective-permute-start.5 = (bf16[64,1024]{1,0:T(8,128)(2,1)S(1)}, bf16[64,1024]{1,0:T(8,128)(2,1)S(1)}, u32[]{:S(2)}, u32[]{:S(2)}) collective-permute-start(bf16[64,1024]{1,0:T(8,128)(2,1)S(1)} %fusion.47), channel_id=1, source_target_pairs={{0,1},{1,2},{2,3},{3,0},{4,5},{5,6},{6,7},{7,4},{8,9},{9,10},{10,1... | collective-permute-start | bytes 393224 | tf_op jit(solution)/shard_map/ppermute | solution.py:81

commit v11 on v8

--- a/solution.py
+++ b/solution.py
@@ -96,8 +96,10 @@
     hub_marks = (jnp.arange(node_dev, dtype=jnp.int32)[:, None] == hub_local[0][None, :]).astype(jnp.bfloat16)
     hub_rows = jnp.dot(hidden_one, hub_marks, preferred_element_type=jnp.float32).astype(jnp.bfloat16)
     hub_count = hub_rows.shape[1]
-    spread = jnp.broadcast_to(hub_rows[None], (n_dom,) + hub_rows.shape)
+    flat = hub_rows.reshape(1, -1)
+    spread = jnp.broadcast_to(flat, (n_dom, flat.shape[1]))
     landed = lax.all_to_all(spread, "dom", split_axis=0, concat_axis=0, tiled=True)
+    landed = landed.reshape((n_dom,) + hub_rows.shape)
     hub_table = landed.transpose(1, 0, 2).reshape(hidden_one.shape[0], n_dom * hub_count)
     tgt_dev, fanout = second_source.shape
     near_places = jnp.arange(node_dev, dtype=jnp.int16)[:, None]

time: 121 us -> 125 us (1.033)
  other arithmetic: 38.1 us -> 41.8 us
    broadcast_in_dim x0 -> x1, other arithmetic: none -> 2.14 us  [body(): spread = jnp.broadcast_to(flat, (n_dom, flat.shape[1]))]
    all_to_all x0 -> x1, other arithmetic: none -> 1.53 us  [body(): lax.all_to_all(spread, 'dom', split_axis=0, concat_axis=0, tiled=True)]
  transfers between devices with their start and end apart: 11 -> 11, of which waited for: 6 -> 6; matrix products, arithmetic and copies ran while one was open for 43% -> 41% of each run, Pallas kernels for 0% -> 0%
where the time goes in v11:
time: 125 us; the launch traced here: 124 us
  other arithmetic  41.8 us (33%)
  matrix products  30 us (24%)
  starting transfers between devices  28.4 us (23%)
  waiting for transfers between devices  13.3 us (11%)
  local copies, waits for them, and re-layouts  10.2 us (8%)
    add x1, other arithmetic, body(): near_tally = near_tally + (near_places == picked).astype(jnp.bfloat16)  17.9 us
    ppermute x9, starting transfers between devices, ring_gather(): parts.append(lax.ppermute(x, 'feat', perm=pairs))  12.7 us
    add x1, other arithmetic, body(): hub_tally = hub_tally + (hub_places == late).astype(jnp.bfloat16)  10.1 us
    dot_general x1, matrix products, add_columns(): total = jnp.dot(spread, marks, preferred_element_type=jnp.float32)  9.81 us
    ppermute x9, waiting for transfers between devices, ring_gather(): parts.append(lax.ppermute(x, 'feat', perm=pairs))  9.47 us
    all_to_all x1, starting transfers between devices, body(): lax.all_to_all(chosen, 'dom', split_axis=1, concat_axis=1, tiled=True)  8.51 us
    all_to_all x1, starting transfers between devices, body(): lax.all_to_all(spread, 'dom', split_axis=0, concat_axis=0, tiled=True)  7.24 us
    dot_general x1, matrix products, pick_columns(): jnp.dot(stacked, onehot, preferred_element_type=jnp.float32)  6.64 us
  transfers between devices with their start and end apart: 11, of which 6 were waited for; matrix products, arithmetic and copies ran while one was open for 41% of the time, Pallas kernels for 0%

profile of v11, /device:TPU:0, one launch (start us, length us, event | category | flops | bytes accessed | tf_op | source)
XLA Modules:
  0.0 124.2 jit_solution(16476975166984624161)
XLA Ops:
  0.0 1.6 %collective-permute-start = (bf16[32,4096]{1,0:T(8,128)(2,1)}, bf16[32,4096]{1,0:T(8,128)(2,1)}, u32[]{:S(2)}, u32[]{:S(2)}) collective-permute-start(bf16[32,4096]{1,0:T(8,128)(2,1)} %param.12), channel_id=1, source_target_pairs={{0,1},{1,2},{2,3},{3,0},{4,5},{5,6},{6,7},{7,4},{8,9},{9,10},{10,1... | collective-permute-start | bytes 786440 | tf_op jit(solution)/shard_map/ppermute | solution.py:81
  1.6 2.7 %collective-permute-start.1 = (bf16[32,4096]{1,0:T(8,128)(2,1)}, bf16[32,4096]{1,0:T(8,128)(2,1)S(1)}, u32[]{:S(2)}, u32[]{:S(2)}) collective-permute-start(bf16[32,4096]{1,0:T(8,128)(2,1)} %param.12), channel_id=1, source_target_pairs={{0,2},{1,3},{2,0},{3,1},{4,6},{5,7},{6,4},{7,5},{8,10},{9,11},{10,... | collective-permute-start | bytes 786440 | tf_op jit(solution)/shard_map/ppermute | solution.py:81
  4.3 1.4 %collective-permute-start.2 = (bf16[32,4096]{1,0:T(8,128)(2,1)}, bf16[32,4096]{1,0:T(8,128)(2,1)S(1)}, u32[]{:S(2)}, u32[]{:S(2)}) collective-permute-start(bf16[32,4096]{1,0:T(8,128)(2,1)} %param.12), channel_id=1, source_target_pairs={{0,3},{1,0},{2,1},{3,2},{4,7},{5,4},{6,5},{7,6},{8,11},{9,8},{10,9... | collective-permute-start | bytes 786440 | tf_op jit(solution)/shard_map/ppermute | solution.py:81
  5.8 1.1 copy.28
  6.9 0.9 copy.27
  7.9 6.6 %fusion.5 = bf16[16384,256]{0,1:T(8,128)(2,1)S(1)} fusion(bf16[256,512]{1,0:T(8,128)(2,1)S(1)} %bitcast.72, s16[16384]{0:T(1024)(128)(2,1)S(1)} %get-tuple-element.31), kind=kOutput, calls=%fused_computation.8 | convolution fusion | flops 4307550208 | bytes 8683520 | tf_op jit(solution)/shard_map/dot_general | solution.py:23
  14.7 2.9 %select_reduce_fusion = bf16[32,16384]{1,0:T(8,128)(2,1)S(1)} fusion(bf16[8,32,16384]{2,1,0:T(8,128)(2,1)S(1)} %bitcast.60, pred[8,16384]{1,0:T(8,128)(4,1)S(1)} %iota_compare_fusion.4), kind=kLoop, calls=%fused_computation.33 | loop fusion | flops 7864320 | bytes 9568256 | tf_op jit(solution)/shard_map/reduce_sum | solution.py:26
  17.6 1.1 copy.31
  18.8 8.5 %all-to-all-start = ((bf16[32,32,512]{2,0,1:T(8,128)(2,1)}), bf16[32,32,512]{2,0,1:T(8,128)(2,1)S(1)}, u32[]{:S(2)}, u32[]{:S(2)}) async-start(bf16[32,32,512]{2,0,1:T(8,128)(2,1)} %bitcast.59), calls=%async_computation | async-start | bytes 2097152 | tf_op jit(solution)/shard_map/all_to_all | solution.py:67
  29.4 17.9 %fusion.20 = bf16[4096,1024]{1,0:T(8,128)(2,1)} fusion(s16[1024]{0:T(1024)(128)(2,1)S(1)} %get-tuple-element.21, s16[1024]{0:T(1024)(128)(2,1)S(1)} %get-tuple-element.22, s16[1024]{0:T(1024)(128)(2,1)S(1)} %get-tuple-element.23, s16[1024]{0:T(1024)(128)(2,1)S(1)} %get-tuple-element.24, s16[1024]{0:T(1024)(128)(2,1)S(1)} %get-tuple-element.25, ...), kind=kLoop, calls=%fused_computation.31 | loop fusion | flops 167772160 | bytes 8409088 | tf_op jit(solution)/shard_map/add | solution.py:111
  48.6 1.0 constant_dynamic-update-slice_fusion.2
  50.0 5.6 %fusion.102 = bf16[8,33,16384]{2,1,0:T(8,128)(2,1)} fusion(pred[8,16384]{1,0:T(8,128)(4,1)S(1)} %iota_compare_fusion.5, bf16[33,16384]{1,0:T(8,128)(2,1)S(1)} %pad_multiply_fusion), kind=kLoop, calls=%fused_computation.21.clone.clone.clone.2 | loop fusion | flops 4325376 | bytes 9863168 | tf_op jit(solution)/shard_map/dot_general | solution.py:40
  55.5 9.8 %fusion.39 = f32[33,8,512]{2,0,1:T(8,128)S(1)} fusion(s16[16384]{0:T(1024)(128)(2,1)S(1)} %get-tuple-element.33, bf16[8,33,16384]{2,1,0:T(8,128)(2,1)} %fusion.102), kind=kOutput, calls=%fused_computation.65 | convolution fusion | flops 4437573632 | bytes 9224192 | tf_op jit(solution)/shard_map/dot_general | solution.py:40
  66.2 0.9 collective-permute-start.4
  67.1 1.9 %collective-permute-start.5 = (bf16[32,4096]{1,0:T(8,128)(2,1)S(1)}, bf16[32,4096]{1,0:T(8,128)(2,1)S(1)}, u32[]{:S(2)}, u32[]{:S(2)}) collective-permute-start(bf16[32,4096]{1,0:T(8,128)(2,1)S(1)} %divide_convert_fusion), channel_id=1, source_target_pairs={{0,3},{1,0},{2,1},{3,2},{4,7},{5,4},{6,5},{7,6},{8,11},{9,8},{10,9... | collective-permute-start | bytes 786440 | tf_op jit(solution)/shard_map/ppermute | solution.py:81
  69.1 10.1 %fusion.35 = bf16[2048,1024]{1,0:T(8,128)(2,1)} fusion(s16[1024]{0:T(1024)(128)(2,1)S(1)} %get-tuple-element.11, s16[1024]{0:T(1024)(128)(2,1)S(1)} %get-tuple-element.12, s16[1024]{0:T(1024)(128)(2,1)S(1)} %get-tuple-element.13, s16[1024]{0:T(1024)(128)(2,1)S(1)} %get-tuple-element.14, s16[1024]{0:T(1024)(128)(2,1)S(1)} %get-tuple-element.15, ...), kind=kLoop, calls=%fused_computation.58 | loop fusion | flops 60817408 | bytes 4218880 | tf_op jit(solution)/shard_map/add | solution.py:113
  79.2 1.5 %collective-permute-done.3 = bf16[32,4096]{1,0:T(8,128)(2,1)S(1)} collective-permute-done((bf16[32,4096]{1,0:T(8,128)(2,1)S(1)}, bf16[32,4096]{1,0:T(8,128)(2,1)S(1)}, u32[]{:S(2)}, u32[]{:S(2)}) %collective-permute-start.3) | collective-permute-done | bytes 262176 | tf_op jit(solution)/shard_map/ppermute | solution.py:81
  83.9 2.1 %reduce.42 = bf16[32,4096]{1,0:T(8,128)(2,1)S(1)} reduce(bf16[32,1,4096]{2,1,0:T(2,128)(2,1)S(1)} %broadcast_in_dim.66, bf16[]{:T(256)} %broadcast.316), dimensions={1}, to_apply=%broadcast_in_dim.66.reduce_sub_computation | reduce | bytes 524290 | tf_op jit(solution)/shard_map/broadcast_in_dim | solution.py:100
  86.0 0.9 reshape.475
  86.9 7.2 %all-to-all-start.1 = ((bf16[32,2,2048]{2,1,0:T(2,128)(2,1)}), bf16[32,2,2048]{2,1,0:T(2,128)(2,1)S(1)}, u32[]{:S(2)}, u32[]{:S(2)}) async-start(bf16[32,2,2048]{2,1,0:T(2,128)(2,1)} %reshape.475), calls=%async_computation.1 | async-start | bytes 524288 | tf_op jit(solution)/shard_map/all_to_all | solution.py:101
  94.1 4.9 %fusion.84 = f32[64,1024]{1,0:T(8,128)S(1)} fusion(bf16[64,4096]{1,0:T(8,128)(2,1)S(1)} %fusion.26, bf16[4096,1024]{1,0:T(8,128)(2,1)} %fusion.20), kind=kOutput, calls=%fused_computation.170 | convolution fusion | flops 536870912 | bytes 9175040 | tf_op jit(solution)/shard_map/dot_general | solution.py:116
  99.1 3.8 %all-to-all-done.1 = bf16[32,2,2048]{2,1,0:T(2,128)(2,1)S(1)} async-done(((bf16[32,2,2048]{2,1,0:T(2,128)(2,1)}), bf16[32,2,2048]{2,1,0:T(2,128)(2,1)S(1)}, u32[]{:S(2)}, u32[]{:S(2)}) %all-to-all-start.1) | async-done | bytes 262176 | tf_op jit(solution)/shard_map/all_to_all | solution.py:101
  103.2 1.5 %reduce.11 = bf16[32,4096]{1,0:T(8,128)(2,1)S(1)} reduce(bf16[32,1,4096]{2,1,0:T(2,128)(2,1)S(1)} %reshape.476, bf16[]{:T(256)} %constant.120), dimensions={1}, to_apply=%all_to_all.8.reduce_sub_computation | reduce | bytes 524290 | tf_op jit(solution)/shard_map/all_to_all | solution.py:101
  106.1 3.0 %fusion.47 = bf16[64,1024]{1,0:T(8,128)(2,1)S(1)} fusion(f32[64,1024]{1,0:T(8,128)S(1)} %fusion.84, bf16[64,2048]{1,0:T(8,128)(2,1)S(1)} %reshape.422, bf16[2048,1024]{1,0:T(8,128)(2,1)} %fusion.35), kind=kOutput, calls=%fused_computation.70 | convolution fusion | flops 268632064 | bytes 4849664 | tf_op jit(solution)/shard_map/dot_general | solution.py:117
  109.1 2.5 %collective-permute-start.8 = (bf16[64,1024]{1,0:T(8,128)(2,1)S(1)}, bf16[64,1024]{1,0:T(8,128)(2,1)S(1)}, u32[]{:S(2)}, u32[]{:S(2)}) collective-permute-start(bf16[64,1024]{1,0:T(8,128)(2,1)S(1)} %fusion.47), channel_id=1, source_target_pairs={{0,3},{1,0},{2,1},{3,2},{4,7},{5,4},{6,5},{7,6},{8,11},{9,8},{10,9... | collective-permute-start | bytes 393224 | tf_op jit(solution)/shard_map/ppermute | solution.py:81
  111.6 0.9 collective-permute-start.6
  112.6 1.1 fusion.60
  113.7 4.0 %collective-permute-done.8 = bf16[64,1024]{1,0:T(8,128)(2,1)S(1)} collective-permute-done((bf16[64,1024]{1,0:T(8,128)(2,1)S(1)}, bf16[64,1024]{1,0:T(8,128)(2,1)S(1)}, u32[]{:S(2)}, u32[]{:S(2)}) %collective-permute-start.8) | collective-permute-done | bytes 131104 | tf_op jit(solution)/shard_map/ppermute | solution.py:81
  117.8 1.8 %collective-permute-done.7 = bf16[64,1024]{1,0:T(8,128)(2,1)S(1)} collective-permute-done((bf16[64,1024]{1,0:T(8,128)(2,1)S(1)}, bf16[64,1024]{1,0:T(8,128)(2,1)S(1)}, u32[]{:S(2)}, u32[]{:S(2)}) %collective-permute-start.7) | collective-permute-done | bytes 131104 | tf_op jit(solution)/shard_map/ppermute | solution.py:81
  119.5 1.6 %collective-permute-done.6 = bf16[64,1024]{1,0:T(8,128)(2,1)S(1)} collective-permute-done((bf16[64,1024]{1,0:T(8,128)(2,1)S(1)}, bf16[64,1024]{1,0:T(8,128)(2,1)S(1)}, u32[]{:S(2)}, u32[]{:S(2)}) %collective-permute-start.6) | collective-permute-done | bytes 131104 | tf_op jit(solution)/shard_map/ppermute | solution.py:81
  121.1 1.1 fusion.51
  122.2 2.0 %fusion.48 = bf16[64,1024]{1,0:T(8,128)(2,1)} fusion(f32[64,1024]{1,0:T(8,128)S(1)} %fusion.51, f32[256,1024]{1,0:T(8,128)S(1)} %fusion.60, bf16[128,256]{1,0:T(8,128)(2,1)} %bitcast.69, bf16[128,4096]{1,0:T(8,128)(2,1)S(1)} %constant_dynamic-update-slice_fusion, bf16[256,256]{1,0:T(8,128)(2,1)S(1)} %copy-done, s32[]{:T(128)S(6)} %select_n.95), kind=kOutput, calls=%fused_computation.71 | convolution fusion | flops 101580800 | bytes 1835012 | tf_op jit(solution)/shard_map/dot_general | solution.py:10
  (77 shorter events, 9.4 us)
Async XLA Ops:
  0.0 122.2 %copy-start = (bf16[256,256]{1,0:T(8,128)(2,1)S(1)}, bf16[256,256]{1,0:T(8,128)(2,1)}, u32[]{:S(2)}) copy-start(bf16[256,256]{1,0:T(8,128)(2,1)} %param.20) | copy-start | bytes 393220
  0.0 48.6 %collective-permute-start = (bf16[32,4096]{1,0:T(8,128)(2,1)}, bf16[32,4096]{1,0:T(8,128)(2,1)}, u32[]{:S(2)}, u32[]{:S(2)}) collective-permute-start(bf16[32,4096]{1,0:T(8,128)(2,1)} %param.12), channel_id=1, source_target_pairs={{0,1},{1,2},{2,3},{3,0},{4,5},{5,6},{6,7},{7,4},{8,9},{9,10},{10,1... | collective-permute-start | bytes 786440 | tf_op jit(solution)/shard_map/ppermute | solution.py:81
  1.6 48.0 %collective-permute-start.1 = (bf16[32,4096]{1,0:T(8,128)(2,1)}, bf16[32,4096]{1,0:T(8,128)(2,1)S(1)}, u32[]{:S(2)}, u32[]{:S(2)}) collective-permute-start(bf16[32,4096]{1,0:T(8,128)(2,1)} %param.12), channel_id=1, source_target_pairs={{0,2},{1,3},{2,0},{3,1},{4,6},{5,7},{6,4},{7,5},{8,10},{9,11},{10,... | collective-permute-start | bytes 786440 | tf_op jit(solution)/shard_map/ppermute | solution.py:81
  4.3 45.3 %collective-permute-start.2 = (bf16[32,4096]{1,0:T(8,128)(2,1)}, bf16[32,4096]{1,0:T(8,128)(2,1)S(1)}, u32[]{:S(2)}, u32[]{:S(2)}) collective-permute-start(bf16[32,4096]{1,0:T(8,128)(2,1)} %param.12), channel_id=1, source_target_pairs={{0,3},{1,0},{2,1},{3,2},{4,7},{5,4},{6,5},{7,6},{8,11},{9,8},{10,9... | collective-permute-start | bytes 786440 | tf_op jit(solution)/shard_map/ppermute | solution.py:81
  14.6 12.7 %copy-start.1 = (bf16[32,4096]{1,0:T(8,128)(2,1)S(1)}, bf16[32,4096]{1,0:T(8,128)(2,1)}, u32[]{:S(2)}) copy-start(bf16[32,4096]{1,0:T(8,128)(2,1)} %param.12) | copy-start | bytes 786436
  14.6 12.9 %copy-start.5 = (s32[32,1,512]{2,1,0:T(1,128)S(1)}, s32[32,1,512]{2,1,0:T(1,128)}, u32[]{:S(2)}) copy-start(s32[32,1,512]{2,1,0:T(1,128)} %param.14) | copy-start | bytes 196612
  14.6 13.1 %copy-start.9 = (s32[32,1]{0,1:T(1,128)S(1)}, s32[32,1]{0,1:T(1,128)}, u32[]{:S(2)}) copy-start(s32[32,1]{0,1:T(1,128)} %param.15) | copy-start | bytes 388
  14.6 13.2 %copy-start.4 = (s32[1024,10]{0,1:T(8,128)S(1)}, s32[1024,10]{0,1:T(8,128)}, u32[]{:S(2)}) copy-start(s32[1024,10]{0,1:T(8,128)} %param.17) | copy-start | bytes 122884
  14.6 13.3 %copy-start.8 = (bf16[256,256]{1,0:T(8,128)(2,1)S(1)}, bf16[256,256]{1,0:T(8,128)(2,1)}, u32[]{:S(2)}) copy-start(bf16[256,256]{1,0:T(8,128)(2,1)} %param.21) | copy-start | bytes 393220
  17.6 29.7 %copy-start.6 = (bf16[128,256]{1,0:T(8,128)(2,1)S(1)}, bf16[128,256]{1,0:T(8,128)(2,1)}, u32[]{:S(2)}) copy-start(bf16[128,256]{1,0:T(8,128)(2,1)} %param.18) | copy-start | bytes 196612
  17.6 30.3 %copy-start.7 = (bf16[128,256]{1,0:T(8,128)(2,1)S(1)}, bf16[128,256]{1,0:T(8,128)(2,1)}, u32[]{:S(2)}) copy-start(bf16[128,256]{1,0:T(8,128)(2,1)} %param.19) | copy-start | bytes 196612
  18.8 30.9 %all-to-all-start = ((bf16[32,32,512]{2,0,1:T(8,128)(2,1)}), bf16[32,32,512]{2,0,1:T(8,128)(2,1)S(1)}, u32[]{:S(2)}, u32[]{:S(2)}) async-start(bf16[32,32,512]{2,0,1:T(8,128)(2,1)} %bitcast.59), calls=%async_computation | async-start | bytes 2097152 | tf_op jit(solution)/shard_map/all_to_all | solution.py:67
  48.5 32.8 %copy-start.3 = (bf16[4,32,256]{2,1,0:T(8,128)(2,1)}, bf16[4,32,256]{2,1,0:T(8,128)(2,1)S(1)}, u32[]{:S(2)}) copy-start(bf16[4,32,256]{2,1,0:T(8,128)(2,1)S(1)} %get-tuple-element.35) | copy-start | bytes 196612
  48.5 33.3 %copy-start.2 = (bf16[4,32,256]{2,1,0:T(8,128)(2,1)}, bf16[4,32,256]{2,1,0:T(8,128)(2,1)S(1)}, u32[]{:S(2)}) copy-start(bf16[4,32,256]{2,1,0:T(8,128)(2,1)S(1)} %get-tuple-element.34) | copy-start | bytes 196612
  65.3 16.9 %copy-start.10 = (s32[1,64]{1,0:T(1,128)S(1)}, s32[1,64]{1,0:T(1,128)}, u32[]{:S(2)}) copy-start(s32[1,64]{1,0:T(1,128)} %param.16) | copy-start | bytes 772
  65.5 15.2 %collective-permute-start.3 = (bf16[32,4096]{1,0:T(8,128)(2,1)S(1)}, bf16[32,4096]{1,0:T(8,128)(2,1)S(1)}, u32[]{:S(2)}, u32[]{:S(2)}) collective-permute-start(bf16[32,4096]{1,0:T(8,128)(2,1)S(1)} %divide_convert_fusion), channel_id=1, source_target_pairs={{0,1},{1,2},{2,3},{3,0},{4,5},{5,6},{6,7},{7,4},{8,9},{9,10},{10,1... | collective-permute-start | bytes 786440 | tf_op jit(solution)/shard_map/ppermute | solution.py:81
  66.2 14.6 %collective-permute-start.4 = (bf16[32,4096]{1,0:T(8,128)(2,1)S(1)}, bf16[32,4096]{1,0:T(8,128)(2,1)S(1)}, u32[]{:S(2)}, u32[]{:S(2)}) collective-permute-start(bf16[32,4096]{1,0:T(8,128)(2,1)S(1)} %divide_convert_fusion), channel_id=1, source_target_pairs={{0,2},{1,3},{2,0},{3,1},{4,6},{5,7},{6,4},{7,5},{8,10},{9,11},{10,... | collective-permute-start | bytes 786440 | tf_op jit(solution)/shard_map/ppermute | solution.py:81
  67.1 14.3 %collective-permute-start.5 = (bf16[32,4096]{1,0:T(8,128)(2,1)S(1)}, bf16[32,4096]{1,0:T(8,128)(2,1)S(1)}, u32[]{:S(2)}, u32[]{:S(2)}) collective-permute-start(bf16[32,4096]{1,0:T(8,128)(2,1)S(1)} %divide_convert_fusion), channel_id=1, source_target_pairs={{0,3},{1,0},{2,1},{3,2},{4,7},{5,4},{6,5},{7,6},{8,11},{9,8},{10,9... | collective-permute-start | bytes 786440 | tf_op jit(solution)/shard_map/ppermute | solution.py:81
  86.9 16.0 %all-to-all-start.1 = ((bf16[32,2,2048]{2,1,0:T(2,128)(2,1)}), bf16[32,2,2048]{2,1,0:T(2,128)(2,1)S(1)}, u32[]{:S(2)}, u32[]{:S(2)}) async-start(bf16[32,2,2048]{2,1,0:T(2,128)(2,1)} %reshape.475), calls=%async_computation.1 | async-start | bytes 524288 | tf_op jit(solution)/shard_map/all_to_all | solution.py:101
  109.1 8.6 %collective-permute-start.8 = (bf16[64,1024]{1,0:T(8,128)(2,1)S(1)}, bf16[64,1024]{1,0:T(8,128)(2,1)S(1)}, u32[]{:S(2)}, u32[]{:S(2)}) collective-permute-start(bf16[64,1024]{1,0:T(8,128)(2,1)S(1)} %fusion.47), channel_id=1, source_target_pairs={{0,3},{1,0},{2,1},{3,2},{4,7},{5,4},{6,5},{7,6},{8,11},{9,8},{10,9... | collective-permute-start | bytes 393224 | tf_op jit(solution)/shard_map/ppermute | solution.py:81
  111.6 7.9 %collective-permute-start.7 = (bf16[64,1024]{1,0:T(8,128)(2,1)S(1)}, bf16[64,1024]{1,0:T(8,128)(2,1)S(1)}, u32[]{:S(2)}, u32[]{:S(2)}) collective-permute-start(bf16[64,1024]{1,0:T(8,128)(2,1)S(1)} %fusion.47), channel_id=1, source_target_pairs={{0,2},{1,3},{2,0},{3,1},{4,6},{5,7},{6,4},{7,5},{8,10},{9,11},{10,... | collective-permute-start | bytes 393224 | tf_op jit(solution)/shard_map/ppermute | solution.py:81
  111.6 9.5 %collective-permute-start.6 = (bf16[64,1024]{1,0:T(8,128)(2,1)S(1)}, bf16[64,1024]{1,0:T(8,128)(2,1)S(1)}, u32[]{:S(2)}, u32[]{:S(2)}) collective-permute-start(bf16[64,1024]{1,0:T(8,128)(2,1)S(1)} %fusion.47), channel_id=1, source_target_pairs={{0,1},{1,2},{2,3},{3,0},{4,5},{5,6},{6,7},{7,4},{8,9},{9,10},{10,1... | collective-permute-start | bytes 393224 | tf_op jit(solution)/shard_map/ppermute | solution.py:81

commit v12 on v8

--- a/solution.py
+++ b/solution.py
@@ -12,7 +12,7 @@
     )
 
 
-def pick_columns(data, index, groups=8):
+def pick_columns(data, index, groups=16):
     width, extent = data.shape
     span = extent // groups
     stacked = data.reshape(width, groups, span).transpose(1, 0, 2).reshape(groups * width, span)

time: 121 us -> 126 us (1.041)
  other arithmetic: 38.1 us -> 42.6 us
  waiting for transfers between devices: 13.3 us -> 11.5 us
  matrix products: 30 us -> 31.5 us
    reduce_sum x1, other arithmetic: 2.95 us -> 7.42 us  [pick_columns(): jnp.sum(jnp.where(keep, rows, 0), axis=0, dtype=jnp.float32)]
    ppermute x9, waiting for transfers between devices: 9.47 us -> 7.66 us  [ring_gather(): parts.append(lax.ppermute(x, 'feat', perm=pairs))]
    dot_general x1, matrix products: 6.64 us -> 8.13 us  [pick_columns(): jnp.dot(stacked, onehot, preferred_element_type=jnp.float32)]
    unnamed x34 -> x32, local copies, waits for them, and re-layouts: 4.58 us -> 4.49 us
  transfers between devices with their start and end apart: 11 -> 11, of which waited for: 6 -> 5; matrix products, arithmetic and copies ran while one was open for 43% -> 47% of each run, Pallas kernels for 0% -> 0%
where the time goes in v12:
time: 126 us; the launch traced here: 125 us
  other arithmetic  42.6 us (34%)
  matrix products  31.5 us (25%)
  starting transfers between devices  28.8 us (23%)
  waiting for transfers between devices  11.5 us (9%)
  local copies, waits for them, and re-layouts  9.74 us (8%)
    add x1, other arithmetic, body(): near_tally = near_tally + (near_places == picked).astype(jnp.bfloat16)  17.9 us
    ppermute x9, starting transfers between devices, ring_gather(): parts.append(lax.ppermute(x, 'feat', perm=pairs))  13.2 us
    add x1, other arithmetic, body(): hub_tally = hub_tally + (hub_places == late).astype(jnp.bfloat16)  10.1 us
    dot_general x1, matrix products, add_columns(): total = jnp.dot(spread, marks, preferred_element_type=jnp.float32)  9.81 us
    all_to_all x1, starting transfers between devices, body(): lax.all_to_all(chosen, 'dom', split_axis=1, concat_axis=1, tiled=True)  8.33 us
    dot_general x1, matrix products, pick_columns(): jnp.dot(stacked, onehot, preferred_element_type=jnp.float32)  8.13 us
    ppermute x9, waiting for transfers between devices, ring_gather(): parts.append(lax.ppermute(x, 'feat', perm=pairs))  7.66 us
    reduce_sum x1, other arithmetic, pick_columns(): jnp.sum(jnp.where(keep, rows, 0), axis=0, dtype=jnp.float32)  7.42 us
  transfers between devices with their start and end apart: 11, of which 5 were waited for; matrix products, arithmetic and copies ran while one was open for 47% of the time, Pallas kernels for 0%

profile of v12, /device:TPU:0, one launch (start us, length us, event | category | flops | bytes accessed | tf_op | source)
XLA Modules:
  0.0 124.5 jit_solution(612891810010047209)
XLA Ops:
  0.0 1.6 %collective-permute-start = (bf16[32,4096]{1,0:T(8,128)(2,1)}, bf16[32,4096]{1,0:T(8,128)(2,1)}, u32[]{:S(2)}, u32[]{:S(2)}) collective-permute-start(bf16[32,4096]{1,0:T(8,128)(2,1)} %param.12), channel_id=1, source_target_pairs={{0,1},{1,2},{2,3},{3,0},{4,5},{5,6},{6,7},{7,4},{8,9},{9,10},{10,1... | collective-permute-start | bytes 786440 | tf_op jit(solution)/shard_map/ppermute | solution.py:81
  1.6 2.7 %collective-permute-start.1 = (bf16[32,4096]{1,0:T(8,128)(2,1)}, bf16[32,4096]{1,0:T(8,128)(2,1)S(1)}, u32[]{:S(2)}, u32[]{:S(2)}) collective-permute-start(bf16[32,4096]{1,0:T(8,128)(2,1)} %param.12), channel_id=1, source_target_pairs={{0,2},{1,3},{2,0},{3,1},{4,6},{5,7},{6,4},{7,5},{8,10},{9,11},{10,... | collective-permute-start | bytes 786440 | tf_op jit(solution)/shard_map/ppermute | solution.py:81
  4.3 1.4 %collective-permute-start.2 = (bf16[32,4096]{1,0:T(8,128)(2,1)}, bf16[32,4096]{1,0:T(8,128)(2,1)S(1)}, u32[]{:S(2)}, u32[]{:S(2)}) collective-permute-start(bf16[32,4096]{1,0:T(8,128)(2,1)} %param.12), channel_id=1, source_target_pairs={{0,3},{1,0},{2,1},{3,2},{4,7},{5,4},{6,5},{7,6},{8,11},{9,8},{10,9... | collective-permute-start | bytes 786440 | tf_op jit(solution)/shard_map/ppermute | solution.py:81
  5.8 0.9 copy.25
  6.7 1.0 copy.26
  7.9 8.1 %convolution_convert_fusion = bf16[16384,512]{0,1:T(8,128)(2,1)} fusion(bf16[512,256]{1,0:T(8,128)(2,1)S(1)} %bitcast.66, s16[16384]{0:T(1024)(128)(2,1)S(1)} %get-tuple-element.31), kind=kOutput, calls=%fused_computation.6 | convolution fusion | flops 4307550208 | bytes 17072128 | tf_op jit(solution)/shard_map/dot_general | solution.py:23
  16.1 7.4 %select_reduce_fusion = bf16[32,16384]{1,0:T(8,128)(2,1)S(1)} fusion(bf16[16,32,16384]{2,1,0:T(8,128)(2,1)} %bitcast.60, pred[16,16384]{1,0:T(8,128)(4,1)S(1)} %iota_compare_fusion.4), kind=kLoop, calls=%fused_computation.8 | loop fusion | flops 16252928 | bytes 18087936 | tf_op jit(solution)/shard_map/reduce_sum | solution.py:26
  23.5 1.1 copy.29
  24.6 8.3 %all-to-all-start = ((bf16[32,32,512]{2,0,1:T(8,128)(2,1)}), bf16[32,32,512]{2,0,1:T(8,128)(2,1)S(1)}, u32[]{:S(2)}, u32[]{:S(2)}) async-start(bf16[32,32,512]{2,0,1:T(8,128)(2,1)} %bitcast.59), calls=%async_computation | async-start | bytes 2097152 | tf_op jit(solution)/shard_map/all_to_all | solution.py:67
  33.6 0.9 constant_dynamic-slice_fusion
  35.1 0.7 bitcast_select_fusion
  35.9 17.9 %fusion.15 = bf16[4096,1024]{1,0:T(8,128)(2,1)} fusion(s16[1024]{0:T(1024)(128)(2,1)S(1)} %get-tuple-element.21, s16[1024]{0:T(1024)(128)(2,1)S(1)} %get-tuple-element.22, s16[1024]{0:T(1024)(128)(2,1)S(1)} %get-tuple-element.23, s16[1024]{0:T(1024)(128)(2,1)S(1)} %get-tuple-element.24, s16[1024]{0:T(1024)(128)(2,1)S(1)} %get-tuple-element.25, ...), kind=kLoop, calls=%fused_computation.30 | loop fusion | flops 167772160 | bytes 8409088 | tf_op jit(solution)/shard_map/add | solution.py:109
  55.1 1.0 constant_dynamic-update-slice_fusion.2
  56.5 5.6 %fusion.98 = bf16[8,33,16384]{2,1,0:T(8,128)(2,1)} fusion(pred[8,16384]{1,0:T(8,128)(4,1)S(1)} %iota_compare_fusion.5, bf16[33,16384]{1,0:T(8,128)(2,1)S(1)} %pad_multiply_fusion), kind=kLoop, calls=%fused_computation.20.clone.clone.clone.2 | loop fusion | flops 4325376 | bytes 9863168 | tf_op jit(solution)/shard_map/dot_general | solution.py:40
  62.0 9.8 %fusion.35 = f32[33,8,512]{2,0,1:T(8,128)S(1)} fusion(s16[16384]{0:T(1024)(128)(2,1)S(1)} %get-tuple-element.33, bf16[8,33,16384]{2,1,0:T(8,128)(2,1)} %fusion.98), kind=kOutput, calls=%fused_computation.64 | convolution fusion | flops 4437573632 | bytes 9224192 | tf_op jit(solution)/shard_map/dot_general | solution.py:40
  72.0 0.7 collective-permute-start.3
  72.7 0.9 collective-permute-start.4
  73.6 1.9 %collective-permute-start.5 = (bf16[32,4096]{1,0:T(8,128)(2,1)S(1)}, bf16[32,4096]{1,0:T(8,128)(2,1)S(1)}, u32[]{:S(2)}, u32[]{:S(2)}) collective-permute-start(bf16[32,4096]{1,0:T(8,128)(2,1)S(1)} %divide_convert_fusion), channel_id=1, source_target_pairs={{0,3},{1,0},{2,1},{3,2},{4,7},{5,4},{6,5},{7,6},{8,11},{9,8},{10,9... | collective-permute-start | bytes 786440 | tf_op jit(solution)/shard_map/ppermute | solution.py:81
  75.6 10.1 %fusion.30 = bf16[2048,1024]{1,0:T(8,128)(2,1)} fusion(s16[1024]{0:T(1024)(128)(2,1)S(1)} %get-tuple-element.11, s16[1024]{0:T(1024)(128)(2,1)S(1)} %get-tuple-element.12, s16[1024]{0:T(1024)(128)(2,1)S(1)} %get-tuple-element.13, s16[1024]{0:T(1024)(128)(2,1)S(1)} %get-tuple-element.14, s16[1024]{0:T(1024)(128)(2,1)S(1)} %get-tuple-element.15, ...), kind=kLoop, calls=%fused_computation.56 | loop fusion | flops 60817408 | bytes 4218880 | tf_op jit(solution)/shard_map/add | solution.py:111
  85.7 1.7 %collective-permute-done.3 = bf16[32,4096]{1,0:T(8,128)(2,1)S(1)} collective-permute-done((bf16[32,4096]{1,0:T(8,128)(2,1)S(1)}, bf16[32,4096]{1,0:T(8,128)(2,1)S(1)}, u32[]{:S(2)}, u32[]{:S(2)}) %collective-permute-start.3) | collective-permute-done | bytes 262176 | tf_op jit(solution)/shard_map/ppermute | solution.py:81
  87.5 0.6 collective-permute-done.5
  89.6 1.1 reshape.461
  90.7 7.2 %all-to-all-start.1 = ((bf16[32,2,2048]{2,1,0:T(2,128)(2,1)}), bf16[32,2,2048]{2,1,0:T(2,128)(2,1)S(1)}, u32[]{:S(2)}, u32[]{:S(2)}) async-start(bf16[32,2,2048]{2,1,0:T(2,128)(2,1)} %reshape.461), calls=%async_computation.1 | async-start | bytes 524288 | tf_op jit(solution)/shard_map/all_to_all | solution.py:100
  97.9 4.9 %fusion.80 = f32[64,1024]{1,0:T(8,128)S(1)} fusion(bf16[64,4096]{1,0:T(8,128)(2,1)S(1)} %fusion.21, bf16[4096,1024]{1,0:T(8,128)(2,1)} %fusion.15), kind=kOutput, calls=%fused_computation.169 | convolution fusion | flops 536870912 | bytes 9175040 | tf_op jit(solution)/shard_map/dot_general | solution.py:114
  102.9 3.8 %all-to-all-done.1 = bf16[32,2,2048]{2,1,0:T(2,128)(2,1)S(1)} async-done(((bf16[32,2,2048]{2,1,0:T(2,128)(2,1)}), bf16[32,2,2048]{2,1,0:T(2,128)(2,1)S(1)}, u32[]{:S(2)}, u32[]{:S(2)}) %all-to-all-start.1) | async-done | bytes 262176 | tf_op jit(solution)/shard_map/all_to_all | solution.py:100
  107.9 3.0 %fusion.43 = bf16[64,1024]{1,0:T(8,128)(2,1)S(1)} fusion(f32[64,1024]{1,0:T(8,128)S(1)} %fusion.80, bf16[64,2048]{1,0:T(8,128)(2,1)S(1)} %reshape.409, bf16[2048,1024]{1,0:T(8,128)(2,1)} %fusion.30), kind=kOutput, calls=%fused_computation.69 | convolution fusion | flops 268632064 | bytes 4849664 | tf_op jit(solution)/shard_map/dot_general | solution.py:115
  111.3 3.6 %collective-permute-start.7 = (bf16[64,1024]{1,0:T(8,128)(2,1)S(1)}, bf16[64,1024]{1,0:T(8,128)(2,1)S(1)}, u32[]{:S(2)}, u32[]{:S(2)}) collective-permute-start(bf16[64,1024]{1,0:T(8,128)(2,1)S(1)} %fusion.43), channel_id=1, source_target_pairs={{0,2},{1,3},{2,0},{3,1},{4,6},{5,7},{6,4},{7,5},{8,10},{9,11},{10,... | collective-permute-start | bytes 393224 | tf_op jit(solution)/shard_map/ppermute | solution.py:81
  114.9 1.2 fusion.56
  116.1 1.9 %collective-permute-done.6 = bf16[64,1024]{1,0:T(8,128)(2,1)S(1)} collective-permute-done((bf16[64,1024]{1,0:T(8,128)(2,1)S(1)}, bf16[64,1024]{1,0:T(8,128)(2,1)S(1)}, u32[]{:S(2)}, u32[]{:S(2)}) %collective-permute-start.6) | collective-permute-done | bytes 131104 | tf_op jit(solution)/shard_map/ppermute | solution.py:81
  118.0 3.5 %collective-permute-done.7 = bf16[64,1024]{1,0:T(8,128)(2,1)S(1)} collective-permute-done((bf16[64,1024]{1,0:T(8,128)(2,1)S(1)}, bf16[64,1024]{1,0:T(8,128)(2,1)S(1)}, u32[]{:S(2)}, u32[]{:S(2)}) %collective-permute-start.7) | collective-permute-done | bytes 131104 | tf_op jit(solution)/shard_map/ppermute | solution.py:81
  121.5 1.1 fusion.47
  122.5 2.0 %fusion.44 = bf16[64,1024]{1,0:T(8,128)(2,1)} fusion(f32[64,1024]{1,0:T(8,128)S(1)} %fusion.47, f32[256,1024]{1,0:T(8,128)S(1)} %fusion.56, bf16[128,256]{1,0:T(8,128)(2,1)} %bitcast.70, bf16[128,4096]{1,0:T(8,128)(2,1)S(1)} %constant_dynamic-update-slice_fusion, bf16[256,256]{1,0:T(8,128)(2,1)S(1)} %copy-done, s32[]{:T(128)S(6)} %select_n.95), kind=kOutput, calls=%fused_computation.70 | convolution fusion | flops 101580800 | bytes 1835012 | tf_op jit(solution)/shard_map/dot_general | solution.py:10
  (70 shorter events, 6.4 us)
Async XLA Ops:
  0.0 122.5 %copy-start = (bf16[256,256]{1,0:T(8,128)(2,1)S(1)}, bf16[256,256]{1,0:T(8,128)(2,1)}, u32[]{:S(2)}) copy-start(bf16[256,256]{1,0:T(8,128)(2,1)} %param.20) | copy-start | bytes 393220
  0.0 55.1 %collective-permute-start = (bf16[32,4096]{1,0:T(8,128)(2,1)}, bf16[32,4096]{1,0:T(8,128)(2,1)}, u32[]{:S(2)}, u32[]{:S(2)}) collective-permute-start(bf16[32,4096]{1,0:T(8,128)(2,1)} %param.12), channel_id=1, source_target_pairs={{0,1},{1,2},{2,3},{3,0},{4,5},{5,6},{6,7},{7,4},{8,9},{9,10},{10,1... | collective-permute-start | bytes 786440 | tf_op jit(solution)/shard_map/ppermute | solution.py:81
  1.6 54.5 %collective-permute-start.1 = (bf16[32,4096]{1,0:T(8,128)(2,1)}, bf16[32,4096]{1,0:T(8,128)(2,1)S(1)}, u32[]{:S(2)}, u32[]{:S(2)}) collective-permute-start(bf16[32,4096]{1,0:T(8,128)(2,1)} %param.12), channel_id=1, source_target_pairs={{0,2},{1,3},{2,0},{3,1},{4,6},{5,7},{6,4},{7,5},{8,10},{9,11},{10,... | collective-permute-start | bytes 786440 | tf_op jit(solution)/shard_map/ppermute | solution.py:81
  4.3 51.8 %collective-permute-start.2 = (bf16[32,4096]{1,0:T(8,128)(2,1)}, bf16[32,4096]{1,0:T(8,128)(2,1)S(1)}, u32[]{:S(2)}, u32[]{:S(2)}) collective-permute-start(bf16[32,4096]{1,0:T(8,128)(2,1)} %param.12), channel_id=1, source_target_pairs={{0,3},{1,0},{2,1},{3,2},{4,7},{5,4},{6,5},{7,6},{8,11},{9,8},{10,9... | collective-permute-start | bytes 786440 | tf_op jit(solution)/shard_map/ppermute | solution.py:81
  16.1 17.0 %copy-start.1 = (bf16[32,4096]{1,0:T(8,128)(2,1)S(1)}, bf16[32,4096]{1,0:T(8,128)(2,1)}, u32[]{:S(2)}) copy-start(bf16[32,4096]{1,0:T(8,128)(2,1)} %param.12) | copy-start | bytes 786436
  16.1 17.0 %copy-start.8 = (s32[32,1]{0,1:T(1,128)S(1)}, s32[32,1]{0,1:T(1,128)}, u32[]{:S(2)}) copy-start(s32[32,1]{0,1:T(1,128)} %param.15) | copy-start | bytes 388
  16.1 17.1 %copy-start.5 = (s32[32,1,512]{2,1,0:T(1,128)S(1)}, s32[32,1,512]{2,1,0:T(1,128)}, u32[]{:S(2)}) copy-start(s32[32,1,512]{2,1,0:T(1,128)} %param.14) | copy-start | bytes 196612
  16.1 17.3 %copy-start.4 = (s32[1024,10]{0,1:T(8,128)S(1)}, s32[1024,10]{0,1:T(8,128)}, u32[]{:S(2)}) copy-start(s32[1024,10]{0,1:T(8,128)} %param.17) | copy-start | bytes 122884
  23.5 30.3 %copy-start.6 = (bf16[128,256]{1,0:T(8,128)(2,1)S(1)}, bf16[128,256]{1,0:T(8,128)(2,1)}, u32[]{:S(2)}) copy-start(bf16[128,256]{1,0:T(8,128)(2,1)} %param.18) | copy-start | bytes 196612
  23.5 30.9 %copy-start.7 = (bf16[128,256]{1,0:T(8,128)(2,1)S(1)}, bf16[128,256]{1,0:T(8,128)(2,1)}, u32[]{:S(2)}) copy-start(bf16[128,256]{1,0:T(8,128)(2,1)} %param.19) | copy-start | bytes 196612
  24.6 31.5 %all-to-all-start = ((bf16[32,32,512]{2,0,1:T(8,128)(2,1)}), bf16[32,32,512]{2,0,1:T(8,128)(2,1)S(1)}, u32[]{:S(2)}, u32[]{:S(2)}) async-start(bf16[32,32,512]{2,0,1:T(8,128)(2,1)} %bitcast.59), calls=%async_computation | async-start | bytes 2097152 | tf_op jit(solution)/shard_map/all_to_all | solution.py:67
  55.1 33.0 %copy-start.3 = (bf16[4,32,256]{2,1,0:T(8,128)(2,1)}, bf16[4,32,256]{2,1,0:T(8,128)(2,1)S(1)}, u32[]{:S(2)}) copy-start(bf16[4,32,256]{2,1,0:T(8,128)(2,1)S(1)} %get-tuple-element.35) | copy-start | bytes 196612
  55.1 33.4 %copy-start.2 = (bf16[4,32,256]{2,1,0:T(8,128)(2,1)}, bf16[4,32,256]{2,1,0:T(8,128)(2,1)S(1)}, u32[]{:S(2)}) copy-start(bf16[4,32,256]{2,1,0:T(8,128)(2,1)S(1)} %get-tuple-element.34) | copy-start | bytes 196612
  71.9 17.1 %copy-start.9 = (s32[1,64]{1,0:T(1,128)S(1)}, s32[1,64]{1,0:T(1,128)}, u32[]{:S(2)}) copy-start(s32[1,64]{1,0:T(1,128)} %param.16) | copy-start | bytes 772
  72.0 15.4 %collective-permute-start.3 = (bf16[32,4096]{1,0:T(8,128)(2,1)S(1)}, bf16[32,4096]{1,0:T(8,128)(2,1)S(1)}, u32[]{:S(2)}, u32[]{:S(2)}) collective-permute-start(bf16[32,4096]{1,0:T(8,128)(2,1)S(1)} %divide_convert_fusion), channel_id=1, source_target_pairs={{0,1},{1,2},{2,3},{3,0},{4,5},{5,6},{6,7},{7,4},{8,9},{9,10},{10,1... | collective-permute-start | bytes 786440 | tf_op jit(solution)/shard_map/ppermute | solution.py:81
  72.7 14.7 %collective-permute-start.4 = (bf16[32,4096]{1,0:T(8,128)(2,1)S(1)}, bf16[32,4096]{1,0:T(8,128)(2,1)S(1)}, u32[]{:S(2)}, u32[]{:S(2)}) collective-permute-start(bf16[32,4096]{1,0:T(8,128)(2,1)S(1)} %divide_convert_fusion), channel_id=1, source_target_pairs={{0,2},{1,3},{2,0},{3,1},{4,6},{5,7},{6,4},{7,5},{8,10},{9,11},{10,... | collective-permute-start | bytes 786440 | tf_op jit(solution)/shard_map/ppermute | solution.py:81
  73.6 14.5 %collective-permute-start.5 = (bf16[32,4096]{1,0:T(8,128)(2,1)S(1)}, bf16[32,4096]{1,0:T(8,128)(2,1)S(1)}, u32[]{:S(2)}, u32[]{:S(2)}) collective-permute-start(bf16[32,4096]{1,0:T(8,128)(2,1)S(1)} %divide_convert_fusion), channel_id=1, source_target_pairs={{0,3},{1,0},{2,1},{3,2},{4,7},{5,4},{6,5},{7,6},{8,11},{9,8},{10,9... | collective-permute-start | bytes 786440 | tf_op jit(solution)/shard_map/ppermute | solution.py:81
  90.7 16.0 %all-to-all-start.1 = ((bf16[32,2,2048]{2,1,0:T(2,128)(2,1)}), bf16[32,2,2048]{2,1,0:T(2,128)(2,1)S(1)}, u32[]{:S(2)}, u32[]{:S(2)}) async-start(bf16[32,2,2048]{2,1,0:T(2,128)(2,1)} %reshape.461), calls=%async_computation.1 | async-start | bytes 524288 | tf_op jit(solution)/shard_map/all_to_all | solution.py:100
  110.9 7.0 %collective-permute-start.6 = (bf16[64,1024]{1,0:T(8,128)(2,1)S(1)}, bf16[64,1024]{1,0:T(8,128)(2,1)S(1)}, u32[]{:S(2)}, u32[]{:S(2)}) collective-permute-start(bf16[64,1024]{1,0:T(8,128)(2,1)S(1)} %fusion.43), channel_id=1, source_target_pairs={{0,1},{1,2},{2,3},{3,0},{4,5},{5,6},{6,7},{7,4},{8,9},{9,10},{10,1... | collective-permute-start | bytes 393224 | tf_op jit(solution)/shard_map/ppermute | solution.py:81
  111.3 10.1 %collective-permute-start.7 = (bf16[64,1024]{1,0:T(8,128)(2,1)S(1)}, bf16[64,1024]{1,0:T(8,128)(2,1)S(1)}, u32[]{:S(2)}, u32[]{:S(2)}) collective-permute-start(bf16[64,1024]{1,0:T(8,128)(2,1)S(1)} %fusion.43), channel_id=1, source_target_pairs={{0,2},{1,3},{2,0},{3,1},{4,6},{5,7},{6,4},{7,5},{8,10},{9,11},{10,... | collective-permute-start | bytes 393224 | tf_op jit(solution)/shard_map/ppermute | solution.py:81
  114.9 6.6 %collective-permute-start.8 = (bf16[64,1024]{1,0:T(8,128)(2,1)S(1)}, bf16[64,1024]{1,0:T(8,128)(2,1)S(1)}, u32[]{:S(2)}, u32[]{:S(2)}) collective-permute-start(bf16[64,1024]{1,0:T(8,128)(2,1)S(1)} %fusion.43), channel_id=1, source_target_pairs={{0,3},{1,0},{2,1},{3,2},{4,7},{5,4},{6,5},{7,6},{8,11},{9,8},{10,9... | collective-permute-start | bytes 393224 | tf_op jit(solution)/shard_map/ppermute | solution.py:81

commit v13 on v12

--- a/solution.py
+++ b/solution.py
@@ -12,7 +12,7 @@
     )
 
 
-def pick_columns(data, index, groups=16):
+def pick_columns(data, index, groups=4):
     width, extent = data.shape
     span = extent // groups
     stacked = data.reshape(width, groups, span).transpose(1, 0, 2).reshape(groups * width, span)

time: 126 us -> 126 us (level)
  other arithmetic: 42.6 us -> 36.9 us
  matrix products: 31.5 us -> 36.3 us
  waiting for transfers between devices: 11.5 us -> 13.3 us
    reduce_sum x1, other arithmetic: 7.42 us -> 1.71 us  [pick_columns(): jnp.sum(jnp.where(keep, rows, 0), axis=0, dtype=jnp.float32)]
    dot_general x1, matrix products: 8.13 us -> 12.9 us  [pick_columns(): jnp.dot(stacked, onehot, preferred_element_type=jnp.float32)]
    ppermute x9, waiting for transfers between devices: 7.66 us -> 9.45 us  [ring_gather(): parts.append(lax.ppermute(x, 'feat', perm=pairs))]
    unnamed x32 -> x33, local copies, waits for them, and re-layouts: 4.49 us -> 3.51 us
  transfers between devices with their start and end apart: 11 -> 11, of which waited for: 5 -> 6; matrix products, arithmetic and copies ran while one was open for 47% -> 45% of each run, Pallas kernels for 0% -> 0%
where the time goes in v13:
time: 126 us; the launch traced here: 124 us
  other arithmetic  36.9 us (29%)
  matrix products  36.3 us (29%)
  starting transfers between devices  28.4 us (23%)
  waiting for transfers between devices  13.3 us (11%)
  local copies, waits for them, and re-layouts  9.11 us (7%)
    add x1, other arithmetic, body(): near_tally = near_tally + (near_places == picked).astype(jnp.bfloat16)  17.9 us
    dot_general x1, matrix products, pick_columns(): jnp.dot(stacked, onehot, preferred_element_type=jnp.float32)  12.9 us
    ppermute x9, starting transfers between devices, ring_gather(): parts.append(lax.ppermute(x, 'feat', perm=pairs))  12.7 us
    add x1, other arithmetic, body(): hub_tally = hub_tally + (hub_places == late).astype(jnp.bfloat16)  10.1 us
    dot_general x1, matrix products, add_columns(): total = jnp.dot(spread, marks, preferred_element_type=jnp.float32)  9.81 us
    ppermute x9, waiting for transfers between devices, ring_gather(): parts.append(lax.ppermute(x, 'feat', perm=pairs))  9.45 us
    all_to_all x1, starting transfers between devices, body(): lax.all_to_all(chosen, 'dom', split_axis=1, concat_axis=1, tiled=True)  8.51 us
    all_to_all x1, starting transfers between devices, body(): lax.all_to_all(spread, 'dom', split_axis=0, concat_axis=0, tiled=True)  7.24 us
  transfers between devices with their start and end apart: 11, of which 6 were waited for; matrix products, arithmetic and copies ran while one was open for 45% of the time, Pallas kernels for 0%

profile of v13, /device:TPU:0, one launch (start us, length us, event | category | flops | bytes accessed | tf_op | source)
XLA Modules:
  0.0 124.4 jit_solution(17099670874092207204)
XLA Ops:
  0.0 1.6 %collective-permute-start = (bf16[32,4096]{1,0:T(8,128)(2,1)}, bf16[32,4096]{1,0:T(8,128)(2,1)}, u32[]{:S(2)}, u32[]{:S(2)}) collective-permute-start(bf16[32,4096]{1,0:T(8,128)(2,1)} %param.12), channel_id=1, source_target_pairs={{0,1},{1,2},{2,3},{3,0},{4,5},{5,6},{6,7},{7,4},{8,9},{9,10},{10,1... | collective-permute-start | bytes 786440 | tf_op jit(solution)/shard_map/ppermute | solution.py:81
  1.6 2.7 %collective-permute-start.1 = (bf16[32,4096]{1,0:T(8,128)(2,1)}, bf16[32,4096]{1,0:T(8,128)(2,1)S(1)}, u32[]{:S(2)}, u32[]{:S(2)}) collective-permute-start(bf16[32,4096]{1,0:T(8,128)(2,1)} %param.12), channel_id=1, source_target_pairs={{0,2},{1,3},{2,0},{3,1},{4,6},{5,7},{6,4},{7,5},{8,10},{9,11},{10,... | collective-permute-start | bytes 786440 | tf_op jit(solution)/shard_map/ppermute | solution.py:81
  4.3 1.4 %collective-permute-start.2 = (bf16[32,4096]{1,0:T(8,128)(2,1)}, bf16[32,4096]{1,0:T(8,128)(2,1)S(1)}, u32[]{:S(2)}, u32[]{:S(2)}) collective-permute-start(bf16[32,4096]{1,0:T(8,128)(2,1)} %param.12), channel_id=1, source_target_pairs={{0,3},{1,0},{2,1},{3,2},{4,7},{5,4},{6,5},{7,6},{8,11},{9,8},{10,9... | collective-permute-start | bytes 786440 | tf_op jit(solution)/shard_map/ppermute | solution.py:81
  5.8 1.2 reshape.403
  7.0 0.9 copy.25
  8.0 12.9 %fusion.6 = bf16[16384,128]{0,1:T(8,128)(2,1)S(1)} fusion(bf16[128,1024]{1,0:T(8,128)(2,1)S(1)} %bitcast.68, s16[16384]{0:T(1024)(128)(2,1)S(1)} %get-tuple-element.31), kind=kOutput, calls=%fused_computation.9 | convolution fusion | flops 4313841664 | bytes 4489216 | tf_op jit(solution)/shard_map/dot_general | solution.py:23
  21.0 1.7 %select_reduce_fusion = bf16[32,16384]{1,0:T(8,128)(2,1)S(1)} fusion(bf16[4,32,16384]{2,1,0:T(8,128)(2,1)S(1)} %bitcast.58, pred[4,16384]{1,0:T(4,128)(4,1)S(1)} %iota_compare_fusion.5), kind=kLoop, calls=%fused_computation.58 | loop fusion | flops 3670016 | bytes 5308416 | tf_op jit(solution)/shard_map/reduce_sum | solution.py:26
  22.7 1.1 copy.28
  23.9 8.5 %all-to-all-start = ((bf16[32,32,512]{2,0,1:T(8,128)(2,1)}), bf16[32,32,512]{2,0,1:T(8,128)(2,1)S(1)}, u32[]{:S(2)}, u32[]{:S(2)}) async-start(bf16[32,32,512]{2,0,1:T(8,128)(2,1)} %bitcast.56), calls=%async_computation | async-start | bytes 2097152 | tf_op jit(solution)/shard_map/all_to_all | solution.py:67
  33.8 0.7 bitcast_select_fusion
  34.5 17.9 %fusion.21 = bf16[4096,1024]{1,0:T(8,128)(2,1)} fusion(s16[1024]{0:T(1024)(128)(2,1)S(1)} %get-tuple-element.21, s16[1024]{0:T(1024)(128)(2,1)S(1)} %get-tuple-element.22, s16[1024]{0:T(1024)(128)(2,1)S(1)} %get-tuple-element.23, s16[1024]{0:T(1024)(128)(2,1)S(1)} %get-tuple-element.24, s16[1024]{0:T(1024)(128)(2,1)S(1)} %get-tuple-element.25, ...), kind=kLoop, calls=%fused_computation.32 | loop fusion | flops 167772160 | bytes 8409088 | tf_op jit(solution)/shard_map/add | solution.py:109
  53.7 1.0 constant_dynamic-update-slice_fusion.2
  55.1 5.6 %fusion.102 = bf16[8,33,16384]{2,1,0:T(8,128)(2,1)} fusion(pred[8,16384]{1,0:T(8,128)(4,1)S(1)} %iota_compare_fusion.4, bf16[33,16384]{1,0:T(8,128)(2,1)S(1)} %pad_multiply_fusion), kind=kLoop, calls=%fused_computation.22.clone.clone.clone.2 | loop fusion | flops 4325376 | bytes 9863168 | tf_op jit(solution)/shard_map/dot_general | solution.py:40
  60.7 9.8 %fusion.39 = f32[33,8,512]{2,0,1:T(8,128)S(1)} fusion(s16[16384]{0:T(1024)(128)(2,1)S(1)} %get-tuple-element.33, bf16[8,33,16384]{2,1,0:T(8,128)(2,1)} %fusion.102), kind=kOutput, calls=%fused_computation.65 | convolution fusion | flops 4437573632 | bytes 9224192 | tf_op jit(solution)/shard_map/dot_general | solution.py:40
  70.6 0.7 collective-permute-start.3
  71.3 0.9 collective-permute-start.4
  72.2 1.9 %collective-permute-start.5 = (bf16[32,4096]{1,0:T(8,128)(2,1)S(1)}, bf16[32,4096]{1,0:T(8,128)(2,1)S(1)}, u32[]{:S(2)}, u32[]{:S(2)}) collective-permute-start(bf16[32,4096]{1,0:T(8,128)(2,1)S(1)} %divide_convert_fusion), channel_id=1, source_target_pairs={{0,3},{1,0},{2,1},{3,2},{4,7},{5,4},{6,5},{7,6},{8,11},{9,8},{10,9... | collective-permute-start | bytes 786440 | tf_op jit(solution)/shard_map/ppermute | solution.py:81
  74.2 10.1 %fusion.35 = bf16[2048,1024]{1,0:T(8,128)(2,1)} fusion(s16[1024]{0:T(1024)(128)(2,1)S(1)} %get-tuple-element.11, s16[1024]{0:T(1024)(128)(2,1)S(1)} %get-tuple-element.12, s16[1024]{0:T(1024)(128)(2,1)S(1)} %get-tuple-element.13, s16[1024]{0:T(1024)(128)(2,1)S(1)} %get-tuple-element.14, s16[1024]{0:T(1024)(128)(2,1)S(1)} %get-tuple-element.15, ...), kind=kLoop, calls=%fused_computation.57 | loop fusion | flops 60817408 | bytes 4218880 | tf_op jit(solution)/shard_map/add | solution.py:111
  84.4 1.5 %collective-permute-done.3 = bf16[32,4096]{1,0:T(8,128)(2,1)S(1)} collective-permute-done((bf16[32,4096]{1,0:T(8,128)(2,1)S(1)}, bf16[32,4096]{1,0:T(8,128)(2,1)S(1)}, u32[]{:S(2)}, u32[]{:S(2)}) %collective-permute-start.3) | collective-permute-done | bytes 262176 | tf_op jit(solution)/shard_map/ppermute | solution.py:81
  88.0 1.1 reshape.461
  89.1 7.2 %all-to-all-start.1 = ((bf16[32,2,2048]{2,1,0:T(2,128)(2,1)}), bf16[32,2,2048]{2,1,0:T(2,128)(2,1)S(1)}, u32[]{:S(2)}, u32[]{:S(2)}) async-start(bf16[32,2,2048]{2,1,0:T(2,128)(2,1)} %reshape.461), calls=%async_computation.1 | async-start | bytes 524288 | tf_op jit(solution)/shard_map/all_to_all | solution.py:100
  96.4 4.9 %fusion.84 = f32[64,1024]{1,0:T(8,128)S(1)} fusion(bf16[64,4096]{1,0:T(8,128)(2,1)S(1)} %fusion.26, bf16[4096,1024]{1,0:T(8,128)(2,1)} %fusion.21), kind=kOutput, calls=%fused_computation.170 | convolution fusion | flops 536870912 | bytes 9175040 | tf_op jit(solution)/shard_map/dot_general | solution.py:114
  101.3 3.8 %all-to-all-done.1 = bf16[32,2,2048]{2,1,0:T(2,128)(2,1)S(1)} async-done(((bf16[32,2,2048]{2,1,0:T(2,128)(2,1)}), bf16[32,2,2048]{2,1,0:T(2,128)(2,1)S(1)}, u32[]{:S(2)}, u32[]{:S(2)}) %all-to-all-start.1) | async-done | bytes 262176 | tf_op jit(solution)/shard_map/all_to_all | solution.py:100
  106.3 3.0 %fusion.47 = bf16[64,1024]{1,0:T(8,128)(2,1)S(1)} fusion(f32[64,1024]{1,0:T(8,128)S(1)} %fusion.84, bf16[64,2048]{1,0:T(8,128)(2,1)S(1)} %reshape.409, bf16[2048,1024]{1,0:T(8,128)(2,1)} %fusion.35), kind=kOutput, calls=%fused_computation.70 | convolution fusion | flops 268632064 | bytes 4849664 | tf_op jit(solution)/shard_map/dot_general | solution.py:115
  109.3 2.5 %collective-permute-start.8 = (bf16[64,1024]{1,0:T(8,128)(2,1)S(1)}, bf16[64,1024]{1,0:T(8,128)(2,1)S(1)}, u32[]{:S(2)}, u32[]{:S(2)}) collective-permute-start(bf16[64,1024]{1,0:T(8,128)(2,1)S(1)} %fusion.47), channel_id=1, source_target_pairs={{0,3},{1,0},{2,1},{3,2},{4,7},{5,4},{6,5},{7,6},{8,11},{9,8},{10,9... | collective-permute-start | bytes 393224 | tf_op jit(solution)/shard_map/ppermute | solution.py:81
  111.9 0.9 collective-permute-start.6
  112.8 1.2 fusion.60
  114.0 4.0 %collective-permute-done.8 = bf16[64,1024]{1,0:T(8,128)(2,1)S(1)} collective-permute-done((bf16[64,1024]{1,0:T(8,128)(2,1)S(1)}, bf16[64,1024]{1,0:T(8,128)(2,1)S(1)}, u32[]{:S(2)}, u32[]{:S(2)}) %collective-permute-start.8) | collective-permute-done | bytes 131104 | tf_op jit(solution)/shard_map/ppermute | solution.py:81
  118.0 1.8 %collective-permute-done.7 = bf16[64,1024]{1,0:T(8,128)(2,1)S(1)} collective-permute-done((bf16[64,1024]{1,0:T(8,128)(2,1)S(1)}, bf16[64,1024]{1,0:T(8,128)(2,1)S(1)}, u32[]{:S(2)}, u32[]{:S(2)}) %collective-permute-start.7) | collective-permute-done | bytes 131104 | tf_op jit(solution)/shard_map/ppermute | solution.py:81
  119.8 1.6 %collective-permute-done.6 = bf16[64,1024]{1,0:T(8,128)(2,1)S(1)} collective-permute-done((bf16[64,1024]{1,0:T(8,128)(2,1)S(1)}, bf16[64,1024]{1,0:T(8,128)(2,1)S(1)}, u32[]{:S(2)}, u32[]{:S(2)}) %collective-permute-start.6) | collective-permute-done | bytes 131104 | tf_op jit(solution)/shard_map/ppermute | solution.py:81
  121.4 1.1 fusion.51
  122.5 2.0 %fusion.48 = bf16[64,1024]{1,0:T(8,128)(2,1)} fusion(f32[64,1024]{1,0:T(8,128)S(1)} %fusion.51, f32[256,1024]{1,0:T(8,128)S(1)} %fusion.60, bf16[128,256]{1,0:T(8,128)(2,1)} %bitcast.65, bf16[128,4096]{1,0:T(8,128)(2,1)S(1)} %constant_dynamic-update-slice_fusion, bf16[256,256]{1,0:T(8,128)(2,1)S(1)} %copy-done, s32[]{:T(128)S(6)} %select_n.95), kind=kOutput, calls=%fused_computation.71 | convolution fusion | flops 101580800 | bytes 1835012 | tf_op jit(solution)/shard_map/dot_general | solution.py:10
  (72 shorter events, 6.6 us)
Async XLA Ops:
  0.0 122.4 %copy-start = (bf16[256,256]{1,0:T(8,128)(2,1)S(1)}, bf16[256,256]{1,0:T(8,128)(2,1)}, u32[]{:S(2)}) copy-start(bf16[256,256]{1,0:T(8,128)(2,1)} %param.20) | copy-start | bytes 393220
  0.0 53.7 %collective-permute-start = (bf16[32,4096]{1,0:T(8,128)(2,1)}, bf16[32,4096]{1,0:T(8,128)(2,1)}, u32[]{:S(2)}, u32[]{:S(2)}) collective-permute-start(bf16[32,4096]{1,0:T(8,128)(2,1)} %param.12), channel_id=1, source_target_pairs={{0,1},{1,2},{2,3},{3,0},{4,5},{5,6},{6,7},{7,4},{8,9},{9,10},{10,1... | collective-permute-start | bytes 786440 | tf_op jit(solution)/shard_map/ppermute | solution.py:81
  1.6 53.1 %collective-permute-start.1 = (bf16[32,4096]{1,0:T(8,128)(2,1)}, bf16[32,4096]{1,0:T(8,128)(2,1)S(1)}, u32[]{:S(2)}, u32[]{:S(2)}) collective-permute-start(bf16[32,4096]{1,0:T(8,128)(2,1)} %param.12), channel_id=1, source_target_pairs={{0,2},{1,3},{2,0},{3,1},{4,6},{5,7},{6,4},{7,5},{8,10},{9,11},{10,... | collective-permute-start | bytes 786440 | tf_op jit(solution)/shard_map/ppermute | solution.py:81
  4.3 50.4 %collective-permute-start.2 = (bf16[32,4096]{1,0:T(8,128)(2,1)}, bf16[32,4096]{1,0:T(8,128)(2,1)S(1)}, u32[]{:S(2)}, u32[]{:S(2)}) collective-permute-start(bf16[32,4096]{1,0:T(8,128)(2,1)} %param.12), channel_id=1, source_target_pairs={{0,3},{1,0},{2,1},{3,2},{4,7},{5,4},{6,5},{7,6},{8,11},{9,8},{10,9... | collective-permute-start | bytes 786440 | tf_op jit(solution)/shard_map/ppermute | solution.py:81
  21.0 11.5 %copy-start.1 = (bf16[32,4096]{1,0:T(8,128)(2,1)S(1)}, bf16[32,4096]{1,0:T(8,128)(2,1)}, u32[]{:S(2)}) copy-start(bf16[32,4096]{1,0:T(8,128)(2,1)} %param.12) | copy-start | bytes 786436
  21.0 11.7 %copy-start.5 = (s32[32,1,512]{2,1,0:T(1,128)S(1)}, s32[32,1,512]{2,1,0:T(1,128)}, u32[]{:S(2)}) copy-start(s32[32,1,512]{2,1,0:T(1,128)} %param.14) | copy-start | bytes 196612
  21.0 11.8 %copy-start.9 = (s32[32,1]{0,1:T(1,128)S(1)}, s32[32,1]{0,1:T(1,128)}, u32[]{:S(2)}) copy-start(s32[32,1]{0,1:T(1,128)} %param.15) | copy-start | bytes 388
  21.0 11.9 %copy-start.4 = (s32[1024,10]{0,1:T(8,128)S(1)}, s32[1024,10]{0,1:T(8,128)}, u32[]{:S(2)}) copy-start(s32[1024,10]{0,1:T(8,128)} %param.17) | copy-start | bytes 122884
  21.0 12.0 %copy-start.8 = (bf16[256,256]{1,0:T(8,128)(2,1)S(1)}, bf16[256,256]{1,0:T(8,128)(2,1)}, u32[]{:S(2)}) copy-start(bf16[256,256]{1,0:T(8,128)(2,1)} %param.21) | copy-start | bytes 393220
  23.9 30.9 %all-to-all-start = ((bf16[32,32,512]{2,0,1:T(8,128)(2,1)}), bf16[32,32,512]{2,0,1:T(8,128)(2,1)S(1)}, u32[]{:S(2)}, u32[]{:S(2)}) async-start(bf16[32,32,512]{2,0,1:T(8,128)(2,1)} %bitcast.56), calls=%async_computation | async-start | bytes 2097152 | tf_op jit(solution)/shard_map/all_to_all | solution.py:67
  32.4 20.1 %copy-start.6 = (bf16[128,256]{1,0:T(8,128)(2,1)S(1)}, bf16[128,256]{1,0:T(8,128)(2,1)}, u32[]{:S(2)}) copy-start(bf16[128,256]{1,0:T(8,128)(2,1)} %param.18) | copy-start | bytes 196612
  32.4 20.6 %copy-start.7 = (bf16[128,256]{1,0:T(8,128)(2,1)S(1)}, bf16[128,256]{1,0:T(8,128)(2,1)}, u32[]{:S(2)}) copy-start(bf16[128,256]{1,0:T(8,128)(2,1)} %param.19) | copy-start | bytes 196612
  53.7 32.8 %copy-start.3 = (bf16[4,32,256]{2,1,0:T(8,128)(2,1)}, bf16[4,32,256]{2,1,0:T(8,128)(2,1)S(1)}, u32[]{:S(2)}) copy-start(bf16[4,32,256]{2,1,0:T(8,128)(2,1)S(1)} %get-tuple-element.35) | copy-start | bytes 196612
  53.7 33.2 %copy-start.2 = (bf16[4,32,256]{2,1,0:T(8,128)(2,1)}, bf16[4,32,256]{2,1,0:T(8,128)(2,1)S(1)}, u32[]{:S(2)}) copy-start(bf16[4,32,256]{2,1,0:T(8,128)(2,1)S(1)} %get-tuple-element.34) | copy-start | bytes 196612
  70.6 15.2 %collective-permute-start.3 = (bf16[32,4096]{1,0:T(8,128)(2,1)S(1)}, bf16[32,4096]{1,0:T(8,128)(2,1)S(1)}, u32[]{:S(2)}, u32[]{:S(2)}) collective-permute-start(bf16[32,4096]{1,0:T(8,128)(2,1)S(1)} %divide_convert_fusion), channel_id=1, source_target_pairs={{0,1},{1,2},{2,3},{3,0},{4,5},{5,6},{6,7},{7,4},{8,9},{9,10},{10,1... | collective-permute-start | bytes 786440 | tf_op jit(solution)/shard_map/ppermute | solution.py:81
  71.3 14.6 %collective-permute-start.4 = (bf16[32,4096]{1,0:T(8,128)(2,1)S(1)}, bf16[32,4096]{1,0:T(8,128)(2,1)S(1)}, u32[]{:S(2)}, u32[]{:S(2)}) collective-permute-start(bf16[32,4096]{1,0:T(8,128)(2,1)S(1)} %divide_convert_fusion), channel_id=1, source_target_pairs={{0,2},{1,3},{2,0},{3,1},{4,6},{5,7},{6,4},{7,5},{8,10},{9,11},{10,... | collective-permute-start | bytes 786440 | tf_op jit(solution)/shard_map/ppermute | solution.py:81
  72.2 14.3 %collective-permute-start.5 = (bf16[32,4096]{1,0:T(8,128)(2,1)S(1)}, bf16[32,4096]{1,0:T(8,128)(2,1)S(1)}, u32[]{:S(2)}, u32[]{:S(2)}) collective-permute-start(bf16[32,4096]{1,0:T(8,128)(2,1)S(1)} %divide_convert_fusion), channel_id=1, source_target_pairs={{0,3},{1,0},{2,1},{3,2},{4,7},{5,4},{6,5},{7,6},{8,11},{9,8},{10,9... | collective-permute-start | bytes 786440 | tf_op jit(solution)/shard_map/ppermute | solution.py:81
  74.2 13.2 %copy-start.10 = (s32[1,64]{1,0:T(1,128)S(1)}, s32[1,64]{1,0:T(1,128)}, u32[]{:S(2)}) copy-start(s32[1,64]{1,0:T(1,128)} %param.16) | copy-start | bytes 772
  89.1 16.0 %all-to-all-start.1 = ((bf16[32,2,2048]{2,1,0:T(2,128)(2,1)}), bf16[32,2,2048]{2,1,0:T(2,128)(2,1)S(1)}, u32[]{:S(2)}, u32[]{:S(2)}) async-start(bf16[32,2,2048]{2,1,0:T(2,128)(2,1)} %reshape.461), calls=%async_computation.1 | async-start | bytes 524288 | tf_op jit(solution)/shard_map/all_to_all | solution.py:100
  109.3 8.6 %collective-permute-start.8 = (bf16[64,1024]{1,0:T(8,128)(2,1)S(1)}, bf16[64,1024]{1,0:T(8,128)(2,1)S(1)}, u32[]{:S(2)}, u32[]{:S(2)}) collective-permute-start(bf16[64,1024]{1,0:T(8,128)(2,1)S(1)} %fusion.47), channel_id=1, source_target_pairs={{0,3},{1,0},{2,1},{3,2},{4,7},{5,4},{6,5},{7,6},{8,11},{9,8},{10,9... | collective-permute-start | bytes 393224 | tf_op jit(solution)/shard_map/ppermute | solution.py:81
  111.9 7.9 %collective-permute-start.7 = (bf16[64,1024]{1,0:T(8,128)(2,1)S(1)}, bf16[64,1024]{1,0:T(8,128)(2,1)S(1)}, u32[]{:S(2)}, u32[]{:S(2)}) collective-permute-start(bf16[64,1024]{1,0:T(8,128)(2,1)S(1)} %fusion.47), channel_id=1, source_target_pairs={{0,2},{1,3},{2,0},{3,1},{4,6},{5,7},{6,4},{7,5},{8,10},{9,11},{10,... | collective-permute-start | bytes 393224 | tf_op jit(solution)/shard_map/ppermute | solution.py:81
  111.9 9.5 %collective-permute-start.6 = (bf16[64,1024]{1,0:T(8,128)(2,1)S(1)}, bf16[64,1024]{1,0:T(8,128)(2,1)S(1)}, u32[]{:S(2)}, u32[]{:S(2)}) collective-permute-start(bf16[64,1024]{1,0:T(8,128)(2,1)S(1)} %fusion.47), channel_id=1, source_target_pairs={{0,1},{1,2},{2,3},{3,0},{4,5},{5,6},{6,7},{7,4},{8,9},{9,10},{10,1... | collective-permute-start | bytes 393224 | tf_op jit(solution)/shard_map/ppermute | solution.py:81
